TPU v7x, 32 devices: a whole 2x2x4 slice. The times are simulated.
32 devices in a mesh: patch: 8 (over z, x), var: 4 (over y, core).
Axes of the slice: x: 2, y: 2, z: 4, core: 2. Of those that a mesh axis runs over, the one named last changes fastest.
Arguments:
- pixels: bfloat16 [48, 4, 8192], P('var', None, 'patch'), may hold values from -6 to 6
- embed: float32 [48, 5, 1024], P('var', None, 'patch'), may hold values from -3 to 3
- query: float32 [1024], P(('patch', 'var')), may hold values from -9 to 9
- w_query: float32 [1024, 1024], P(('patch', 'var')), may hold values from -0.1875 to 0.1875
- w_key: float32 [1024, 1024], P(('patch', 'var')), may hold values from -0.1875 to 0.1875
- w_value: float32 [1024, 1024], P(('patch', 'var')), may hold values from -0.1875 to 0.1875
- w_out: float32 [1024, 1024], P('patch', 'var'), may hold values from -0.5 to 0.5
- b_out: float32 [1024], P(('patch', 'var')), may hold values from -3 to 3
- pos_embed: float32 [2048, 1024], P('patch', 'var'), may hold values from -3 to 3
- w_lead: float32 [1024], P(('patch', 'var')), may hold values from -3 to 3
- avail: int32 [4, 48], replicated, may hold values from 0 to 1, as said below
- lengths: int32 [4], replicated, may hold values from 1024 to 2048, as said below
- lead_hours: int32 [4], replicated, may hold values from 6 to 168
- cotangent: bfloat16 [8192, 1024], P('patch', 'var'), may hold values from -6 to 6
Outputs:
- mixed: bfloat16 [8192, 1024], P('patch', 'var')
- grad_pixels: bfloat16 [48, 4, 8192], P('var', None, 'patch')
- grad_embed: float32 [48, 5, 1024], P('var', None, 'patch')
- grad_query: float32 [1024], P(('patch', 'var'))
- grad_w_query: float32 [1024, 1024], P(('patch', 'var'))
- grad_w_key: float32 [1024, 1024], P(('patch', 'var'))
- grad_w_value: float32 [1024, 1024], P(('patch', 'var'))
- grad_w_out: float32 [1024, 1024], P('patch', 'var')
- grad_b_out: float32 [1024], P(('patch', 'var'))
- grad_pos_embed: float32 [2048, 1024], P('patch', 'var')
- grad_w_lead: float32 [1024], P(('patch', 'var'))
Inputs may be any that keep to these rules, and one draw needn't show every extreme that they name: `avail`: every sample has at least one available variable. `lengths`: at least one group is full.
All inputs are finite; a program needn't handle non-finite values.
Results may differ from a plain program's by a relative error of at most 0.018.
Values may be sent and summed in bfloat16 or wider, within the bound.
No kernel may reach another device: no remote copies, remote signals or barrier semaphores. Data moves between devices by JAX's collectives and lax.ppermute only.
A program may use at most 256 MiB of HBM per device.

v0:
```python
import math

import jax
import jax.numpy as jnp
from jax import lax
from jax.sharding import PartitionSpec as P

D = 1024
HEADS = 16
GROUP = 2048


highest = lax.Precision.HIGHEST
neg_large = -1e30


def combined_all(part, axis, combine):
    gathered = jax.tree.map(lambda a: lax.all_gather(a, axis), part)

    def take(source):
        return jax.tree.map(lambda a: lax.dynamic_index_in_dim(a, source, 0, False), gathered)

    return lax.fori_loop(
        1, lax.axis_size(axis), lambda source, state: combine(state, take(source)), take(0)
    )


def row_tables(row_start, count, avail, lengths, lead_hours):
    rows = row_start + jnp.arange(count, dtype=jnp.int32)
    sample = rows // GROUP
    match = sample[:, None] == jnp.arange(avail.shape[0], dtype=jnp.int32)[None, :]
    avail_rows = jnp.dot(match.astype(jnp.float32), avail.astype(jnp.float32), precision=highest)
    length_rows = jnp.sum(jnp.where(match, lengths[None, :], 0), axis=1)
    lead_rows = (
        jnp.sum(jnp.where(match, lead_hours[None, :], 0), axis=1).astype(jnp.float32) / 100.0
    )
    position = rows % GROUP
    return (avail_rows, position < length_rows, lead_rows)


def spread_heads(numer, total):
    rows = numer.shape[0]
    return (numer.reshape(rows, HEADS, -1) / total[:, :, None]).reshape(rows, -1)


def combine_partials(first_part, second_part):
    top_a, total_a, numer_a = first_part
    top_b, total_b, numer_b = second_part
    top_new = jnp.maximum(top_a, top_b)
    scale_a = jnp.exp(top_a - top_new)
    scale_b = jnp.exp(top_b - top_new)
    rows = numer_a.shape[0]
    numer_new = (
        numer_a.reshape(rows, HEADS, -1) * scale_a[:, :, None]
        + numer_b.reshape(rows, HEADS, -1) * scale_b[:, :, None]
    )
    return (top_new, total_a * scale_a + total_b * scale_b, numer_new.reshape(rows, -1))


def local_forward(pixel_block, embed_block, fold_low, value_weight, avail_rows, first_var):
    count = pixel_block.shape[0]
    rows = pixel_block.shape[2]
    token = jnp.einsum(
        "vpt,vpd->vtd", pixel_block, embed_block[:, :4], preferred_element_type=jnp.float32
    )
    token = (token + embed_block[:, 4][:, None, :].astype(jnp.float32)).astype(jnp.bfloat16)
    scores = jnp.einsum("vtd,dh->vth", token, fold_low, preferred_element_type=jnp.float32)
    values = jnp.einsum(
        "vtd,de->vte", token, value_weight, preferred_element_type=jnp.float32
    ).astype(jnp.bfloat16)
    local_avail = lax.dynamic_slice_in_dim(avail_rows, first_var, count, 1)
    present = (local_avail.T > 0.5)[:, :, None]
    masked = jnp.where(present, scores, neg_large)
    top = jnp.max(masked, axis=0)
    weight = jnp.where(present, jnp.exp(masked - top), 0.0)
    total = jnp.sum(weight, axis=0)
    numer = jnp.einsum(
        "vth,vthe->the",
        weight,
        values.reshape(count, rows, HEADS, -1),
        preferred_element_type=jnp.float32,
    )
    return (token, values, scores, present, top, total, numer.reshape(rows, -1))


def local_backward(
    pixel_block,
    embed_block,
    fold_low,
    value_weight,
    token,
    values,
    scores,
    present,
    top,
    total,
    attended,
    grad_att,
):
    count = values.shape[0]
    rows = values.shape[1]
    hsize = values.shape[2] // HEADS
    prob = jnp.where(present, jnp.exp(jnp.where(present, scores, neg_large) - top), 0.0) / total
    grad_heads = grad_att.astype(jnp.float32).reshape(rows, HEADS, hsize)
    grad_values = (prob[..., None] * grad_heads[None]).reshape(count, rows, -1).astype(jnp.bfloat16)
    grad_prob = jnp.einsum(
        "the,vthe->vth",
        grad_heads,
        values.reshape(count, rows, HEADS, hsize),
        preferred_element_type=jnp.float32,
    )
    inner = jnp.sum(grad_heads * attended.reshape(rows, HEADS, hsize), axis=2)
    grad_scores = (prob * (grad_prob - inner)).astype(jnp.bfloat16)
    grad_token = jnp.einsum(
        "vte,de->vtd", grad_values, value_weight, preferred_element_type=jnp.float32
    )
    grad_token = (
        grad_token
        + jnp.einsum("vth,dh->vtd", grad_scores, fold_low, preferred_element_type=jnp.float32)
    ).astype(jnp.bfloat16)
    grad_value_w = jnp.einsum("vtd,vte->de", token, grad_values, preferred_element_type=jnp.float32)
    grad_fold = jnp.einsum("vtd,vth->dh", token, grad_scores, preferred_element_type=jnp.float32)
    pixel_part = jnp.einsum(
        "vpt,vtd->vpd", pixel_block, grad_token, preferred_element_type=jnp.float32
    )
    embed_sum = jnp.sum(grad_token, axis=1, dtype=jnp.float32)[:, None, :]
    grad_embed = jnp.concatenate([pixel_part, embed_sum], axis=1)
    grad_pixels = jnp.einsum(
        "vpd,vtd->vpt", embed_block[:, :4], grad_token, preferred_element_type=jnp.float32
    ).astype(jnp.bfloat16)
    return (grad_value_w, grad_fold, grad_embed, grad_pixels)


def shards(
    pixels,
    embed,
    query,
    w_query,
    w_key,
    w_value,
    w_out,
    b_out,
    pos_embed,
    w_lead,
    avail,
    lengths,
    lead_hours,
    cotangent,
):
    var_index = lax.axis_index("var")
    patch_index = lax.axis_index("patch")
    local_vars = pixels.shape[0]
    rows_dev = pixels.shape[2]
    col_width = w_out.shape[1]
    hsize = D // HEADS
    query_full, qweight_full, key_full, value_full, bias_full, lead_full = (
        lax.all_gather(w_query.astype(jnp.bfloat16), ("patch", "var"), axis=0, tiled=True),
        lax.all_gather(w_key.astype(jnp.bfloat16), ("patch", "var"), axis=0, tiled=True),
        lax.all_gather(w_value.astype(jnp.bfloat16), ("patch", "var"), axis=0, tiled=True),
        lax.all_gather(query.astype(jnp.bfloat16), ("patch", "var"), axis=0, tiled=True),
        lax.all_gather(b_out.astype(jnp.bfloat16), ("patch", "var"), axis=0, tiled=True),
        lax.all_gather(w_lead.astype(jnp.bfloat16), ("patch", "var"), axis=0, tiled=True),
    )
    qweight_full, key_full, value_full, query_full = (
        query_full,
        qweight_full,
        key_full,
        value_full,
    )
    qvec = jnp.dot(query_full[None, :], qweight_full, preferred_element_type=jnp.float32)[0]
    key_heads = key_full.astype(jnp.float32).reshape(D, HEADS, hsize)
    fold = jnp.einsum("dhe,he->dh", key_heads, qvec.reshape(HEADS, hsize), precision=highest)
    fold_low = (fold / math.sqrt(hsize)).astype(jnp.bfloat16)
    out_weight, pos_full = (
        lax.all_gather(w_out.astype(jnp.bfloat16), "patch", axis=0, tiled=True),
        lax.all_gather(pos_embed.astype(jnp.bfloat16), "patch", axis=0, tiled=True),
    )
    embed_own = lax.all_gather(embed.astype(jnp.bfloat16), "patch", axis=2, tiled=True)
    row_first = patch_index * rows_dev
    avail_rows, valid, lead_rows = row_tables(row_first, rows_dev, avail, lengths, lead_hours)
    token, values, scores, present, top, total, numer = local_forward(
        pixels, embed_own, fold_low, value_full, avail_rows, var_index * local_vars
    )
    top, total, numer = combined_all((top, total, numer), "var", combine_partials)
    attended = spread_heads(numer, total)
    att_rows = attended.astype(jnp.bfloat16)
    col_first = var_index * col_width
    bias_cols = lax.dynamic_slice_in_dim(bias_full, col_first, col_width).astype(jnp.float32)
    lead_cols = lax.dynamic_slice_in_dim(lead_full, col_first, col_width).astype(jnp.float32)
    pos_rows = lax.dynamic_slice_in_dim(pos_full, row_first % GROUP, rows_dev, 0)
    result = jnp.dot(att_rows, out_weight, preferred_element_type=jnp.float32)
    result = result + bias_cols + pos_rows.astype(jnp.float32) + lead_rows[:, None] * lead_cols
    mixed = jnp.where(valid[:, None], result, 0.0).astype(jnp.bfloat16)
    grad_rows = jnp.where(valid[:, None], cotangent, jnp.zeros_like(cotangent))
    grad_float = grad_rows.astype(jnp.float32)
    grad_w_out = jnp.einsum("td,tc->dc", att_rows, grad_rows, preferred_element_type=jnp.float32)
    grad_pos = lax.dynamic_update_slice_in_dim(
        jnp.zeros((GROUP, col_width), jnp.float32), grad_float, row_first % GROUP, 0
    )
    grad_bias = lax.dynamic_update_slice_in_dim(
        jnp.zeros((D,), jnp.float32), jnp.sum(grad_float, axis=0), col_first, 0
    )
    grad_lead = lax.dynamic_update_slice_in_dim(
        jnp.zeros((D,), jnp.float32), jnp.sum(lead_rows[:, None] * grad_float, axis=0), col_first, 0
    )
    grad_att_part = jnp.einsum(
        "tc,dc->td", grad_rows, out_weight, preferred_element_type=jnp.float32
    )
    grad_w_out, grad_pos = (
        lax.psum_scatter(
            grad_w_out.astype(jnp.bfloat16), "patch", scatter_dimension=0, tiled=True
        ).astype(jnp.float32),
        lax.psum_scatter(
            grad_pos.astype(jnp.bfloat16), "patch", scatter_dimension=0, tiled=True
        ).astype(jnp.float32),
    )
    grad_att = lax.psum(grad_att_part, "var").astype(jnp.bfloat16)
    grad_value_w, grad_fold, grad_embed, grad_pixels = local_backward(
        pixels,
        embed_own,
        fold_low,
        value_full,
        token,
        values,
        scores,
        present,
        top,
        total,
        attended,
        grad_att,
    )
    grad_embed_shard = lax.psum_scatter(
        grad_embed.astype(jnp.bfloat16), "patch", scatter_dimension=2, tiled=True
    ).astype(jnp.float32)
    grad_key = (grad_fold[:, :, None] * qvec.reshape(HEADS, hsize)[None]).reshape(D, D) / math.sqrt(
        hsize
    )
    grad_qvec = jnp.sum(key_heads * grad_fold[:, :, None], axis=0).reshape(D) / math.sqrt(hsize)
    grad_wq = query_full.astype(jnp.float32)[:, None] * grad_qvec[None, :]
    grad_query = jnp.dot(qweight_full.astype(jnp.float32), grad_qvec, precision=highest)
    summed = (
        lax.psum_scatter(grad_wq, ("patch", "var"), scatter_dimension=0, tiled=True),
        lax.psum_scatter(grad_key, ("patch", "var"), scatter_dimension=0, tiled=True),
        lax.psum_scatter(grad_value_w, ("patch", "var"), scatter_dimension=0, tiled=True),
        lax.psum_scatter(grad_query, ("patch", "var"), scatter_dimension=0, tiled=True),
        lax.psum_scatter(grad_bias, ("patch", "var"), scatter_dimension=0, tiled=True),
        lax.psum_scatter(grad_lead, ("patch", "var"), scatter_dimension=0, tiled=True),
    )
    grad_wq_out, grad_key_out, grad_value_out = (summed[0], summed[1], summed[2])
    grad_query_out, grad_bias_out, grad_lead_out = (summed[3], summed[4], summed[5])
    return (
        mixed,
        grad_pixels,
        grad_embed_shard,
        grad_query_out,
        grad_wq_out,
        grad_key_out,
        grad_value_out,
        grad_w_out,
        grad_bias_out,
        grad_pos,
        grad_lead_out,
    )


def solution(mesh):
    return jax.shard_map(
        shards,
        mesh=mesh,
        in_specs=(
            P("var", None, "patch"),
            P("var", None, "patch"),
            P(("patch", "var")),
            P(("patch", "var"), None),
            P(("patch", "var"), None),
            P(("patch", "var"), None),
            P("patch", "var"),
            P(("patch", "var")),
            P("patch", "var"),
            P(("patch", "var")),
            P(),
            P(),
            P(),
            P("patch", "var"),
        ),
        out_specs=(
            P("patch", "var"),
            P("var", None, "patch"),
            P("var", None, "patch"),
            P(("patch", "var")),
            P(("patch", "var"), None),
            P(("patch", "var"), None),
            P(("patch", "var"), None),
            P("patch", "var"),
            P(("patch", "var")),
            P("patch", "var"),
            P(("patch", "var")),
        ),
        check_vma=False,
    )
```

profile of v0, /device:TPU:0, one launch (start us, length us, event | category | flops | bytes accessed | tf_op | source)
XLA Modules:
  0.0 1130.4 jit_solution(6467497296468175274)
XLA Ops:
  13.7 28.0 %all_gather.42 = bf16[12,5,1024]{2,0,1:T(8,128)(2,1)S(1)} all-gather(bf16[12,5,128]{2,0,1:T(8,128)(2,1)S(1)} %convert_element_type.115), channel_id=1, replica_groups=mesh['patch'=8,'var'=4] {'patch'}, dimensions={2}, use_global_device_ids=true | all-gather | bytes 138240 | tf_op jit(solution)/shard_map/all_gather | solution.py:178
  44.5 39.3 %all-reduce.7 = (bf16[1024]{0:T(1024)(128)(2,1)S(1)}, bf16[1024]{0:T(1024)(128)(2,1)}, bf16[1024]{0:T(1024)(128)(2,1)}) all-reduce(bf16[1024]{0:T(1024)(128)(2,1)S(1)} %dynamic-update-slice, bf16[1024]{0:T(1024)(128)(2,1)S(1)} %dynamic-update-slice.2, ...), channel_id=1, replica_groups=mesh['patch'=8,'var'=4] {'patch','var'}, use_global_device_ids=true, to_apply=%add | all-reduce | flops 3072 | bytes 12288
  87.1 31.6 %all_gather.52 = bf16[1024,256]{1,0:T(8,128)(2,1)S(1)} all-gather(bf16[128,256]{1,0:T(8,128)(2,1)S(1)} %convert_element_type.124), channel_id=1, replica_groups=mesh['patch'=8,'var'=4] {'patch'}, dimensions={0}, use_global_device_ids=true | all-gather | bytes 589824 | tf_op jit(solution)/shard_map/all_gather | solution.py:175
  123.2 82.7 %all-reduce.9 = bf16[1024,1024]{1,0:T(8,128)(2,1)S(1)} all-reduce(f32[1024,1024]{1,0:T(8,128)} %fusion.40), channel_id=1, replica_groups=mesh['patch'=8,'var'=4] {'var'}, use_global_device_ids=true, to_apply=%region_6.7 | all-reduce | flops 1048576 | bytes 6291456 | tf_op jit(solution)/shard_map/psum | solution.py:217
  212.6 11.7 %add_convert_fusion.1 = bf16[12,1024,1024]{2,1,0:T(8,128)(2,1)} fusion(f32[12,1024]{1,0:T(8,128)S(1)} %fusion.25, bf16[12,4,1024]{2,1,0:T(4,128)(2,1)S(1)} %copy-done, bf16[12,4,1024]{2,0,1:T(8,128)(2,1)S(1)} %slice.14), kind=kOutput, calls=%fused_computation.18 | convolution fusion | flops 125829120 | bytes 25411584 | tf_op jit(solution)/shard_map/vpt,vpd->vtd/dot_general | solution.py:63
  232.9 11.6 %fusion.42 = (f32[1024,16]{0,1:T(8,128)S(1)}, f32[12,1024,16]{1,2,0:T(8,128)S(1)}) fusion(bf16[12,1024,1024]{2,1,0:T(8,128)(2,1)} %add_convert_fusion.1, f32[16,1,1024]{2,1,0:T(1,128)S(1)} %fusion.45, pred[12,1024]{1,0:T(8,128)(4,1)S(1)} %fusion.21), kind=kOutput, calls=%fused_computation.93 | convolution fusion | flops 403062784 | bytes 26095616 | tf_op jit(solution)/shard_map/vtd,dh->vth/dot_general | solution.py:67
  246.8 36.6 %multiply_reduce_fusion = (f32[1024,16,12]{0,1,2:T(8,128)}, bf16[12,1024,1024]{1,2,0:T(8,128)(2,1)}) fusion(f32[1024,16,64]{0,2,1:T(8,128)} %bitcast_convert_fusion, bf16[12,1024,1024]{2,1,0:T(8,128)(2,1)} %add_convert_fusion.1, bf16[1024,1024]{1,0:T(8,128)(2,1)} %all-gather.12.cloned.1.call-done), kind=kOutput, calls=%fused_computation.15 | convolution fusion | flops 25819938816 | bytes 57409536 | tf_op jit(solution)/shard_map/vtd,de->vte/dot_general | solution.py:68
  283.4 16.5 %multiply_reduce_fusion.1 = f32[1024,16,64]{0,2,1:T(8,128)} fusion(bf16[1024,16,12,64]{0,3,1,2:T(8,128)(2,1)} %bitcast.143, f32[1024,16,12]{0,1,2:T(8,128)} %get-tuple-element.307), kind=kLoop, calls=%fused_computation.16 | loop fusion | flops 36700160 | bytes 30146560 | tf_op jit(solution)/shard_map/vth,vthe->the/dot_general | solution.py:77
  313.1 7.8 all-gather
  321.1 7.7 all-gather.1
  329.0 83.2 %all-gather.14.cloned.1.call-done = f32[4,1024,1024]{2,1,0:T(8,128)} async-done(((f32[1,1024,1024]{2,1,0:T(8,128)}), f32[4,1024,1024]{2,1,0:T(8,128)}) %all-gather.14.cloned.1.call-update) | async-done | bytes 16777232 | tf_op jit(solution)/shard_map/all_gather | solution.py:18
  422.5 51.9 %while.19 = (s32[]{:T(128)}, f32[1024,16]{0,1:T(8,128)S(1)}, f32[1024,16]{0,1:T(8,128)S(1)}, f32[1024,1024]{0,1:T(8,128)}, f32[4,1024,16]{1,0,2:T(4,128)S(1)}, /...) while((s32[]{:T(128)}, f32[1024,16]{0,1:T(8,128)S(1)}, ...), condition=%wide.region_4.5_spmd, body=%wide.region_3.4_spmd.sunk | while | flops 3244037 | bytes 30277776 | solution.py:23
  450.2 6.9 fusion.72
  482.4 12.0 %fusion.4 = bf16[12,1024,1024]{1,2,0:T(8,128)(2,1)} fusion(f32[1024,1024]{0,1:T(8,128)S(1)} %copy-done.2, f32[12,1024,16]{1,2,0:T(8,128)S(1)} %get-tuple-element.304), kind=kLoop, calls=%fused_computation.14 | loop fusion | flops 25165824 | bytes 30146560 | tf_op jit(solution)/shard_map/convert_element_type | solution.py:105
  494.4 19.3 %fusion.27 = f32[12,1024,1024]{2,1,0:T(8,128)} fusion(bf16[12,1024,16]{1,2,0:T(8,128)(2,1)S(1)} %get-tuple-element.303, f32[16,1,1024]{2,1,0:T(1,128)S(1)} %copy-done.16), kind=kOutput, calls=%fused_computation.69 | convolution fusion | flops 402685952 | bytes 50790400 | tf_op jit(solution)/shard_map/vth,dh->vtd/dot_general | solution.py:119
  513.8 40.2 %fusion.43 = (bf16[12,1024]{1,0:T(8,128)(2,1)S(1)}, bf16[12,1024,1024]{2,1,0:T(8,128)(2,1)}) fusion(f32[12,1024,1024]{2,1,0:T(8,128)} %fusion.27, bf16[12,1024,1024]{1,2,0:T(8,128)(2,1)} %fusion.4, bf16[1024,1024]{1,0:T(8,128)(2,1)S(1)} %copy-done.28), kind=kOutput, calls=%fused_computation.94 | convolution fusion | flops 25807540224 | bytes 102785024 | tf_op jit(solution)/shard_map/vte,de->vtd/dot_general | solution.py:114
  554.0 9.9 fusion.15
  576.8 10.1 convolution_bitcast_fusion.1
  597.8 33.3 %convolution_bitcast_fusion = f32[1024,1024]{1,0:T(8,128)} fusion(bf16[12,1024,1024]{2,1,0:T(8,128)(2,1)} %add_convert_fusion.1, bf16[12,1024,1024]{1,2,0:T(8,128)(2,1)} %fusion.4), kind=kOutput, calls=%fused_computation.28 | convolution fusion | flops 25769803776 | bytes 54525952 | tf_op jit(solution)/shard_map/vtd,vte->de/dot_general | solution.py:121
  636.3 38.9 %all-reduce.6 = (f32[1024]{0:T(1024)S(1)}, f32[1024]{0:T(1024)S(1)}, f32[1024]{0:T(1024)S(1)}) all-reduce(f32[1024]{0:T(1024)S(1)} %bitcast.153, f32[1024]{0:T(1024)S(1)} %dynamic_update_slice.9, f32[1024]{0:T(1024)S(1)} %dynamic_update_slice.11), channel_id=5, replica_groups=mesh['patch'=8,'var'=4] {'patch','var'}, use_global_device_ids=true, to_apply=%region_11.12.clone | all-reduce | flops 3072 | bytes 24576
  680.4 12.2 %fusion.14 = bf16[12,4,1024]{2,1,0:T(4,128)(2,1)} fusion(bf16[12,1024,1024]{2,1,0:T(8,128)(2,1)} %get-tuple-element.317, bf16[12,4,1024]{2,0,1:T(8,128)(2,1)S(1)} %copy-done.11), kind=kOutput, calls=%fused_computation.44 | convolution fusion | flops 100712448 | bytes 25362432 | tf_op jit(solution)/shard_map/vpd,vtd->vpt/dot_general | solution.py:128
  701.9 141.5 %reduce-scatter.21.cloned.1.call-done = f32[32,1024]{1,0:T(8,128)} async-done(((f32[1024,1024]{1,0:T(8,128)}), f32[32,1024]{1,0:T(8,128)}) %reduce-scatter.21.cloned.1.call-update) | async-done | bytes 131088
  843.4 139.8 %reduce-scatter.11.cloned.1.call-done = f32[32,1024]{1,0:T(8,128)} async-done(((f32[1024,1024]{1,0:T(8,128)}), f32[32,1024]{1,0:T(8,128)}) %reduce-scatter.11.cloned.1.call-update) | async-done | bytes 131088 | tf_op jit(solution)/shard_map/reduce_scatter | solution.py:242
  983.2 139.8 %reduce-scatter.13.cloned.1.call-done = f32[32,1024]{1,0:T(8,128)} async-done(((f32[1024,1024]{1,0:T(8,128)}), f32[32,1024]{1,0:T(8,128)}) %reduce-scatter.13.cloned.1.call-update) | async-done | bytes 131088 | tf_op jit(solution)/shard_map/reduce_scatter | solution.py:244
  (171 shorter events, 153.7 us)
Async XLA Ops:
  8.0 204.6 %copy-start = (bf16[12,4,1024]{2,1,0:T(4,128)(2,1)S(1)}, bf16[12,4,1024]{2,1,0:T(4,128)(2,1)}, u32[]{:S(2)}) copy-start(bf16[12,4,1024]{2,1,0:T(4,128)(2,1)} %param.16) | copy-start | bytes 294916
  8.0 216.3 %all-gather.8.cloned.1.call-start = ((), (), s32[]{:S(2)}) async-start(), calls=%async_computation.6 | async-start | bytes 2162688 | tf_op jit(solution)/shard_map/all_gather | solution.py:157
  9.6 216.8 %all-gather.10.cloned.1.call-start = ((), (), s32[]{:S(2)}) async-start(), calls=%async_computation.7 | async-start | bytes 2162688 | tf_op jit(solution)/shard_map/all_gather | solution.py:158
  11.3 235.6 %all-gather.12.cloned.1.call-start = ((), (), s32[]{:S(2)}) async-start(), calls=%async_computation.8 | async-start | bytes 2162688 | tf_op jit(solution)/shard_map/all_gather | solution.py:159
  12.9 399.3 %all-gather.14.cloned.1.call-start = ((), (), s32[]{:S(2)}) async-start(), calls=%async_computation.9 | async-start | bytes 20971520 | tf_op jit(solution)/shard_map/all_gather | solution.py:18
  41.8 170.8 %copy-start.10 = (bf16[12,4,1024]{2,0,1:T(8,128)(2,1)}, bf16[12,4,1024]{2,0,1:T(8,128)(2,1)S(1)}, u32[]{:S(2)}) copy-start(bf16[12,4,1024]{2,0,1:T(8,128)(2,1)S(1)} %slice.14) | copy-start | bytes 294916
  85.2 221.3 %copy-start.22 = (pred[1024]{0:T(1024)(128)(4,1)}, pred[1024]{0:T(1024)(128)(4,1)S(1)}, u32[]{:S(2)}) copy-start(pred[1024]{0:T(1024)(128)(4,1)S(1)} %fusion.31) | copy-start | bytes 3076
  232.9 11.6 %copy-start.15 = (f32[16,1,1024]{2,1,0:T(1,128)}, f32[16,1,1024]{2,1,0:T(1,128)S(1)}, u32[]{:S(2)}) copy-start(f32[16,1,1024]{2,1,0:T(1,128)S(1)} %fusion.45) | copy-start | bytes 196612
  305.4 327.6 %reduce-scatter.17.cloned.1.call-start = ((), (), s32[]{:S(2)}) async-start(), calls=%async_computation.14 | async-start | bytes 1179648 | tf_op jit(solution)/shard_map/reduce_scatter | solution.py:213
  308.2 12.9 %copy-start.17 = (f32[1024,16]{0,1:T(8,128)S(1)}, f32[1024,16]{0,1:T(8,128)}, u32[]{:S(2)}) copy-start(f32[1024,16]{0,1:T(8,128)} %get-tuple-element.308) | copy-start | bytes 196612
  308.3 368.7 %all-gather.16.cloned.1.call-start = ((), (), s32[]{:S(2)}) async-start(), calls=%async_computation.10 | async-start | bytes 1179648 | tf_op jit(solution)/shard_map/all_gather | solution.py:176
  309.9 382.7 %reduce-scatter.19.cloned.1.call-start = ((), (), s32[]{:S(2)}) async-start(), calls=%async_computation.15 | async-start | bytes 294912
  482.4 12.0 %copy-start.16 = (f32[16,1,1024]{2,1,0:T(1,128)S(1)}, f32[16,1,1024]{2,1,0:T(1,128)}, u32[]{:S(2)}) copy-start(f32[16,1,1024]{2,1,0:T(1,128)} %copy-done.15) | copy-start | bytes 196612
  494.4 19.3 %copy-start.28 = (bf16[1024,1024]{1,0:T(8,128)(2,1)S(1)}, bf16[1024,1024]{1,0:T(8,128)(2,1)}, u32[]{:S(2)}) copy-start(bf16[1024,1024]{1,0:T(8,128)(2,1)} %all-gather.12.cloned.1.call-done) | copy-start | bytes 6291460
  564.1 10.9 copy-start.5
  564.1 10.9 copy-start.7
  564.1 10.9 copy-start.23
  574.9 125.5 %reduce-scatter.15.cloned.1.call-start = ((), (), s32[]{:S(2)}) async-start(), calls=%async_computation.13 | async-start | bytes 589824 | tf_op jit(solution)/shard_map/reduce_scatter | solution.py:210
  576.7 10.1 copy-start.3
  576.7 266.7 %reduce-scatter.21.cloned.1.call-start = ((), (), s32[]{:S(2)}) async-start(), calls=%async_computation.16 | async-start | bytes 4325376
  594.8 388.4 %reduce-scatter.11.cloned.1.call-start = ((), (), s32[]{:S(2)}) async-start(), calls=%async_computation.11 | async-start | bytes 4325376 | tf_op jit(solution)/shard_map/reduce_scatter | solution.py:242
  597.8 525.2 %reduce-scatter.13.cloned.1.call-start = ((), (), s32[]{:S(2)}) async-start(), calls=%async_computation.12 | async-start | bytes 4325376 | tf_op jit(solution)/shard_map/reduce_scatter | solution.py:244
  631.1 45.8 %copy-start.9 = (bf16[1024,256]{1,0:T(8,128)(2,1)S(1)}, bf16[1024,256]{1,0:T(8,128)(2,1)}, u32[]{:S(2)}) copy-start(bf16[1024,256]{1,0:T(8,128)(2,1)} %copy-done.8) | copy-start | bytes 1572868
  631.2 45.8 %copy-start.21 = (f32[1024]{0:T(1024)S(1)}, f32[1024]{0:T(1024)}, u32[]{:S(2)}) copy-start(f32[1024]{0:T(1024)} %copy-done.20) | copy-start | bytes 12292
  (16 other events, 45.6 us)
Sparse Core Ops, SparseCore 0:
  12.3 59.3 all-gather.7
  75.1 56.1 all-gather.9
  134.8 58.1 all-gather.11
  305.5 106.6 all-gather.13
  414.7 39.2 all-gather.15
Sparse Core Ops, SparseCore 1:
  309.2 61.9 reduce-scatter.16
  575.0 60.6 reduce-scatter.18
  639.2 61.1 reduce-scatter.14
  703.3 140.1 reduce-scatter.20
  846.3 136.8 reduce-scatter.10
  986.1 136.9 reduce-scatter.12
where the time goes:
time: 1130 us
  waiting for transfers between devices  510 us (45%)
  blocking collectives  236 us (21%)
  matrix products  201 us (18%)
  other arithmetic  84.6 us (7%)
  local copies, waits for them, and re-layouts  82.3 us (7%)
  between operations  16 us (1%)
    unnamed x13, waiting for transfers between devices  142 us
    reduce_scatter x1, waiting for transfers between devices, shards(): lax.psum_scatter(grad_value_w, ('patch', 'var'), scatter_dimension=0, til...  140 us
    reduce_scatter x1, waiting for transfers between devices, shards(): lax.psum_scatter(grad_wq, ('patch', 'var'), scatter_dimension=0, tiled=True)  140 us
    all_gather x1, waiting for transfers between devices, combined_all(): gathered = jax.tree.map(lambda a: lax.all_gather(a, axis), part)  83.2 us
    psum x1, blocking collectives, shards(): grad_att = lax.psum(grad_att_part, 'var').astype(jnp.bfloat16)  82.7 us
    unnamed x2, blocking collectives  78.2 us
    dot_general x1, matrix products, local_backward(): jnp.einsum('vte,de->vtd', grad_values, value_weight, preferred_element_ty...  40.2 us
    dot_general x1, matrix products, local_forward(): jnp.einsum('vtd,de->vte', token, value_weight, preferred_element_type=jnp...  36.6 us
  transfers between devices with their start and end apart: 11, of which 5 were waited for; matrix products, arithmetic and copies ran while one was open for 27% of the time, Pallas kernels for 0%

commit v1 on v0

v1 whole, which is shorter than its diff:
```python
import functools
import math

import jax
import jax.numpy as jnp
from jax import lax
from jax.experimental import pallas as pl
from jax.experimental.pallas import tpu as pltpu
from jax.sharding import PartitionSpec as P

D = 1024
HEADS = 16
HS = D // HEADS
GROUP = 2048
F32 = jnp.float32
BF16 = jnp.bfloat16
NEG = -1e30


def exchange(x, axis, groups=None):
    return lax.all_to_all(x, axis, 0, 0, tiled=True, axis_index_groups=groups)


def spread(x, axis):
    n = lax.axis_size(axis)
    return exchange(jnp.broadcast_to(x[None], (n,) + x.shape).reshape((n * x.shape[0],) + x.shape[1:]), axis)


def flip(x, axis, bit):
    n = lax.axis_size(axis)
    return lax.ppermute(x, axis, [(i, i ^ bit) for i in range(n)])


def hi_lo(x):
    hi = x.astype(BF16)
    return hi, (x - hi.astype(F32)).astype(BF16)


def nt(a, b):
    return lax.dot_general(a, b, (((1,), (1,)), ((), ())), preferred_element_type=F32)


def tn(a, b):
    return lax.dot_general(a, b, (((0,), (0,)), ((), ())), preferred_element_type=F32)


def nn(a, b):
    return jnp.dot(a, b, preferred_element_type=F32)


def forward_kernel(tile, x_ref, ef_ref, vwt_ref, mask_ref, att_ref, prob_ref):
    nv = x_ref.shape[1]
    heads = prob_ref.shape[0]
    present = mask_ref[...] > 0.5

    def step(i, carry):
        cols = pl.ds(pl.multiple_of(i * tile, tile), tile)
        xs = [x_ref[p, :, cols].astype(F32) for p in range(4)]
        for h in range(heads):
            s = jnp.broadcast_to(ef_ref[4, :, h : h + 1], (nv, tile))
            for p in range(4):
                s = s + ef_ref[p, :, h : h + 1] * xs[p]
            s = jnp.where(present, s, NEG)
            w = jnp.where(present, jnp.exp(s - jnp.max(s, axis=0, keepdims=True)), 0.0)
            prob = w / jnp.sum(w, axis=0, keepdims=True)
            prob_ref[h, :, cols] = prob
            a = jnp.concatenate([(prob * x).astype(BF16) for x in xs] + [prob.astype(BF16)], axis=0)
            att_ref[h * HS : (h + 1) * HS, cols] = nn(vwt_ref[h * HS : (h + 1) * HS, :], a).astype(BF16)
        return carry

    lax.fori_loop(0, x_ref.shape[2] // tile, step, 0)


def backward_kernel(tile, x_ref, ef_ref, vw_ref, prob_ref, grad_ref, gx_ref, gv_ref, gs_ref, acc_ref):
    nv = x_ref.shape[1]
    heads = prob_ref.shape[0]
    gv_ref[...] = jnp.zeros_like(gv_ref)
    acc_ref[...] = jnp.zeros_like(acc_ref)

    def step(i, carry):
        cols = pl.ds(pl.multiple_of(i * tile, tile), tile)
        xs = [x_ref[p, :, cols].astype(F32) for p in range(4)]
        gx = [jnp.zeros((nv, tile), F32) for _ in range(4)]
        for h in range(heads):
            hc = slice(h * HS, (h + 1) * HS)
            prob = prob_ref[h, :, cols]
            gh = grad_ref[hc, cols]
            g = nn(vw_ref[:, hc], gh)
            gp = [g[p * nv : (p + 1) * nv] for p in range(5)]
            gprob = gp[4]
            for p in range(4):
                gprob = gprob + xs[p] * gp[p]
            inner = jnp.sum(prob * gprob, axis=0, keepdims=True)
            gs = prob * (gprob - inner)
            for p in range(4):
                gx[p] = gx[p] + prob * gp[p] + ef_ref[p, :, h : h + 1] * gs
            a = jnp.concatenate([(prob * x).astype(BF16) for x in xs] + [prob.astype(BF16)], axis=0)
            gv_ref[:, hc] += nt(a, gh)
            for p in range(5):
                t = gs if p == 4 else gs * xs[p]
                part = t[:, :128]
                for k in range(1, tile // 128):
                    part = part + t[:, k * 128 : (k + 1) * 128]
                acc_ref[p * heads + h] += part
        for p in range(4):
            gx_ref[p, :, cols] = gx[p].astype(BF16)
        return carry

    lax.fori_loop(0, x_ref.shape[2] // tile, step, 0)
    for p in range(5):
        gs_ref[p * nv : (p + 1) * nv, :] = jnp.concatenate(
            [jnp.sum(acc_ref[p * heads + h], axis=1, keepdims=True) for h in range(heads)], axis=1
        )


def attention_forward(x, ef, vwt, mask):
    nv, rows = x.shape[1:]
    cw = vwt.shape[0]
    heads = cw // HS
    return pl.pallas_call(
        functools.partial(forward_kernel, 256),
        out_shape=(
            jax.ShapeDtypeStruct((cw, rows), BF16),
            jax.ShapeDtypeStruct((heads, nv, rows), F32),
        ),
        name="attention_forward",
        cost_estimate=pl.CostEstimate(flops=heads * nv * rows * 800, bytes_accessed=3 << 20, transcendentals=0),
    )(x, ef, vwt, mask)


def attention_backward(x, ef, vw, prob, grad):
    nv, rows = x.shape[1:]
    cw = grad.shape[0]
    heads = cw // HS
    return pl.pallas_call(
        functools.partial(backward_kernel, 256),
        out_shape=(
            jax.ShapeDtypeStruct((4, nv, rows), BF16),
            jax.ShapeDtypeStruct((5 * nv, cw), F32),
            jax.ShapeDtypeStruct((5 * nv, heads), F32),
        ),
        scratch_shapes=[pltpu.VMEM((5 * heads, nv, 128), F32)],
        name="attention_backward",
        cost_estimate=pl.CostEstimate(flops=heads * nv * rows * 1600, bytes_accessed=3 << 20, transcendentals=0),
    )(x, ef, vw, prob, grad)


def shards(pixels, embed, query, w_query, w_key, w_value, w_out, b_out, pos_embed, w_lead, avail, lengths, lead_hours, cotangent):
    n_p = lax.axis_size("patch")
    n_j = lax.axis_size("var")
    p_id = lax.axis_index("patch")
    j_id = lax.axis_index("var")
    vl, _, rows = pixels.shape
    nv = vl * n_j
    cw = w_out.shape[1]
    hl = cw // HS
    dp = embed.shape[2]
    rl = w_value.shape[0]
    eb = -(-5 * vl // 16) * 16 if (5 * vl) % 16 else 5 * vl + 16
    scale = 1.0 / math.sqrt(HS)

    row0 = p_id * rows
    sample = row0 // GROUP
    pos0 = row0 % GROUP
    length = lax.dynamic_index_in_dim(lengths, sample, 0, False)
    lead = lax.dynamic_index_in_dim(lead_hours, sample, 0, False).astype(F32) / 100.0
    mask = lax.dynamic_index_in_dim(avail, sample, 0, False).astype(F32)[:, None]
    valid = (pos0 + jnp.arange(rows, dtype=jnp.int32) < length)[:, None]
    grad_rows = jnp.where(valid, cotangent, jnp.zeros_like(cotangent))
    colsum = jnp.sum(grad_rows.astype(F32), axis=0)

    q_low = query.astype(BF16)
    wq_low = w_query.astype(BF16)
    v_low = w_value.astype(BF16)
    k_low = w_key.astype(BF16)
    q_part = nn(q_low[None, :], wq_low).reshape(n_j, 1, cw)
    q_hi, q_lo = hi_lo(q_part)
    e_own = embed.astype(BF16).reshape(5 * vl, dp)
    e_pad = jnp.broadcast_to(jnp.pad(e_own, ((0, 0), (0, cw - dp)))[None], (n_j, 5 * vl, cw))

    def by_dest(w):
        return w.reshape(rl, n_j, cw).transpose(1, 0, 2)

    tail = jnp.zeros((n_j, eb - 5 * vl - 2, cw), BF16)
    pack = jnp.concatenate([e_pad, q_hi, q_lo, tail, by_dest(v_low), by_dest(k_low)], axis=1)
    got = exchange(pack.reshape(-1, cw), "var").reshape(n_j, eb + 2 * rl, cw)
    e_all = got[:, : 5 * vl, :dp].reshape(5 * nv, dp)
    q_sum = jnp.sum(got[:, 5 * vl : 5 * vl + 2].astype(F32), axis=(0, 1))
    v_blk = got[:, eb : eb + rl].reshape(dp, cw)
    k_blk = got[:, eb + rl :].reshape(dp, cw)

    part = nn(e_all, jnp.concatenate([v_blk, k_blk], axis=1)).astype(BF16)
    small = jnp.stack([q_sum, colsum, lead * colsum])
    s_hi, s_lo = hi_lo(small)
    rc = -(-(5 * nv + 3) // (16 * n_p)) * 16 if n_p <= 8 else -(-(5 * nv + 3) // (8 * n_p)) * 8
    full = rc * n_p
    part = jnp.concatenate(
        [part, jnp.concatenate([s_hi, s_lo], axis=1), jnp.zeros((full - 5 * nv - 3, 2 * cw), BF16)], axis=0
    )
    got2 = exchange(part, "patch").reshape(n_p, rc, 2 * cw)
    total2 = jnp.sum(got2.astype(F32), axis=0)
    extra = (p_id * rc + jnp.arange(rc) >= 5 * nv)[:, None]
    both_hi, both_lo = hi_lo(total2[:, :cw] + total2[:, cw:])
    chunk = jnp.where(extra, jnp.concatenate([both_hi, both_lo], axis=1), total2.astype(BF16))
    vk = spread(chunk, "patch")
    small = vk[5 * nv : 5 * nv + 3].astype(F32)
    small = small[:, :cw] + small[:, cw:]
    qvec = small[0]
    vw_nat = vk[: 5 * nv, :cw]
    ke_nat = vk[: 5 * nv, cw:].astype(F32)
    ef_nat = jnp.sum((ke_nat * (qvec * scale)[None]).reshape(5 * nv, hl, HS), axis=2)
    vw = vw_nat.reshape(nv, 5, cw).transpose(1, 0, 2).reshape(5 * nv, cw)
    ef = ef_nat.reshape(nv, 5, hl).transpose(1, 0, 2)

    pix = lax.all_gather(pixels, "var", axis=0, tiled=True).transpose(1, 0, 2)

    att, prob = attention_forward(pix, ef, vw.T, mask)

    wo = spread(w_out.astype(BF16), "patch")
    held = nt(wo, grad_rows).reshape(n_j, cw, rows)
    bit = 1
    while bit < n_j:
        mine = (j_id // bit) % 2
        pair = held.reshape(held.shape[0] // 2, 2, cw, rows)
        keep = lax.dynamic_index_in_dim(pair, mine, 1, False)
        send = lax.dynamic_index_in_dim(pair, 1 - mine, 1, False).astype(BF16)
        held = keep + flip(send, "var", bit).astype(F32)
        bit *= 2
    grad_att = held.reshape(cw, rows).astype(BF16)

    gx, gv, gs = attention_backward(pix, ef, vw, prob, grad_att)

    gx = gx.reshape(4, n_j, vl, rows).transpose(1, 2, 0, 3).reshape(nv, 4, rows)
    gx = exchange(gx, "var").reshape(n_j, vl, 4, rows)
    grad_pixels = jnp.sum(gx.astype(F32), axis=0).astype(BF16)

    blocks = [att]
    bit = 1
    while bit < n_j:
        blocks = blocks + [flip(b, "var", bit) for b in blocks]
        bit *= 2
    wo_blocks = wo.reshape(n_j, cw, cw)
    result = None
    gwo = []
    for k, b in enumerate(blocks):
        term = tn(b, lax.dynamic_index_in_dim(wo_blocks, j_id ^ k, 0, False))
        result = term if result is None else result + term
        gwo.append(nn(b, grad_rows).astype(BF16))
    gwo = jnp.stack(gwo)
    bit = 1
    while bit < n_j:
        pair = gwo.reshape(n_j // (2 * bit), 2, bit, cw, cw)
        gwo = jnp.where((j_id // bit) % 2 == 1, pair[:, ::-1], pair).reshape(n_j, cw, cw)
        bit *= 2
    gwo = exchange(gwo.reshape(D, cw), "patch").reshape(n_p, dp, cw)
    grad_w_out = jnp.sum(gwo.astype(F32), axis=0)

    parts = GROUP // rows
    owners = n_p // parts
    per = pos_embed.shape[0]
    groups = [[parts * i + k for i in range(owners)] for k in range(parts)]
    there = [(k * owners + i, parts * i + k) for i in range(owners) for k in range(parts)]
    back = [(b, a) for a, b in there]
    pos = lax.ppermute(pos_embed.astype(BF16), "patch", there)
    pos = exchange(jnp.broadcast_to(pos[None], (owners, per, cw)).reshape(rows, cw), "patch", groups)
    gpos = exchange(grad_rows, "patch", groups).reshape(owners, per, cw)
    gpos = jnp.sum(gpos.astype(F32), axis=0).astype(BF16)
    grad_pos = lax.ppermute(gpos, "patch", back).astype(F32)

    bl_hi, bl_lo = hi_lo(jnp.stack([b_out, w_lead]))
    del bl_lo
    bl = lax.all_gather(bl_hi, ("patch", "var"), axis=1, tiled=True)
    bl = lax.dynamic_slice_in_dim(bl, j_id * cw, cw, 1).astype(F32)
    result = result + bl[0] + pos.astype(F32) + lead * bl[1]
    mixed = jnp.where(valid, result, 0.0).astype(BF16)

    gs_hi, gs_lo = hi_lo(gs)
    z = jnp.concatenate([gv.astype(BF16), gs_hi, gs_lo, jnp.zeros((5 * nv, 128 - 2 * hl), BF16)], axis=1)
    z = z.reshape(5, nv, cw + 128).transpose(1, 0, 2).reshape(5 * nv, cw + 128)
    z = jnp.concatenate([z, jnp.zeros((full - 5 * nv, cw + 128), BF16)], axis=0)
    z = jnp.sum(exchange(z, "patch").reshape(n_p, rc, cw + 128).astype(F32), axis=0)
    gst_hi, gst_lo = hi_lo(z[:, cw : cw + hl] + z[:, cw + hl : cw + 2 * hl])
    z = jnp.concatenate([z[:, :cw].astype(BF16), gst_hi, gst_lo, jnp.zeros((rc, 128 - 2 * hl), BF16)], axis=1)
    z = spread(z, "patch")
    gst = z[: 5 * nv, cw : cw + hl].astype(F32) + z[: 5 * nv, cw + hl : cw + 2 * hl].astype(F32)
    gq_own = jnp.sum(jnp.repeat(gst, HS, axis=1) * ke_nat, axis=0) * scale
    fold = jnp.sum((k_blk.astype(F32) * (qvec * scale)[None]).reshape(dp, hl, HS), axis=2)
    rows4 = jnp.stack([gq_own, qvec, small[1], small[2]])
    r_hi, r_lo = hi_lo(rows4)
    lanes = jnp.pad(fold.astype(BF16), ((0, 8), (0, 128 - hl)))
    last = jnp.concatenate(
        [z[: 5 * nv], jnp.concatenate([jnp.concatenate([r_hi, r_lo], axis=0), jnp.zeros((8, 128), BF16)], axis=1)], axis=0
    )
    last = jnp.concatenate([last, jnp.pad(lanes[:dp], ((0, 0), (cw, 0)))], axis=0)
    allz = lax.all_gather(last, "var", axis=0, tiled=False)
    zz = allz[:, : 5 * nv, :cw]
    gsa = allz[:, : 5 * nv, cw : cw + hl].astype(F32) + allz[:, : 5 * nv, cw + hl : cw + 2 * hl].astype(F32)
    rowsa = allz[:, 5 * nv : 5 * nv + 4, :cw].astype(F32) + allz[:, 5 * nv + 4 : 5 * nv + 8, :cw].astype(F32)
    rowsa = rowsa.transpose(1, 0, 2).reshape(4, D)
    gq, qv = rowsa[0], rowsa[1]
    folda = allz[:, 5 * nv + 8 :, cw : cw + hl].astype(F32)
    e_mine = lax.dynamic_slice_in_dim(e_all, j_id * rl, rl, 1)
    grad_w_value = jnp.einsum("rd,jrc->djc", e_mine, zz, preferred_element_type=F32).reshape(rl, D)
    gfold = jnp.einsum("rd,jrh->djh", e_mine.astype(F32), gsa, precision=lax.Precision.HIGHEST).reshape(rl, HEADS)
    grad_w_key = jnp.repeat(gfold, HS, axis=1) * (qv * scale)[None]
    v_rows = lax.all_gather(v_low, "var", axis=0, tiled=True)
    z_mine = lax.dynamic_slice_in_dim(zz, j_id * 5 * vl, 5 * vl, 1)
    gs_mine = lax.dynamic_slice_in_dim(gsa, j_id * 5 * vl, 5 * vl, 1)
    ge = jnp.einsum("jrc,djc->rd", z_mine, v_rows.reshape(dp, n_j, cw), preferred_element_type=F32)
    ge = ge + jnp.einsum("jrh,jdh->rd", gs_mine, folda, precision=lax.Precision.HIGHEST)
    grad_embed = ge.reshape(vl, 5, dp)
    grad_w_query = q_low.astype(F32)[:, None] * gq[None, :]
    grad_query = jnp.sum(wq_low.astype(F32) * gq[None, :], axis=1)
    out0 = (p_id * n_j + j_id) * rl
    grad_bias = lax.dynamic_slice_in_dim(rowsa[2], out0, rl)
    grad_lead = lax.dynamic_slice_in_dim(rowsa[3], out0, rl)
    return (
        mixed,
        grad_pixels,
        grad_embed,
        grad_query,
        grad_w_query,
        grad_w_key,
        grad_w_value,
        grad_w_out,
        grad_bias,
        grad_pos,
        grad_lead,
    )


def solution(mesh):
    both = P(("patch", "var"))
    rows2 = P(("patch", "var"), None)
    return jax.shard_map(
        shards,
        mesh=mesh,
        in_specs=(
            P("var", None, "patch"),
            P("var", None, "patch"),
            both,
            rows2,
            rows2,
            rows2,
            P("patch", "var"),
            both,
            P("patch", "var"),
            both,
            P(),
            P(),
            P(),
            P("patch", "var"),
        ),
        out_specs=(
            P("patch", "var"),
            P("var", None, "patch"),
            P("var", None, "patch"),
            both,
            rows2,
            rows2,
            rows2,
            P("patch", "var"),
            both,
            P("patch", "var"),
            both,
        ),
        check_vma=False,
    )
```

time: 1130 us -> 258 us (0.23)
  waiting for transfers between devices: 510 us -> 56.8 us
  matrix products: 201 us -> 14.4 us
  blocking collectives: 236 us -> 54.4 us
  other arithmetic: 84.6 us -> 22.6 us
  starting transfers between devices: 0.47 us -> 57.5 us
  local copies, waits for them, and re-layouts: 82.3 us -> 26.3 us
    reduce_scatter x4 -> x0, waiting for transfers between devices: 285 us -> none  [the longest x1 140 us: shards(): lax.psum_scatter(grad_value_w, ('patch', 'var'), scatter_dimension=0, til...]
    dot_general x16 -> x15, matrix products: 201 us -> 14.4 us  [the longest x6 7.02 us: nn(): return jnp.dot(a, b, preferred_element_type=F32)]
    unnamed x13 -> x1, waiting for transfers between devices: 142 us -> 0.02 us
    all_gather x5 -> x1, waiting for transfers between devices: 83.2 us -> 0.01 us  [shards(): allz = lax.all_gather(last, 'var', axis=0, tiled=False)]
    psum x1 -> x0, blocking collectives: 82.7 us -> none  [shards(): grad_att = lax.psum(grad_att_part, 'var').astype(jnp.bfloat16)]
    unnamed x2 -> x0, blocking collectives: 78.2 us -> none
    all_to_all x0 -> x10, waiting for transfers between devices: none -> 51.7 us  [exchange(): return lax.all_to_all(x, axis, 0, 0, tiled=True, axis_index_groups=groups)]
    all_to_all x0 -> x10, starting transfers between devices: none -> 51 us  [exchange(): return lax.all_to_all(x, axis, 0, 0, tiled=True, axis_index_groups=groups)]
  transfers between devices with their start and end apart: 11 -> 18, of which waited for: 5 -> 9; matrix products, arithmetic and copies ran while one was open for 27% -> 17% of each run, Pallas kernels for 0% -> 3%
where the time goes in v1:
time: 258 us; the launch traced here: 256 us
  starting transfers between devices  57.5 us (22%)
  waiting for transfers between devices  56.8 us (22%)
  blocking collectives  54.4 us (21%)
  local copies, waits for them, and re-layouts  26.3 us (10%)
  other arithmetic  22.6 us (9%)
  between operations  15.4 us (6%)
  matrix products  14.4 us (6%)
  Pallas kernels  8.61 us (3%)
    all_to_all x10, waiting for transfers between devices, exchange(): return lax.all_to_all(x, axis, 0, 0, tiled=True, axis_index_groups=groups)  51.7 us
    all_to_all x10, starting transfers between devices, exchange(): return lax.all_to_all(x, axis, 0, 0, tiled=True, axis_index_groups=groups)  51 us
    all_gather x1, blocking collectives, shards(): bl = lax.all_gather(bl_hi, ('patch', 'var'), axis=1, tiled=True)  42 us
    dot_general x6, matrix products, nn(): return jnp.dot(a, b, preferred_element_type=F32)  7.02 us
    all_gather x1, blocking collectives, shards(): pix = lax.all_gather(pixels, 'var', axis=0, tiled=True).transpose(1, 0, 2)  6.54 us
    all_gather x1, blocking collectives, shards(): v_rows = lax.all_gather(v_low, 'var', axis=0, tiled=True)  5.79 us
  transfers between devices with their start and end apart: 18, of which 9 were waited for; matrix products, arithmetic and copies ran while one was open for 17% of the time, Pallas kernels for 3%

profile of v1, /device:TPU:0, one launch (start us, length us, event | category | flops | bytes accessed | tf_op | source)
XLA Modules:
  0.0 256.0 jit_solution(7943627609413302146)
XLA Ops:
  11.2 3.3 %concatenate.37 = bf16[4,128,256]{2,1,0:T(8,128)(2,1)} concatenate(bf16[4,60,256]{2,1,0:T(8,128)(2,1)S(1)} %broadcast_in_dim.52, bf16[4,1,256]{2,1,0:T(2,128)(2,1)S(1)} %copy.143, bf16[4,1,256]{2,1,0:T(2,128)(2,1)S(1)} %copy.144, bf16[4,2,256]{2,1,0:T(2,128)(2,1)S(1)} %broadcast_in_dim.53, bf16[4,32,256]{2,1,0:T(8,128)(2,1)S(1)} %copy.145, bf16[4,32,256]{2,1,0:T(8,128)(2,1)S(1)} %copy.146), dimensions={1} | concatenate | bytes 524288 | tf_op jit(solution)/shard_map/concatenate | solution.py:185
  14.5 4.4 %all-to-all-start = ((bf16[4,128,256]{2,1,0:T(8,128)(2,1)}), bf16[4,128,256]{2,1,0:T(8,128)(2,1)S(1)}, u32[]{:S(2)}, u32[]{:S(2)}) async-start(bf16[4,128,256]{2,1,0:T(8,128)(2,1)} %concatenate.37), calls=%async_computation | async-start | bytes 524288 | tf_op jit(solution)/shard_map/all_to_all | solution.py:21
  26.1 6.4 %all-to-all-start.1 = ((bf16[8,32,512]{2,1,0:T(8,128)(2,1)}), bf16[8,32,512]{2,1,0:T(8,128)(2,1)S(1)}, u32[]{:S(2)}, u32[]{:S(2)}) async-start(bf16[8,32,512]{2,1,0:T(8,128)(2,1)} %bitcast.11), calls=%async_computation.1 | async-start | bytes 524288 | tf_op jit(solution)/shard_map/all_to_all | solution.py:21
  35.3 6.6 %all-to-all-done.1 = bf16[8,32,512]{2,1,0:T(8,128)(2,1)S(1)} async-done(((bf16[8,32,512]{2,1,0:T(8,128)(2,1)}), bf16[8,32,512]{2,1,0:T(8,128)(2,1)S(1)}, u32[]{:S(2)}, u32[]{:S(2)}) %all-to-all-start.1) | async-done | bytes 262176 | tf_op jit(solution)/shard_map/all_to_all | solution.py:21
  42.7 3.5 %all-to-all-start.3 = ((bf16[8,128,256]{2,1,0:T(8,128)(2,1)}), bf16[8,128,256]{2,1,0:T(8,128)(2,1)S(1)}, u32[]{:S(2)}, u32[]{:S(2)}) async-start(bf16[8,128,256]{2,1,0:T(8,128)(2,1)} %broadcast_in_dim.57), calls=%async_computation.3 | async-start | bytes 1048576 | tf_op jit(solution)/shard_map/all_to_all | solution.py:21
  46.3 42.0 %all-gather.1 = bf16[32,32,2]{1,2,0:T(2,128)(2,1)S(1)} all-gather(bf16[1,32,2]{1,2,0:T(2,128)(2,1)S(1)} %maximum_bitcast_fusion), channel_id=1, replica_groups=mesh['patch'=8,'var'=4] {'patch','var'}, dimensions={0}, use_global_device_ids=true | all-gather | bytes 4224 | tf_op jit(solution)/shard_map/all_gather | solution.py:272
  89.1 6.5 %all_gather.15 = bf16[48,4,1024]{2,1,0:T(4,128)(2,1)S(1)} all-gather(bf16[12,4,1024]{2,1,0:T(4,128)(2,1)S(1)} %copy-done.14), channel_id=1, replica_groups=mesh['patch'=8,'var'=4] {'var'}, dimensions={0}, use_global_device_ids=true | all-gather | bytes 491520 | tf_op jit(solution)/shard_map/all_gather | solution.py:215
  95.7 3.5 %all-to-all-start.9 = ((bf16[4,256,256]{2,1,0:T(8,128)(2,1)}), bf16[4,256,256]{2,1,0:T(8,128)(2,1)S(1)}, u32[]{:S(2)}, u32[]{:S(2)}) async-start(bf16[4,256,256]{2,1,0:T(8,128)(2,1)} %bitcast.68), calls=%async_computation.9 | async-start | bytes 1048576 | tf_op jit(solution)/shard_map/all_to_all | solution.py:21
  103.7 10.8 %all-to-all-done.9 = bf16[4,256,256]{2,1,0:T(8,128)(2,1)S(1)} async-done(((bf16[4,256,256]{2,1,0:T(8,128)(2,1)}), bf16[4,256,256]{2,1,0:T(8,128)(2,1)S(1)}, u32[]{:S(2)}, u32[]{:S(2)}) %all-to-all-start.9) | async-done | bytes 524320 | tf_op jit(solution)/shard_map/all_to_all | solution.py:21
  115.2 3.4 %all-to-all-start.2 = ((bf16[8,32,512]{2,1,0:T(8,128)(2,1)}), bf16[8,32,512]{2,1,0:T(8,128)(2,1)S(1)}, u32[]{:S(2)}, u32[]{:S(2)}) async-start(bf16[8,32,512]{2,1,0:T(8,128)(2,1)} %broadcast_in_dim.56), calls=%async_computation.2 | async-start | bytes 524288 | tf_op jit(solution)/shard_map/all_to_all | solution.py:21
  118.6 5.8 %all_gather.19 = bf16[128,1024]{1,0:T(8,128)(2,1)S(1)} all-gather(bf16[32,1024]{1,0:T(8,128)(2,1)S(1)} %convert_element_type.257), channel_id=1, replica_groups=mesh['patch'=8,'var'=4] {'var'}, dimensions={0}, use_global_device_ids=true | all-gather | bytes 327680 | tf_op jit(solution)/shard_map/all_gather | solution.py:306
  136.8 3.9 %attention_forward.1 = (bf16[256,1024]{1,0:T(8,128)(2,1)}, f32[4,48,1024]{2,1,0:T(8,128)}) custom-call(bf16[4,48,1024]{2,1,0:T(8,128)(2,1)} %bitcast.153, f32[5,48,4]{2,1,0:T(8,128)} %bitcast.171, bf16[256,240]{1,0:T(8,128)(2,1)} %copy.150.vwt_ref, f32[48,1]{1,0:T(8,128)} %copy.151.mask_ref), custom_call_target="tpu_custom_call" | custom-call | flops 157286400 | bytes 3145728 | tf_op jit(solution)/shard_map/attention_forward/pallas_call | solution.py:120
  143.5 5.0 %collective-permute-done.5 = bf16[1,256,1024]{2,1,0:T(8,128)(2,1)} collective-permute-done((bf16[1,256,1024]{2,1,0:T(8,128)(2,1)}, bf16[1,256,1024]{2,1,0:T(8,128)(2,1)}, u32[]{:S(2)}, u32[]{:S(2)}) %collective-permute-start.5) | collective-permute-done | bytes 524320 | tf_op jit(solution)/shard_map/ppermute | solution.py:31
  150.5 4.8 %attention_backward.1 = (bf16[4,48,1024]{2,1,0:T(8,128)(2,1)}, f32[240,256]{1,0:T(8,128)}, f32[240,4]{1,0:T(8,128)}) custom-call(bf16[4,48,1024]{2,1,0:T(8,128)(2,1)} %bitcast.154, f32[5,48,4]{2,1,0:T(8,128)} %bitcast.172, bf16[240,256]{1,0:T(8,128)(2,1)} %bitcast.170, f32[4,48,1024]{2,1,0:T(8,128)} %get-tuple-element.17.prob_ref, ...), custom_call_target="tpu_custom_call" | custom-call | flops 314572800 | bytes 3145728 | tf_op jit(solution)/shard_map/attention_backward/pallas_call | solution.py:135
  158.1 13.5 %all-to-all-start.6 = ((bf16[8,32,384]{2,1,0:T(8,128)(2,1)}), bf16[8,32,384]{2,1,0:T(8,128)(2,1)S(1)}, u32[]{:S(2)}, u32[]{:S(2)}) async-start(bf16[8,32,384]{2,1,0:T(8,128)(2,1)} %bitcast.29), calls=%async_computation.6 | async-start | bytes 393216 | tf_op jit(solution)/shard_map/all_to_all | solution.py:21
  175.7 3.7 %all-to-all-done.6 = bf16[8,32,384]{2,1,0:T(8,128)(2,1)S(1)} async-done(((bf16[8,32,384]{2,1,0:T(8,128)(2,1)}), bf16[8,32,384]{2,1,0:T(8,128)(2,1)S(1)}, u32[]{:S(2)}, u32[]{:S(2)}) %all-to-all-start.6) | async-done | bytes 196640 | tf_op jit(solution)/shard_map/all_to_all | solution.py:21
  180.3 3.4 %all-to-all-start.7 = ((bf16[8,32,384]{2,1,0:T(8,128)(2,1)}), bf16[8,32,384]{2,1,0:T(8,128)(2,1)S(1)}, u32[]{:S(2)}, u32[]{:S(2)}) async-start(bf16[8,32,384]{2,1,0:T(8,128)(2,1)} %broadcast_in_dim.100), calls=%async_computation.7 | async-start | bytes 393216 | tf_op jit(solution)/shard_map/all_to_all | solution.py:21
  188.8 2.7 %all-to-all-done.7 = bf16[8,32,384]{2,1,0:T(8,128)(2,1)S(1)} async-done(((bf16[8,32,384]{2,1,0:T(8,128)(2,1)}), bf16[8,32,384]{2,1,0:T(8,128)(2,1)S(1)}, u32[]{:S(2)}, u32[]{:S(2)}) %all-to-all-start.7) | async-done | bytes 196640 | tf_op jit(solution)/shard_map/all_to_all | solution.py:21
  193.2 4.2 %all-to-all-start.4 = ((bf16[4,256,256]{2,1,0:T(8,128)(2,1)}), bf16[4,256,256]{2,1,0:T(8,128)(2,1)}, u32[]{:S(2)}, u32[]{:S(2)}) async-start(bf16[4,256,256]{2,1,0:T(8,128)(2,1)} %broadcast_in_dim.96), calls=%async_computation.4 | async-start | bytes 1048576 | tf_op jit(solution)/shard_map/all_to_all | solution.py:21
  198.8 8.9 %all-to-all-done.4 = bf16[4,256,256]{2,1,0:T(8,128)(2,1)} async-done(((bf16[4,256,256]{2,1,0:T(8,128)(2,1)}), bf16[4,256,256]{2,1,0:T(8,128)(2,1)}, u32[]{:S(2)}, u32[]{:S(2)}) %all-to-all-start.4) | async-done | bytes 524320 | tf_op jit(solution)/shard_map/all_to_all | solution.py:21
  207.7 3.5 %all-to-all-start.5 = ((bf16[48,4,1024]{2,1,0:T(4,128)(2,1)}), bf16[48,4,1024]{2,1,0:T(4,128)(2,1)S(1)}, u32[]{:S(2)}, u32[]{:S(2)}) async-start(bf16[48,4,1024]{2,1,0:T(4,128)(2,1)} %bitcast.140), calls=%async_computation.5 | async-start | bytes 786432 | tf_op jit(solution)/shard_map/all_to_all | solution.py:21
  212.2 7.7 %all-to-all-done.5 = bf16[48,4,1024]{2,1,0:T(4,128)(2,1)S(1)} async-done(((bf16[48,4,1024]{2,1,0:T(4,128)(2,1)}), bf16[48,4,1024]{2,1,0:T(4,128)(2,1)S(1)}, u32[]{:S(2)}, u32[]{:S(2)}) %all-to-all-start.5) | async-done | bytes 393248 | tf_op jit(solution)/shard_map/all_to_all | solution.py:21
  219.9 5.3 %all-to-all-start.8 = ((bf16[8,128,256]{2,1,0:T(8,128)(2,1)}), bf16[8,128,256]{2,1,0:T(8,128)(2,1)S(1)}, u32[]{:S(2)}, u32[]{:S(2)}) async-start(bf16[8,128,256]{2,1,0:T(8,128)(2,1)} %bitcast.66), calls=%async_computation.8 | async-start | bytes 1048576 | tf_op jit(solution)/shard_map/all_to_all | solution.py:21
  230.6 8.9 %all-to-all-done.8 = bf16[8,128,256]{2,1,0:T(8,128)(2,1)S(1)} async-done(((bf16[8,128,256]{2,1,0:T(8,128)(2,1)}), bf16[8,128,256]{2,1,0:T(8,128)(2,1)S(1)}, u32[]{:S(2)}, u32[]{:S(2)}) %all-to-all-start.8) | async-done | bytes 524320 | tf_op jit(solution)/shard_map/all_to_all | solution.py:21
  (198 shorter events, 69.0 us)
Async XLA Ops:
  11.2 21.3 %copy-start.11 = (f32[256,256]{1,0:T(8,128)S(1)}, f32[256,256]{1,0:T(8,128)}, u32[]{:S(2)}) copy-start(f32[256,256]{1,0:T(8,128)} %param.22) | copy-start | bytes 786436
  14.5 10.4 %all-to-all-start = ((bf16[4,128,256]{2,1,0:T(8,128)(2,1)}), bf16[4,128,256]{2,1,0:T(8,128)(2,1)S(1)}, u32[]{:S(2)}, u32[]{:S(2)}) async-start(bf16[4,128,256]{2,1,0:T(8,128)(2,1)} %concatenate.37), calls=%async_computation | async-start | bytes 524288 | tf_op jit(solution)/shard_map/all_to_all | solution.py:21
  25.0 21.3 %copy-start.17 = (f32[32]{0:T(128)S(1)}, f32[32]{0:T(128)}, u32[]{:S(2)}) copy-start(f32[32]{0:T(128)} %param.23) | copy-start | bytes 388
  25.0 21.3 %copy-start.18 = (f32[32]{0:T(128)S(1)}, f32[32]{0:T(128)}, u32[]{:S(2)}) copy-start(f32[32]{0:T(128)} %param.21) | copy-start | bytes 388
  25.0 64.1 %copy-start.14 = (bf16[12,4,1024]{2,1,0:T(4,128)(2,1)S(1)}, bf16[12,4,1024]{2,1,0:T(4,128)(2,1)}, u32[]{:S(2)}) copy-start(bf16[12,4,1024]{2,1,0:T(4,128)(2,1)} %param.14) | copy-start | bytes 294916
  26.1 15.8 %all-to-all-start.1 = ((bf16[8,32,512]{2,1,0:T(8,128)(2,1)}), bf16[8,32,512]{2,1,0:T(8,128)(2,1)S(1)}, u32[]{:S(2)}, u32[]{:S(2)}) async-start(bf16[8,32,512]{2,1,0:T(8,128)(2,1)} %bitcast.11), calls=%async_computation.1 | async-start | bytes 524288 | tf_op jit(solution)/shard_map/all_to_all | solution.py:21
  33.1 155.6 %collective-permute-start.3 = (bf16[256,256]{1,0:T(8,128)(2,1)}, bf16[256,256]{1,0:T(8,128)(2,1)}, u32[]{:S(2)}, u32[]{:S(2)}) collective-permute-start(bf16[256,256]{1,0:T(8,128)(2,1)} %convert_element_type.277), channel_id=1, source_target_pairs={{0,0},{16,4},{4,8},{20,12},{8,16},{24,20},{12,24},{28,28},{1,1},{1... | collective-permute-start | bytes 393224 | tf_op jit(solution)/shard_map/ppermute | solution.py:264
  42.7 53.0 %all-to-all-start.3 = ((bf16[8,128,256]{2,1,0:T(8,128)(2,1)}), bf16[8,128,256]{2,1,0:T(8,128)(2,1)S(1)}, u32[]{:S(2)}, u32[]{:S(2)}) async-start(bf16[8,128,256]{2,1,0:T(8,128)(2,1)} %broadcast_in_dim.57), calls=%async_computation.3 | async-start | bytes 1048576 | tf_op jit(solution)/shard_map/all_to_all | solution.py:21
  95.7 18.7 %all-to-all-start.9 = ((bf16[4,256,256]{2,1,0:T(8,128)(2,1)}), bf16[4,256,256]{2,1,0:T(8,128)(2,1)S(1)}, u32[]{:S(2)}, u32[]{:S(2)}) async-start(bf16[4,256,256]{2,1,0:T(8,128)(2,1)} %bitcast.68), calls=%async_computation.9 | async-start | bytes 1048576 | tf_op jit(solution)/shard_map/all_to_all | solution.py:21
  103.2 25.0 %copy-start.16 = (f32[32]{0:T(128)S(1)}, f32[32]{0:T(128)}, u32[]{:S(2)}) copy-start(f32[32]{0:T(128)} %param.16) | copy-start | bytes 388
  103.2 27.1 %collective-permute-start.4 = (bf16[2,256,1024]{2,1,0:T(8,128)(2,1)S(1)}, bf16[2,256,1024]{2,1,0:T(8,128)(2,1)}, u32[]{:S(2)}, u32[]{:S(2)}) collective-permute-start(bf16[2,256,1024]{2,1,0:T(8,128)(2,1)S(1)} %fusion.10), channel_id=1, source_target_pairs={{0,1},{1,0},{2,3},{3,2},{4,5},{5,4},{6,7},{7,6},{8,9},{9,8},{10,11... | collective-permute-start | bytes 3145736 | tf_op jit(solution)/shard_map/ppermute | solution.py:31
  115.2 15.1 %all-to-all-start.2 = ((bf16[8,32,512]{2,1,0:T(8,128)(2,1)}), bf16[8,32,512]{2,1,0:T(8,128)(2,1)S(1)}, u32[]{:S(2)}, u32[]{:S(2)}) async-start(bf16[8,32,512]{2,1,0:T(8,128)(2,1)} %broadcast_in_dim.56), calls=%async_computation.2 | async-start | bytes 524288 | tf_op jit(solution)/shard_map/all_to_all | solution.py:21
  127.5 2.0 collective-permute-start.6
  133.4 15.1 %collective-permute-start.5 = (bf16[1,256,1024]{2,1,0:T(8,128)(2,1)}, bf16[1,256,1024]{2,1,0:T(8,128)(2,1)}, u32[]{:S(2)}, u32[]{:S(2)}) collective-permute-start(bf16[1,256,1024]{2,1,0:T(8,128)(2,1)} %dynamic-slice_convert_fusion), channel_id=1, source_target_pairs={{0,2},{1,3},{2,0},{3,1},{4,6},{5,7},{6,4},{7,5},{8,10},{9,11},{10,... | collective-permute-start | bytes 1572872 | tf_op jit(solution)/shard_map/ppermute | solution.py:31
  140.7 43.1 %collective-permute-start.1 = (bf16[256,1024]{1,0:T(8,128)(2,1)}, bf16[256,1024]{1,0:T(8,128)(2,1)S(1)}, u32[]{:S(2)}, u32[]{:S(2)}) collective-permute-start(bf16[256,1024]{1,0:T(8,128)(2,1)} %get-tuple-element.16), channel_id=1, source_target_pairs={{0,2},{1,3},{2,0},{3,1},{4,6},{5,7},{6,4},{7,5},{8,10},{9,11},{10,... | collective-permute-start | bytes 1572872 | tf_op jit(solution)/shard_map/ppermute | solution.py:31
  141.6 31.4 %collective-permute-start = (bf16[256,1024]{1,0:T(8,128)(2,1)}, bf16[256,1024]{1,0:T(8,128)(2,1)}, u32[]{:S(2)}, u32[]{:S(2)}) collective-permute-start(bf16[256,1024]{1,0:T(8,128)(2,1)} %get-tuple-element.16), channel_id=1, source_target_pairs={{0,1},{1,0},{2,3},{3,2},{4,5},{5,4},{6,7},{7,6},{8,9},{9,8},{10,11... | collective-permute-start | bytes 1572872 | tf_op jit(solution)/shard_map/ppermute | solution.py:31
  150.5 21.2 %copy-start.2 = (bf16[256,1024]{1,0:T(8,128)(2,1)S(1)}, bf16[256,1024]{1,0:T(8,128)(2,1)}, u32[]{:S(2)}) copy-start(bf16[256,1024]{1,0:T(8,128)(2,1)} %get-tuple-element.16) | copy-start | bytes 1572868
  158.1 21.3 %all-to-all-start.6 = ((bf16[8,32,384]{2,1,0:T(8,128)(2,1)}), bf16[8,32,384]{2,1,0:T(8,128)(2,1)S(1)}, u32[]{:S(2)}, u32[]{:S(2)}) async-start(bf16[8,32,384]{2,1,0:T(8,128)(2,1)} %bitcast.29), calls=%async_computation.6 | async-start | bytes 393216 | tf_op jit(solution)/shard_map/all_to_all | solution.py:21
  173.0 12.1 %collective-permute-start.2 = (bf16[256,1024]{1,0:T(8,128)(2,1)}, bf16[256,1024]{1,0:T(8,128)(2,1)S(1)}, u32[]{:S(2)}, u32[]{:S(2)}) collective-permute-start(bf16[256,1024]{1,0:T(8,128)(2,1)} %collective-permute-done), channel_id=1, source_target_pairs={{0,2},{1,3},{2,0},{3,1},{4,6},{5,7},{6,4},{7,5},{8,10},{9,11},{10,... | collective-permute-start | bytes 1572872 | tf_op jit(solution)/shard_map/ppermute | solution.py:31
  180.3 11.1 %all-to-all-start.7 = ((bf16[8,32,384]{2,1,0:T(8,128)(2,1)}), bf16[8,32,384]{2,1,0:T(8,128)(2,1)S(1)}, u32[]{:S(2)}, u32[]{:S(2)}) async-start(bf16[8,32,384]{2,1,0:T(8,128)(2,1)} %broadcast_in_dim.100), calls=%async_computation.7 | async-start | bytes 393216 | tf_op jit(solution)/shard_map/all_to_all | solution.py:21
  193.2 14.5 %all-to-all-start.4 = ((bf16[4,256,256]{2,1,0:T(8,128)(2,1)}), bf16[4,256,256]{2,1,0:T(8,128)(2,1)}, u32[]{:S(2)}, u32[]{:S(2)}) async-start(bf16[4,256,256]{2,1,0:T(8,128)(2,1)} %broadcast_in_dim.96), calls=%async_computation.4 | async-start | bytes 1048576 | tf_op jit(solution)/shard_map/all_to_all | solution.py:21
  197.3 42.9 %all-gather.4.cloned.1.call-start = ((), (), s32[]{:S(2)}) async-start(), calls=%async_computation.10 | async-start | bytes 1443840 | tf_op jit(solution)/shard_map/all_gather | solution.py:295
  207.7 12.2 %all-to-all-start.5 = ((bf16[48,4,1024]{2,1,0:T(4,128)(2,1)}), bf16[48,4,1024]{2,1,0:T(4,128)(2,1)S(1)}, u32[]{:S(2)}, u32[]{:S(2)}) async-start(bf16[48,4,1024]{2,1,0:T(4,128)(2,1)} %bitcast.140), calls=%async_computation.5 | async-start | bytes 786432 | tf_op jit(solution)/shard_map/all_to_all | solution.py:21
  219.9 19.6 %all-to-all-start.8 = ((bf16[8,128,256]{2,1,0:T(8,128)(2,1)}), bf16[8,128,256]{2,1,0:T(8,128)(2,1)S(1)}, u32[]{:S(2)}, u32[]{:S(2)}) async-start(bf16[8,128,256]{2,1,0:T(8,128)(2,1)} %bitcast.66), calls=%async_computation.8 | async-start | bytes 1048576 | tf_op jit(solution)/shard_map/all_to_all | solution.py:21
  (16 other events, 174.2 us)
Sparse Core Ops, SparseCore 0:
  199.7 18.8 all-gather.3

commit v2 on v1

v2 whole, which is shorter than its diff:
```python
import functools
import math

import jax
import jax.numpy as jnp
from jax import lax
from jax.experimental import pallas as pl
from jax.experimental.pallas import tpu as pltpu
from jax.sharding import PartitionSpec as P

D = 1024
HEADS = 16
HS = D // HEADS
GROUP = 2048
F32 = jnp.float32
BF16 = jnp.bfloat16
NEG = -1e30
SCALE = 1.0 / math.sqrt(HS)


def exchange(x, axis):
    return lax.all_to_all(x, axis, 0, 0, tiled=True)


def flip(x, axis, bit):
    n = lax.axis_size(axis)
    return lax.ppermute(x, axis, [(i, i ^ bit) for i in range(n)])


def nt(a, b):
    return lax.dot_general(a, b, (((1,), (1,)), ((), ())), preferred_element_type=F32)


def tn(a, b):
    return lax.dot_general(a, b, (((0,), (0,)), ((), ())), preferred_element_type=F32)


def nn(a, b):
    return jnp.dot(a, b, preferred_element_type=F32)


def pad16(n):
    return -(-n // 16) * 16


def log2(n):
    return n.bit_length() - 1


def split(value):
    hi = value.astype(BF16).astype(F32)
    return hi, value - hi


def put_pair(ref, row, lanes, value):
    ref[row : row + 1, :lanes], ref[row : row + 1, lanes : 2 * lanes] = split(value)


def put_rows(ref, block, row, lanes, value):
    ref[block, row : row + 1, :lanes], ref[block, row + 1 : row + 2, :lanes] = split(value)


def reversed_bits(x, bits):
    out = 0
    for b in range(bits):
        out = out | (((x >> b) & 1) << (bits - 1 - b))
    return out


def rows_kernel(length_ref, lead_ref, cot_ref, out_ref, sums_ref):
    rows = cot_ref.shape[0]
    row0 = lax.axis_index("patch") * rows
    sample = row0 // GROUP
    pos = row0 % GROUP + lax.broadcasted_iota(jnp.int32, cot_ref.shape, 0)
    kept = jnp.where(pos < length_ref[sample], cot_ref[...].astype(F32), 0.0)
    out_ref[...] = kept.astype(BF16)
    total = jnp.sum(kept, axis=0, keepdims=True)
    sums_ref[0:1, :] = total
    sums_ref[1:2, :] = total * (lead_ref[sample].astype(F32) / 100.0)


def pack_kernel(eb, v_ref, k_ref, wq_ref, q_ref, e_ref, b_ref, l_ref, *refs):
    outs, tmp_ref = refs[:-1], refs[-1]
    cw = outs[0].shape[1]
    rl = v_ref.shape[0]
    _, vl, dp = e_ref.shape
    spare = 5 * vl
    j = lax.axis_index("var")
    q = jnp.broadcast_to(q_ref[...].astype(BF16), (16, rl))
    tmp_ref[...] = jnp.zeros_like(tmp_ref)
    for p in range(5):
        tmp_ref[p * vl : (p + 1) * vl, :dp] = e_ref[p]
    own = lax.broadcasted_iota(jnp.int32, (1, dp), 1) // rl == j
    for i, ref in enumerate((b_ref, l_ref)):
        tiled = jnp.concatenate([ref[...]] * (dp // rl), axis=1)
        tmp_ref[spare + 2 + i : spare + 3 + i, :dp] = jnp.where(own, tiled, 0.0)
    for k, out_ref in enumerate(outs):
        cols = pl.ds(pl.multiple_of((j ^ k) * cw, 128), cw)
        hi, lo = split(nn(q, wq_ref[:, cols].astype(BF16))[0:1])
        tmp_ref[spare : spare + 1, :] = hi
        tmp_ref[spare + 1 : spare + 2, :] = lo
        tmp_ref[eb : eb + rl, :] = v_ref[:, cols]
        tmp_ref[eb + rl : eb + 2 * rl, :] = k_ref[:, cols]
        out_ref[...] = tmp_ref[...].astype(BF16)


def place(ref, at, j, size, parts, lanes):
    if size % 16 == 0:
        for k, part in enumerate(parts):
            ref[pl.ds(pl.multiple_of((j ^ k) * size, size), size), lanes] = part
        return
    for s in range(len(parts)):
        value = parts[0]
        for k in range(1, len(parts)):
            value = jnp.where(j ^ k == s, parts[k], value)
        ref[s * size : (s + 1) * size, lanes] = value


def product_kernel(eb, vl, rl, dp, *refs):
    n = len(refs) - 6
    got, (sums_ref, out_ref, e_ref, kb_ref, w_ref, p_ref) = refs[:n], refs[n:]
    cw = got[0].shape[1]
    spare = 5 * vl
    p_id = lax.axis_index("patch")
    j = lax.axis_index("var")
    live = lax.broadcasted_iota(jnp.int32, (eb, dp), 0) < spare
    small = jnp.zeros((4, cw), F32)
    vs = []
    ks = []
    for k in range(n):
        g = got[k][...].astype(F32)
        small = small + g[spare : spare + 4]
        vs.append(g[eb : eb + rl])
        ks.append(g[eb + rl : eb + 2 * rl])
        e_ref[pl.ds(pl.multiple_of((j ^ k) * eb, eb), eb), :] = jnp.where(live, g[:eb, :dp], 0.0).astype(BF16)
    place(w_ref, 0, j, rl, vs, slice(0, cw))
    place(w_ref, 0, j, rl, ks, slice(cw, 2 * cw))
    w = w_ref[...].astype(BF16)
    kb_ref[...] = w[:, cw:]
    p_ref[...] = nn(e_ref[...], w)
    put_pair(p_ref, spare, cw, small[0:1] + small[1:2])
    put_pair(p_ref, spare + 1, cw, sums_ref[0:1])
    put_pair(p_ref, spare + 2, cw, sums_ref[1:2])
    per = cw // dp
    here = (lax.broadcasted_iota(jnp.int32, (1, cw), 1) // dp == p_id % per) & (p_id // per == j)
    for i in range(2):
        tiled = jnp.concatenate([small[2 + i : 3 + i, :dp]] * per, axis=1)
        p_ref[spare + 3 : spare + 4, i * cw : (i + 1) * cw] = jnp.where(here, tiled, 0.0)
    out_ref[...] = p_ref[...].astype(BF16)


def sum_kernel(vl, got_ref, out_ref):
    n_p, rc, lanes = got_ref.shape
    cw = lanes // 2
    total = got_ref[0].astype(F32)
    for s in range(1, n_p):
        total = total + got_ref[s].astype(F32)
    row = lax.axis_index("patch") * rc + lax.broadcasted_iota(jnp.int32, (rc, cw), 0)
    paired = (row >= 5 * vl) & (row < 5 * vl + 3)
    a, b = total[:, :cw], total[:, cw:]
    hi, lo = split(a + b)
    a, b = jnp.where(paired, hi, a).astype(BF16), jnp.where(paired, lo, b).astype(BF16)
    for s in range(n_p):
        out_ref[s, :, :cw] = a
        out_ref[s, :, cw:] = b


def forward_kernel(tile, eb, vk_ref, x_ref, avail_ref, att_ref, prob_ref, ef_ref, vw_ref, s_ref, vs_ref):
    nv, rows = x_ref.shape[1:]
    heads = prob_ref.shape[0]
    cw = att_ref.shape[0]
    n_j = vk_ref.shape[0] // eb
    vl = nv // n_j
    spare = 5 * vl
    j = lax.axis_index("var")
    for s in range(n_j):
        s_ref[s] = vk_ref[s * eb : (s + 1) * eb, :].astype(F32)
    q = (s_ref[0, spare : spare + 1, :cw] + s_ref[0, spare : spare + 1, cw:]) * SCALE
    for k in range(n_j):
        for p in range(5):
            vs_ref[p * nv + k * vl : p * nv + (k + 1) * vl, :] = s_ref[j ^ k, p * vl : (p + 1) * vl, :]
    vw_ref[...] = vs_ref[:, :cw].astype(BF16)
    for p in range(5):
        kq = vs_ref[p * nv : (p + 1) * nv, cw:] * q
        ef_ref[p] = jnp.concatenate(
            [jnp.sum(kq[:, h * HS : (h + 1) * HS], axis=1, keepdims=True) for h in range(heads)], axis=1
        )
    sample = lax.axis_index("patch") * rows // GROUP
    row = lax.broadcasted_iota(jnp.int32, (nv, nv), 0)
    shift = jnp.zeros((nv, nv), jnp.int32)
    for k in range(n_j):
        shift = jnp.where((row >= k * vl) & (row < (k + 1) * vl), ((j ^ k) - k) * vl, shift)
    same = row + shift == lax.broadcasted_iota(jnp.int32, (nv, nv), 1)
    flags = jnp.broadcast_to(avail_ref[pl.ds(sample, 1), :], (nv, nv))
    present = jnp.sum(jnp.where(same, flags.astype(F32), 0.0), axis=1, keepdims=True) > 0.5
    vw = [vw_ref[:, h * HS : (h + 1) * HS] for h in range(heads)]

    def step(i, carry):
        cols = pl.ds(pl.multiple_of(i * tile, tile), tile)
        xs = [x_ref[p, :, cols].astype(F32) for p in range(4)]
        for h in range(heads):
            s = jnp.broadcast_to(ef_ref[4, :, h : h + 1], (nv, tile))
            for p in range(4):
                s = s + ef_ref[p, :, h : h + 1] * xs[p]
            s = jnp.where(present, s, NEG)
            w = jnp.where(present, jnp.exp(s - jnp.max(s, axis=0, keepdims=True)), 0.0)
            prob = w / jnp.sum(w, axis=0, keepdims=True)
            prob_ref[h, :, cols] = prob
            a = jnp.concatenate([(prob * x).astype(BF16) for x in xs] + [prob.astype(BF16)], axis=0)
            att_ref[h * HS : (h + 1) * HS, cols] = tn(vw[h], a).astype(BF16)
        return carry

    lax.fori_loop(0, rows // tile, step, 0)


def partial_kernel(keep, lo_ref, hi_ref, rows_ref, out_ref, w_ref):
    half, dp, cw = lo_ref.shape
    p_id = lax.axis_index("patch")
    j = lax.axis_index("var")
    low = j & 1 if keep else 1 - (j & 1)
    per = cw // dp
    for b in range(out_ref.shape[0]):
        dest = 2 * ((j >> 1) ^ b) + low
        for t in range(per):
            block = reversed_bits((dest * per + t) ^ p_id, log2(2 * half))
            at = slice((b * per + t) * dp, (b * per + t + 1) * dp)

            @pl.when(block < half)
            def _(at=at, block=block):
                w_ref[at, :] = lo_ref[block]

            @pl.when(block >= half)
            def _(at=at, block=block):
                w_ref[at, :] = hi_ref[block - half]

    for b in range(out_ref.shape[0]):
        out_ref[b] = nt(w_ref[b * cw : (b + 1) * cw, :], rows_ref[...]).astype(BF16)


def head_rows(half, lo_ref, hi_ref, w_ref):
    p_id = lax.axis_index("patch")
    for q in range(2 * half):
        block = reversed_bits(q ^ p_id, log2(2 * half))
        dp = lo_ref.shape[1]
        at = slice(q * dp, (q + 1) * dp)

        @pl.when(block < half)
        def _(at=at, block=block):
            w_ref[at, :] = lo_ref[block]

        @pl.when(block >= half)
        def _(at=at, block=block):
            w_ref[at, :] = hi_ref[block - half]


def first_kernel(n, lo_ref, hi_ref, rows_ref, *refs):
    atts, (acc_ref, gwo_ref, w_ref) = refs[:n], refs[n:]
    cw = rows_ref.shape[1]
    j = lax.axis_index("var")
    head_rows(lo_ref.shape[0], lo_ref, hi_ref, w_ref)
    for k in range(n):
        w = w_ref[pl.ds(pl.multiple_of((j ^ k) * cw, cw), cw), :]
        term = tn(atts[k][...], w)
        acc_ref[...] = term if k == 0 else acc_ref[...] + term
        gwo_ref[k] = nn(atts[k][...], rows_ref[...]).astype(BF16)


def second_kernel(vl, n0, n_j, length_ref, lead_ref, lo_ref, hi_ref, rows_ref, acc_ref, gwo0_ref, vk_ref, plo_ref, phi_ref, *refs):
    atts, (out_ref, gwo_ref, w_ref, pos_ref) = refs[: n_j - n0], refs[n_j - n0 :]
    rows, cw = rows_ref.shape
    spare = 5 * vl
    base = pad16(spare) - 16
    row0 = lax.axis_index("patch") * rows
    sample = row0 // GROUP
    me = lax.axis_index("patch") // (GROUP // rows)
    j = lax.axis_index("var")
    head_rows(lo_ref.shape[0], lo_ref, hi_ref, w_ref)
    for k in range(n0):
        gwo_ref[j ^ k] = gwo0_ref[k]
    for k in range(n0, n_j):
        gwo_ref[j ^ k] = nn(atts[k - n0][...], rows_ref[...]).astype(BF16)
    half, per, _ = plo_ref.shape
    pos_ref[:half] = plo_ref[...]
    pos_ref[half:] = phi_ref[...]
    bl = vk_ref[base : base + 32, :].astype(F32)[spare - base + 3 : spare - base + 4]
    add = bl[:, :cw] + lead_ref[sample].astype(F32) / 100.0 * bl[:, cw:]
    for b in range(2 * half):
        at = slice(b * per, (b + 1) * per)
        total = acc_ref[at, :] + add + pos_ref[reversed_bits(b ^ me, log2(2 * half))].astype(F32)
        for k in range(n0, n_j):
            w = w_ref[pl.ds(pl.multiple_of((j ^ k) * cw, cw), cw), :]
            total = total + tn(atts[k - n0][:, at], w)
        pos = row0 % GROUP + b * per + lax.broadcasted_iota(jnp.int32, (per, cw), 0)
        out_ref[at, :] = jnp.where(pos < length_ref[sample], total, 0.0).astype(BF16)


def backward_kernel(tile, eb, n_j, x_ref, ef_ref, vw_ref, prob_ref, *refs):
    grads = refs[: -(n_j + 4)]
    gx_refs = refs[-(n_j + 4) : -4]
    z_ref, gv_ref, acc_ref, s_ref = refs[-4:]
    nv, rows = x_ref.shape[1:]
    heads = prob_ref.shape[0]
    vl = nv // n_j
    cw = gv_ref.shape[1]
    j = lax.axis_index("var")
    gv_ref[...] = jnp.zeros_like(gv_ref)
    acc_ref[...] = jnp.zeros_like(acc_ref)

    def step(i, carry):
        cols = pl.ds(pl.multiple_of(i * tile, tile), tile)
        xs = [x_ref[p, :, cols].astype(F32) for p in range(4)]
        gx = [jnp.zeros((nv, tile), F32) for _ in range(4)]
        for h in range(heads):
            hc = slice(h * HS, (h + 1) * HS)
            prob = prob_ref[h, :, cols]
            gh = grads[0][hc, cols].astype(F32)
            for ref in grads[1:]:
                gh = gh + ref[hc, cols].astype(F32)
            gh = gh.astype(BF16)
            g = nn(vw_ref[:, hc], gh)
            gp = [g[p * nv : (p + 1) * nv] for p in range(5)]
            gprob = gp[4]
            for p in range(4):
                gprob = gprob + xs[p] * gp[p]
            inner = jnp.sum(prob * gprob, axis=0, keepdims=True)
            gs = prob * (gprob - inner)
            for p in range(4):
                gx[p] = gx[p] + prob * gp[p] + ef_ref[p, :, h : h + 1] * gs
            a = jnp.concatenate([(prob * x).astype(BF16) for x in xs] + [prob.astype(BF16)], axis=0)
            gv_ref[:, hc] += nt(a, gh)
            for p in range(5):
                t = gs if p == 4 else gs * xs[p]
                part = t[:, :128]
                for k in range(1, tile // 128):
                    part = part + t[:, k * 128 : (k + 1) * 128]
                acc_ref[p * heads + h] += part
        for p in range(4):
            for k in range(n_j):
                gx_refs[k][p, :, cols] = gx[p][k * vl : (k + 1) * vl].astype(BF16)
        return carry

    lax.fori_loop(0, rows // tile, step, 0)
    s_ref[...] = jnp.zeros_like(s_ref)
    for p in range(5):
        gs = jnp.concatenate(
            [jnp.sum(acc_ref[p * heads + h], axis=1, keepdims=True) for h in range(heads)], axis=1
        )
        hi, lo = split(gs)
        pair = jnp.concatenate([hi, lo, jnp.zeros((nv, 128 - 2 * heads), F32)], axis=1)
        for k in range(n_j):
            at = slice(p * nv + k * vl, p * nv + (k + 1) * vl)
            s_ref[j ^ k, p * vl : (p + 1) * vl, :cw] = gv_ref[at, :]
            s_ref[j ^ k, p * vl : (p + 1) * vl, cw:] = pair[k * vl : (k + 1) * vl]
    for s in range(n_j):
        z_ref[s * eb : (s + 1) * eb, :] = s_ref[s].astype(BF16)


def sum_z_kernel(heads, got_ref, out_ref):
    n_p, rc, lanes = got_ref.shape
    cw = lanes - 128
    total = got_ref[0].astype(F32)
    for s in range(1, n_p):
        total = total + got_ref[s].astype(F32)
    main = total[:, :cw].astype(BF16)
    hi, lo = split(total[:, cw : cw + heads] + total[:, cw + heads : cw + 2 * heads])
    pair = jnp.concatenate([hi, lo, jnp.zeros((rc, 128 - 2 * heads), F32)], axis=1).astype(BF16)
    for s in range(n_p):
        out_ref[s, :, :cw] = main
        out_ref[s, :, cw:] = pair


def middle_kernel(eb, vl, z_ref, vk_ref, kb_ref, out_ref, s_ref):
    n_j = z_ref.shape[0] // eb
    dp, cw = kb_ref.shape
    heads = cw // HS
    spare = 5 * vl
    base = pad16(spare) - 16
    small = vk_ref[base : base + 32, :].astype(F32)[spare - base : spare - base + 3]
    small = small[:, :cw] + small[:, cw:]
    gq = [jnp.zeros((1, HS), F32) for _ in range(heads)]
    live = lax.broadcasted_iota(jnp.int32, (eb, 1), 0) < spare
    for s in range(n_j):
        z = z_ref[s * eb : (s + 1) * eb, :].astype(F32)
        s_ref[s] = z
        ke = jnp.where(live, vk_ref[s * eb : (s + 1) * eb, cw:].astype(F32), 0.0)
        gs = z[:, cw : cw + heads] + z[:, cw + heads : cw + 2 * heads]
        for h in range(heads):
            gq[h] = gq[h] + jnp.sum(ke[:, h * HS : (h + 1) * HS] * gs[:, h : h + 1], axis=0, keepdims=True)
    put_rows(s_ref, 0, spare, cw, jnp.concatenate(gq, axis=1) * SCALE)
    put_rows(s_ref, 0, spare + 2, cw, small[0:1])
    put_rows(s_ref, 1, spare, cw, small[1:2])
    put_rows(s_ref, 1, spare + 2, cw, small[2:3])
    head = lax.broadcasted_iota(jnp.int32, (8, cw), 0) == lax.broadcasted_iota(jnp.int32, (8, cw), 1) // HS
    hi, lo = split(jnp.where(head, small[0:1] * SCALE, 0.0))
    fold = nt(hi.astype(BF16), kb_ref[...]) + nt(lo.astype(BF16), kb_ref[...])
    s_ref[2, spare : spare + heads, :dp] = fold[:heads]
    for s in range(n_j):
        out_ref[s * eb : (s + 1) * eb, :] = s_ref[s].astype(BF16)


def own_rows(ref, index, size):
    if size % 8 == 0:
        return ref[pl.ds(pl.multiple_of(index * size, size), size), :]
    out = ref[:size, :]
    for k in range(1, ref.shape[0] // size):
        out = jnp.where(index == k, ref[k * size : (k + 1) * size, :], out)
    return out


def final_kernel(eb, vl, n_j, z_ref, e_ref, wq_ref, q_ref, *refs):
    vs = refs[:n_j]
    gwv_ref, gwk_ref, gwq_ref, gq_ref, ge_ref, gb_ref, gl_ref, s_ref, f_ref, v_ref = refs[n_j:]
    cw = z_ref.shape[2] - 128
    heads = cw // HS
    dp = v_ref.shape[0]
    rl = dp // n_j
    spare = 5 * vl
    p_id = lax.axis_index("patch")
    j = lax.axis_index("var")
    place(v_ref, 0, j, rl, [ref[...].astype(F32) for ref in vs], slice(0, D))
    own = pl.ds(pl.multiple_of(j * eb, eb), eb)
    base = pad16(spare) - 16
    at = spare - base
    gqs = []
    ge = jnp.zeros((eb, dp), F32)
    gb = []
    gl = []
    for s in range(n_j):
        s_ref[...] = tn(e_ref[...], z_ref[s])
        cols = slice(s * cw, (s + 1) * cw)
        picked = own_rows(s_ref, j, rl)
        gwv_ref[:, cols] = picked[:, :cw]
        pair = picked[:, cw:]
        gfold = (pair[:, :heads] + pair[:, heads : 2 * heads]) * SCALE
        rows0 = z_ref[s, base : base + 32, :].astype(F32)
        rows1 = z_ref[s, eb + base : eb + base + 32, :].astype(F32)
        rows2 = z_ref[s, 2 * eb + base : 2 * eb + base + 32, :].astype(F32)
        gqs.append(rows0[at : at + 1, :cw] + rows0[at + 1 : at + 2, :cw])
        qv = rows0[at + 2 : at + 3, :cw] + rows0[at + 3 : at + 4, :cw]
        gb.append(rows1[at : at + 1, :cw] + rows1[at + 1 : at + 2, :cw])
        gl.append(rows1[at + 2 : at + 3, :cw] + rows1[at + 3 : at + 4, :cw])
        gwk_ref[:, cols] = jnp.concatenate(
            [gfold[:, h : h + 1] * qv[:, h * HS : (h + 1) * HS] for h in range(heads)], axis=1
        )
        zo = z_ref[s, own, :]
        ge = ge + nt(zo[:, :cw], v_ref[:, cols].astype(BF16))
        gs = zo[:, cw : cw + heads].astype(F32) + zo[:, cw + heads : cw + 2 * heads].astype(F32)
        for h in range(heads):
            ge = ge + gs[:, h : h + 1] * rows2[at + h : at + h + 1, :dp]
    f_ref[...] = ge
    for p in range(5):
        ge_ref[p] = f_ref[p * vl : (p + 1) * vl, :]
    gq = jnp.concatenate(gqs, axis=1)
    gwq_ref[...] = q_ref[...].astype(BF16).astype(F32) * gq
    hi, lo = split(gq)
    wq = wq_ref[...].astype(BF16)
    both = jnp.concatenate([jnp.broadcast_to(hi, (8, D)), jnp.broadcast_to(lo, (8, D))], axis=0).astype(BF16)
    two = nt(both, wq)
    gq_ref[...] = two[0:1] + two[8:9]
    at_out = p_id * n_j + j
    for rows, ref in ((gb, gb_ref), (gl, gl_ref)):
        acc = jnp.zeros((1, rl), F32)
        for s in range(n_j):
            for g in range(cw // rl):
                acc = acc + jnp.where(at_out == s * (cw // rl) + g, rows[s][:, g * rl : (g + 1) * rl], 0.0)
        ref[...] = acc


def call(kernel, name, out_shape, args, scratch=(), flops=1 << 20, nbytes=1 << 20, smem=0, after=()):
    n = len(args)
    specs = [pl.BlockSpec(memory_space=pltpu.SMEM)] * smem + [pl.BlockSpec(memory_space=pltpu.VMEM)] * (n - smem)
    specs += [pl.BlockSpec(memory_space=pl.ANY)] * len(after)

    def body(*refs):
        kernel(*refs[:n], *refs[n + len(after) :])

    return pl.pallas_call(
        body,
        out_shape=out_shape,
        in_specs=specs,
        scratch_shapes=list(scratch),
        name=name,
        cost_estimate=pl.CostEstimate(flops=flops, bytes_accessed=nbytes, transcendentals=0),
    )(*args, *after)


def shape(dims, kind=F32):
    return jax.ShapeDtypeStruct(dims, kind)


def shards(pixels, embed, query, w_query, w_key, w_value, w_out, b_out, pos_embed, w_lead, avail, lengths, lead_hours, cotangent):
    n_p = lax.axis_size("patch")
    n_j = lax.axis_size("var")
    p_id = lax.axis_index("patch")
    vl, _, rows = pixels.shape
    nv = vl * n_j
    cw = w_out.shape[1]
    hl = cw // HS
    dp = embed.shape[2]
    rl = w_value.shape[0]
    eb = pad16(5 * vl + 4)
    nr = n_j * eb
    ch = pad16(eb + 2 * rl)
    rc = nr // n_p
    others = range(1, n_j)

    pack = call(
        functools.partial(pack_kernel, eb),
        "pack",
        [shape((ch, cw), BF16)] * n_j,
        (w_value, w_key, w_query, query[None, :], embed.transpose(1, 0, 2), b_out[None, :], w_lead[None, :]),
        [pltpu.VMEM((ch, cw), F32)],
    )
    got = [pack[0]] + [flip(pack[k], "var", k) for k in others]

    grad_rows, sums = call(
        rows_kernel, "rows", (shape((rows, cw), BF16), shape((2, cw))), (lengths, lead_hours, cotangent), smem=2
    )
    pix = [pixels] + [flip(pixels, "var", k) for k in others]
    pix = jnp.concatenate(pix, axis=0).transpose(1, 0, 2)

    part, e_all, k_blk = call(
        functools.partial(product_kernel, eb, vl, rl, dp),
        "product",
        (shape((nr, 2 * cw), BF16), shape((nr, dp), BF16), shape((dp, cw), BF16)),
        (*got, sums),
        [pltpu.VMEM((dp, 2 * cw), F32), pltpu.VMEM((nr, 2 * cw), F32)],
    )
    got2 = exchange(part, "patch").reshape(n_p, rc, 2 * cw)
    copies = call(functools.partial(sum_kernel, vl), "sum", shape((n_p, rc, 2 * cw), BF16), (got2,))
    vk = exchange(copies.reshape(nr, 2 * cw), "patch")

    wo_lo = w_out.astype(BF16)[None]
    wo_hi = flip(wo_lo, "patch", n_p // 2)
    bit = n_p // 4
    while bit:
        wo_lo = jnp.concatenate([wo_lo, wo_hi], axis=0)
        wo_hi = flip(wo_lo, "patch", bit)
        bit //= 2

    half = shape((n_j // 2, cw, rows), BF16)
    wide = [pltpu.VMEM((n_j // 2 * cw, cw), BF16)]
    send = call(
        functools.partial(partial_kernel, False), "partial_send", half, (wo_lo, wo_hi, grad_rows), wide, 1 << 29, after=(copies,)
    )
    sent = flip(send, "var", 1)
    keep = call(
        functools.partial(partial_kernel, True), "partial_keep", half, (wo_lo, wo_hi, grad_rows), wide, 1 << 29, after=(send,)
    )
    grads = [keep, sent]
    bit = 2
    while bit < n_j:
        grads = [g.reshape(g.shape[0] // 2, 2, cw, rows) for g in grads]
        send = sum(g[:, 1].astype(F32) for g in grads).astype(BF16)
        grads = [g[:, 0] for g in grads] + [flip(send, "var", bit)]
        bit *= 2
    grads = [g.reshape(cw, rows) for g in grads]

    att, prob, ef, vw = call(
        functools.partial(forward_kernel, 256, eb),
        "attention_forward",
        (shape((cw, rows), BF16), shape((hl, nv, rows)), shape((5, nv, hl)), shape((5 * nv, cw), BF16)),
        (vk, pix, avail),
        [pltpu.VMEM((n_j, eb, 2 * cw), F32), pltpu.VMEM((5 * nv, 2 * cw), F32)],
        hl * nv * rows * 800,
        3 << 20,
    )

    *gx, z = call(
        functools.partial(backward_kernel, 256, eb, n_j),
        "attention_backward",
        [shape((4, vl, rows), BF16)] * n_j + [shape((nr, cw + 128), BF16)],
        (pix, ef, vw, prob, *grads),
        [pltpu.VMEM((5 * nv, cw), F32), pltpu.VMEM((5 * hl, nv, 128), F32), pltpu.VMEM((n_j, eb, cw + 128), F32)],
        hl * nv * rows * 1600,
        3 << 20,
    )

    gx = [gx[0]] + [flip(gx[k], "var", k) for k in others]
    grad_pixels = sum(g.astype(F32) for g in gx).astype(BF16).transpose(1, 0, 2)

    blocks = [att]
    bit = 1
    while bit < n_j:
        blocks = blocks + [flip(b, "var", bit) for b in blocks]
        bit *= 2
    n0 = max(n_j // 2, 1)
    acc, gwo0 = call(
        functools.partial(first_kernel, n0),
        "out_first",
        (shape((rows, cw)), shape((n0, cw, cw), BF16)),
        (wo_lo, wo_hi, grad_rows, *blocks[:n0]),
        [pltpu.VMEM((D, cw), BF16)],
        1 << 30,
        2 << 20,
        after=(z,),
    )

    parts = GROUP // rows
    owners = n_p // parts
    per = pos_embed.shape[0]
    there = [(k * owners + i, parts * i + k) for i in range(owners) for k in range(parts)]
    back = [(b, a) for a, b in there]
    me = p_id // parts
    pos_lo = lax.ppermute(pos_embed.astype(BF16), "patch", there)[None]
    pos_hi = flip(pos_lo, "patch", n_p // 2)
    bit = n_p // 4
    while bit >= parts:
        pos_lo = jnp.concatenate([pos_lo, pos_hi], axis=0)
        pos_hi = flip(pos_lo, "patch", bit)
        bit //= 2
    gpos = grad_rows.reshape(owners, per, cw)
    bit = 1
    while bit < owners:
        pair = gpos.reshape(gpos.shape[0] // 2, 2, per, cw)
        mine = (me // bit) % 2
        send = lax.dynamic_index_in_dim(pair, 1 - mine, 1, False)
        keep = lax.dynamic_index_in_dim(pair, mine, 1, False)
        gpos = (keep.astype(F32) + flip(send, "patch", bit * parts).astype(F32)).astype(BF16)
        bit *= 2
    grad_pos = lax.ppermute(gpos.reshape(per, cw), "patch", back).astype(F32)

    mixed, gwo = call(
        functools.partial(second_kernel, vl, n0, n_j),
        "out_second",
        (shape((rows, cw), BF16), shape((n_j, cw, cw), BF16)),
        (lengths, lead_hours, wo_lo, wo_hi, grad_rows, acc, gwo0, vk, pos_lo, pos_hi, *blocks[n0:]),
        [pltpu.VMEM((D, cw), BF16), pltpu.VMEM((owners, per, cw), BF16)],
        1 << 30,
        2 << 20,
        smem=2,
    )

    got3 = exchange(z, "patch").reshape(n_p, rc, cw + 128)
    copies = call(functools.partial(sum_z_kernel, hl), "sum_z", shape((n_p, rc, cw + 128), BF16), (got3,))
    z = exchange(copies.reshape(nr, cw + 128), "patch")
    z = call(
        functools.partial(middle_kernel, eb, vl),
        "middle",
        shape((nr, cw + 128), BF16),
        (z, vk, k_blk),
        [pltpu.VMEM((n_j, eb, cw + 128), F32)],
    )
    gwo, z = lax.optimization_barrier((gwo, z))
    gwo = exchange(gwo.reshape(D, cw), "patch").reshape(n_p, dp, cw)
    grad_w_out = jnp.sum(gwo.astype(F32), axis=0)
    allz = lax.all_gather(z, "var", axis=0, tiled=False)
    v_low = w_value.astype(BF16)
    v_rows = [v_low] + [flip(v_low, "var", k) for k in others]
    gwv, gwk, gwq, gq, ge, gb, gl = call(
        functools.partial(final_kernel, eb, vl, n_j),
        "final",
        (
            shape((rl, D)),
            shape((rl, D)),
            shape((rl, D)),
            shape((1, rl)),
            shape((5, vl, dp)),
            shape((1, rl)),
            shape((1, rl)),
        ),
        (allz, e_all, w_query, query[:, None], *v_rows),
        [pltpu.VMEM((dp, cw + 128), F32), pltpu.VMEM((eb, dp), F32), pltpu.VMEM((dp, D), F32)],
    )
    return (
        mixed,
        grad_pixels,
        ge.transpose(1, 0, 2),
        gq.reshape(rl),
        gwq,
        gwk,
        gwv,
        grad_w_out,
        gb.reshape(rl),
        grad_pos,
        gl.reshape(rl),
    )


def solution(mesh):
    both = P(("patch", "var"))
    rows2 = P(("patch", "var"), None)
    return jax.shard_map(
        shards,
        mesh=mesh,
        in_specs=(
            P("var", None, "patch"),
            P("var", None, "patch"),
            both,
            rows2,
            rows2,
            rows2,
            P("patch", "var"),
            both,
            P("patch", "var"),
            both,
            P(),
            P(),
            P(),
            P("patch", "var"),
        ),
        out_specs=(
            P("patch", "var"),
            P("var", None, "patch"),
            P("var", None, "patch"),
            both,
            rows2,
            rows2,
            rows2,
            P("patch", "var"),
            both,
            P("patch", "var"),
            both,
        ),
        check_vma=False,
    )
```

time: 258 us -> 147 us (0.57)
  the two profiles are of different devices: /device:TPU:0 before, /device:TPU:9 now
where the time goes in v2:
time: 147 us; the launch traced here: 146 us
  starting transfers between devices  60.7 us (41%)
  Pallas kernels  37.2 us (25%)
  waiting for transfers between devices  22.5 us (15%)
  local copies, waits for them, and re-layouts  10.4 us (7%)
  blocking collectives  9.15 us (6%)
  other arithmetic  4.85 us (3%)
    pallas_call x13, Pallas kernels, call(): pl.pallas_call(body, out_shape=out_shape, in_specs=specs, scratch_shapes=...  37.2 us
    ppermute x24, starting transfers between devices, flip(): return lax.ppermute(x, axis, [(i, i ^ bit) for i in range(n)])  32.5 us
    all_to_all x5, starting transfers between devices, exchange(): return lax.all_to_all(x, axis, 0, 0, tiled=True)  22.2 us
    ppermute x24, waiting for transfers between devices, flip(): return lax.ppermute(x, axis, [(i, i ^ bit) for i in range(n)])  12.6 us
    all_gather x1, blocking collectives, shards(): allz = lax.all_gather(z, 'var', axis=0, tiled=False)  9.15 us
    unnamed x60, local copies, waits for them, and re-layouts  8.06 us
    all_to_all x5, waiting for transfers between devices, exchange(): return lax.all_to_all(x, axis, 0, 0, tiled=True)  5.18 us
    ppermute x1, waiting for transfers between devices, shards(): grad_pos = lax.ppermute(gpos.reshape(per, cw), 'patch', back).astype(F32)  4.81 us
  transfers between devices with their start and end apart: 31, of which 6 were waited for; matrix products, arithmetic and copies ran while one was open for 4% of the time, Pallas kernels for 24%

profile of v2, /device:TPU:9, one launch (start us, length us, event | category | flops | bytes accessed | tf_op | source)
XLA Modules:
  0.0 145.9 jit_solution(9575697540200483301)
XLA Ops:
  1.6 2.4 %collective-permute-start = (bf16[1,128,256]{2,1,0:T(8,128)(2,1)S(1)}, bf16[1,128,256]{2,1,0:T(8,128)(2,1)S(1)}, u32[]{:S(2)}, u32[]{:S(2)}) collective-permute-start(bf16[1,128,256]{2,1,0:T(8,128)(2,1)S(1)} %convert_bitcast_fusion), channel_id=1, source_target_pairs={{0,16},{4,20},{8,24},{12,28},{16,0},{20,4},{24,8},{28,12},{1,17},{... | collective-permute-start | bytes 196616 | tf_op jit(solution)/shard_map/ppermute | solution.py:27
  15.1 3.7 %all-to-all-start = ((bf16[8,32,512]{2,1,0:T(8,128)(2,1)}), bf16[8,32,512]{2,1,0:T(8,128)(2,1)S(1)}, u32[]{:S(2)}, u32[]{:S(2)}) async-start(bf16[8,32,512]{2,1,0:T(8,128)(2,1)} %bitcast.53), calls=%async_computation | async-start | bytes 524288 | tf_op jit(solution)/shard_map/all_to_all | solution.py:22
  20.1 5.2 %all-to-all-done.refs_0_ = bf16[8,32,512]{2,1,0:T(8,128)(2,1)S(1)} async-done(((bf16[8,32,512]{2,1,0:T(8,128)(2,1)}), bf16[8,32,512]{2,1,0:T(8,128)(2,1)S(1)}, u32[]{:S(2)}, u32[]{:S(2)}) %all-to-all-start) | async-done | bytes 262176 | tf_op jit(solution)/shard_map/all_to_all | solution.py:22
  29.3 2.7 %partial_send.1.refs_3_ = bf16[2,256,1024]{2,1,0:T(8,128)(2,1)} custom-call(bf16[4,128,256]{2,1,0:T(8,128)(2,1)} %copy-done.2, bf16[4,128,256]{2,1,0:T(8,128)(2,1)} %copy-done.4, bf16[1024,256]{1,0:T(8,128)(2,1)} %get-tuple-element.42.refs_2_.refs_4_, bf16[8,32,512]{2,1,0:T(8,128)(2,1)} %sum.1.refs_3_), custom_call_target="tpu_custom_call" | custom-call | flops 536870912 | bytes 1048576 | tf_op jit(solution)/shard_map/partial_send/pallas_call | solution.py:477
  36.2 2.8 %collective-permute-start.12 = (bf16[256,256]{1,0:T(8,128)(2,1)S(1)}, bf16[256,256]{1,0:T(8,128)(2,1)S(1)}, u32[]{:S(2)}, u32[]{:S(2)}) collective-permute-start(bf16[256,256]{1,0:T(8,128)(2,1)S(1)} %convert_element_type.96), channel_id=1, source_target_pairs={{0,0},{16,4},{4,8},{20,12},{8,16},{24,20},{12,24},{28,28},{1,1},{1... | collective-permute-start | bytes 393224 | tf_op jit(solution)/shard_map/ppermute | solution.py:605
  39.1 4.6 %all-to-all-start.1 = ((bf16[8,32,512]{2,1,0:T(8,128)(2,1)}), bf16[8,32,512]{2,1,0:T(8,128)(2,1)S(1)}, u32[]{:S(2)}, u32[]{:S(2)}) async-start(bf16[8,32,512]{2,1,0:T(8,128)(2,1)} %sum.1.refs_3_), calls=%async_computation.1 | async-start | bytes 524288 | tf_op jit(solution)/shard_map/all_to_all | solution.py:22
  43.6 2.7 %partial_keep.1 = bf16[2,256,1024]{2,1,0:T(8,128)(2,1)} custom-call(bf16[4,128,256]{2,1,0:T(8,128)(2,1)} %copy-done.2, bf16[4,128,256]{2,1,0:T(8,128)(2,1)} %copy-done.4, bf16[1024,256]{1,0:T(8,128)(2,1)} %get-tuple-element.42.refs_2_.refs_4_, bf16[2,256,1024]{2,1,0:T(8,128)(2,1)} %partial_send.1.refs_3_), custom_call_target="tpu_custom_call" | custom-call | flops 536870912 | bytes 1048576 | tf_op jit(solution)/shard_map/partial_keep/pallas_call | solution.py:477
  51.4 4.8 %attention_forward.1 = (bf16[256,1024]{1,0:T(8,128)(2,1)}, f32[4,48,1024]{2,1,0:T(8,128)}, f32[5,48,4]{2,1,0:T(8,128)}, bf16[240,256]{1,0:T(8,128)(2,1)}) custom-call(bf16[256,512]{1,0:T(8,128)(2,1)} %bitcast.45, bf16[4,48,1024]{2,1,0:T(8,128)(2,1)} %maximum_bitcast_fusion.refs_1_.refs_0_, s32[4,48]{1,0:T(4,128)} %refs_2_.6), custom_call_target="tpu_custom_call" | custom-call | flops 157286400 | bytes 3145728 | tf_op jit(solution)/shard_map/attention_forward/pallas_call | solution.py:477
  61.3 5.4 %attention_backward.1 = (bf16[4,12,1024]{2,1,0:T(8,128)(2,1)}, bf16[4,12,1024]{2,1,0:T(8,128)(2,1)}, bf16[4,12,1024]{2,1,0:T(8,128)(2,1)}, bf16[4,12,1024]{2,1,0:T(8,128)(2,1)}, bf16[256,384]{1,0:T(8,128)(2,1)}) custom-call(bf16[4,48,1024]{2,1,0:T(8,128)(2,1)} %maximum_bitcast_fusion.refs_1_.refs_0_, f32[5,48,4]{2,1,0:T(8,128)} %get-tuple-element.50.refs_1_, ...), custom_call_target="tpu_custom_call" | custom-call | flops 314572800 | bytes 3145728 | tf_op jit(solution)/shard_map/attention_backward/pallas_call | solution.py:477
  66.7 5.5 %all-to-all-start.2 = ((bf16[8,32,384]{2,1,0:T(8,128)(2,1)}), bf16[8,32,384]{2,1,0:T(8,128)(2,1)S(1)}, u32[]{:S(2)}, u32[]{:S(2)}) async-start(bf16[8,32,384]{2,1,0:T(8,128)(2,1)} %bitcast.54), calls=%async_computation.2 | async-start | bytes 393216 | tf_op jit(solution)/shard_map/all_to_all | solution.py:22
  72.3 2.3 %collective-permute-start.13 = (bf16[1,256,256]{2,1,0:T(8,128)(2,1)S(1)}, bf16[1,256,256]{2,1,0:T(8,128)(2,1)S(1)}, u32[]{:S(2)}, u32[]{:S(2)}) collective-permute-start(bf16[1,256,256]{2,1,0:T(8,128)(2,1)S(1)} %bitcast.55), channel_id=1, source_target_pairs={{0,16},{4,20},{8,24},{12,28},{16,0},{20,4},{24,8},{28,12},{1,17},{... | collective-permute-start | bytes 393224 | tf_op jit(solution)/shard_map/ppermute | solution.py:27
  76.1 8.5 %collective-permute-done.13 = bf16[1,256,256]{2,1,0:T(8,128)(2,1)S(1)} collective-permute-done((bf16[1,256,256]{2,1,0:T(8,128)(2,1)S(1)}, bf16[1,256,256]{2,1,0:T(8,128)(2,1)S(1)}, u32[]{:S(2)}, u32[]{:S(2)}) %collective-permute-start.13) | collective-permute-done | bytes 131104 | tf_op jit(solution)/shard_map/ppermute | solution.py:27
  87.2 4.7 %all-to-all-start.3 = ((bf16[8,32,384]{2,1,0:T(8,128)(2,1)}), bf16[8,32,384]{2,1,0:T(8,128)(2,1)S(1)}, u32[]{:S(2)}, u32[]{:S(2)}) async-start(bf16[8,32,384]{2,1,0:T(8,128)(2,1)} %sum_z.1), calls=%async_computation.3 | async-start | bytes 393216 | tf_op jit(solution)/shard_map/all_to_all | solution.py:22
  92.0 2.2 %collective-permute-start.24 = (bf16[1,256,256]{2,1,0:T(8,128)(2,1)S(1)}, bf16[1,256,256]{2,1,0:T(8,128)(2,1)S(1)}, u32[]{:S(2)}, u32[]{:S(2)}) collective-permute-start(bf16[1,256,256]{2,1,0:T(8,128)(2,1)S(1)} %constant_dynamic-slice_fusion), channel_id=1, source_target_pairs={{0,16},{4,20},{8,24},{12,28},{16,0},{20,4},{24,8},{28,12},{1,17},{... | collective-permute-start | bytes 393224 | tf_op jit(solution)/shard_map/ppermute | solution.py:27
  94.2 3.4 %out_first.1 = (f32[1024,256]{1,0:T(8,128)}, bf16[2,256,256]{2,1,0:T(8,128)(2,1)}) custom-call(bf16[4,128,256]{2,1,0:T(8,128)(2,1)} %copy-done.2, bf16[4,128,256]{2,1,0:T(8,128)(2,1)} %copy-done.4, bf16[1024,256]{1,0:T(8,128)(2,1)} %get-tuple-element.42.refs_2_.refs_4_, bf16[256,1024]{1,0:T(8,128)(2,1)} %get-tuple-element.49.refs_3_, ...), custom_call_target="tpu_custom_call" | custom-call | flops 1073741824 | bytes 2097152 | tf_op jit(solution)/shard_map/out_first/pallas_call | solution.py:477
  98.7 3.9 %out_second.1 = (bf16[1024,256]{1,0:T(8,128)(2,1)}, bf16[4,256,256]{2,1,0:T(8,128)(2,1)}) custom-call(s32[4]{0:T(128)} %refs_0_.5, s32[4]{0:T(128)} %refs_1_.5, bf16[4,128,256]{2,1,0:T(8,128)(2,1)} %copy-done.2, bf16[4,128,256]{2,1,0:T(8,128)(2,1)} %copy-done.4, bf16[1024,256]{1,0:T(8,128)(2,1)} %get-tuple-element.42.refs_2_.refs_4_, ...), custom_call_target="tpu_custom_call" | custom-call | flops 1073741824 | bytes 2097152 | tf_op jit(solution)/shard_map/out_second/pallas_call | solution.py:477
  103.3 2.2 %middle.1 = bf16[256,384]{1,0:T(8,128)(2,1)} custom-call(bf16[256,384]{1,0:T(8,128)(2,1)} %bitcast.51, bf16[256,512]{1,0:T(8,128)(2,1)} %bitcast.47, bf16[128,256]{1,0:T(8,128)(2,1)} %get-tuple-element.62.refs_2_), custom_call_target="tpu_custom_call" | custom-call | flops 1048576 | bytes 1048576 | tf_op jit(solution)/shard_map/middle/pallas_call | solution.py:477
  105.5 3.8 %all-to-all-start.4 = ((bf16[8,128,256]{2,1,0:T(8,128)(2,1)}), bf16[8,128,256]{2,1,0:T(8,128)(2,1)S(1)}, u32[]{:S(2)}, u32[]{:S(2)}) async-start(bf16[8,128,256]{2,1,0:T(8,128)(2,1)} %bitcast.22), calls=%async_computation.4 | async-start | bytes 1048576 | tf_op jit(solution)/shard_map/all_to_all | solution.py:22
  109.3 3.2 %collective-permute-start.25 = (bf16[256,256]{1,0:T(8,128)(2,1)S(1)}, bf16[256,256]{1,0:T(8,128)(2,1)S(1)}, u32[]{:S(2)}, u32[]{:S(2)}) collective-permute-start(bf16[256,256]{1,0:T(8,128)(2,1)S(1)} %fusion.3), channel_id=1, source_target_pairs={{0,0},{4,16},{8,4},{12,20},{16,8},{20,24},{24,12},{28,28},{1,1},{5... | collective-permute-start | bytes 393224 | tf_op jit(solution)/shard_map/ppermute | solution.py:621
  112.6 5.5 %collective-permute-start.17 = (bf16[4,12,1024]{2,1,0:T(8,128)(2,1)S(1)}, bf16[4,12,1024]{2,1,0:T(8,128)(2,1)S(1)}, u32[]{:S(2)}, u32[]{:S(2)}) collective-permute-start(bf16[4,12,1024]{2,1,0:T(8,128)(2,1)S(1)} %copy-done.28), channel_id=1, source_target_pairs={{0,1},{1,0},{2,3},{3,2},{4,5},{5,4},{6,7},{7,6},{8,9},{9,8},{10,11... | collective-permute-start | bytes 294920 | tf_op jit(solution)/shard_map/ppermute | solution.py:27
  121.2 4.8 %collective-permute-done.25 = bf16[256,256]{1,0:T(8,128)(2,1)S(1)} collective-permute-done((bf16[256,256]{1,0:T(8,128)(2,1)S(1)}, bf16[256,256]{1,0:T(8,128)(2,1)S(1)}, u32[]{:S(2)}, u32[]{:S(2)}) %collective-permute-start.25) | collective-permute-done | bytes 131104 | tf_op jit(solution)/shard_map/ppermute | solution.py:621
  128.1 3.4 %collective-permute-start.22 = (bf16[32,1024]{1,0:T(8,128)(2,1)S(1)}, bf16[32,1024]{1,0:T(8,128)(2,1)S(1)}, u32[]{:S(2)}, u32[]{:S(2)}) collective-permute-start(bf16[32,1024]{1,0:T(8,128)(2,1)S(1)} %convert_element_type.102.refs_4_), channel_id=1, source_target_pairs={{0,3},{1,2},{2,1},{3,0},{4,7},{5,6},{6,5},{7,4},{8,11},{9,10},{10,... | collective-permute-start | bytes 196616 | tf_op jit(solution)/shard_map/ppermute | solution.py:27
  132.6 9.2 %all-gather = bf16[1024,384]{1,0:T(8,128)(2,1)} all-gather(bf16[256,384]{1,0:T(8,128)(2,1)S(1)} %copy-done.9), channel_id=2, replica_groups=mesh['patch'=8,'var'=4] {'var'}, dimensions={0}, use_global_device_ids=true | all-gather | bytes 983040 | tf_op jit(solution)/shard_map/all_gather | solution.py:647
  142.4 2.8 %final.1 = (f32[32,1024]{1,0:T(8,128)}, f32[32,1024]{1,0:T(8,128)}, f32[32,1024]{1,0:T(8,128)}, f32[1,32]{1,0:T(1,128)}, f32[5,12,128]{2,1,0:T(8,128)}, /*index=5*/f32[1,32]{1,0:T(1,128)}, f32[1,32]{1,0:T(1,128)}) custom-call(bf16[4,256,384]{2,1,0:T(8,128)(2,1)} %bitcast.48, bf16[256,128]{1,0:T(8,128)(2,1)} %get-tuple-element.64.refs_1_, ...), custom_call_target="tpu_custom_call" | custom-call | flops 1048576 | bytes 1048576 | tf_op jit(solution)/shard_map/final/pallas_call | solution.py:477
  (130 shorter events, 45.3 us)
Async XLA Ops:
  32.0 14.3 %collective-permute-start.10 = (bf16[2,256,1024]{2,1,0:T(8,128)(2,1)}, bf16[2,256,1024]{2,1,0:T(8,128)(2,1)S(1)}, u32[]{:S(2)}, u32[]{:S(2)}) collective-permute-start(bf16[2,256,1024]{2,1,0:T(8,128)(2,1)} %partial_send.1.refs_3_), channel_id=1, source_target_pairs={{0,1},{1,0},{2,3},{3,2},{4,5},{5,4},{6,7},{7,6},{8,9},{9,8},{10,11... | collective-permute-start | bytes 3145736 | tf_op jit(solution)/shard_map/ppermute | solution.py:27
  34.0 14.9 %collective-permute-start.6 = (bf16[12,4,1024]{2,0,1:T(8,128)(2,1)S(1)}, bf16[12,4,1024]{2,0,1:T(8,128)(2,1)S(1)}, u32[]{:S(2)}, u32[]{:S(2)}) collective-permute-start(bf16[12,4,1024]{2,0,1:T(8,128)(2,1)S(1)} %copy.28), channel_id=1, source_target_pairs={{0,1},{1,0},{2,3},{3,2},{4,5},{5,4},{6,7},{7,6},{8,9},{9,8},{10,11... | collective-permute-start | bytes 294920 | tf_op jit(solution)/shard_map/ppermute | solution.py:27
  34.1 14.9 %collective-permute-start.7 = (bf16[12,4,1024]{2,0,1:T(8,128)(2,1)S(1)}, bf16[12,4,1024]{2,0,1:T(8,128)(2,1)S(1)}, u32[]{:S(2)}, u32[]{:S(2)}) collective-permute-start(bf16[12,4,1024]{2,0,1:T(8,128)(2,1)S(1)} %copy.28), channel_id=1, source_target_pairs={{0,2},{1,3},{2,0},{3,1},{4,6},{5,7},{6,4},{7,5},{8,10},{9,11},{10,... | collective-permute-start | bytes 294920 | tf_op jit(solution)/shard_map/ppermute | solution.py:27
  35.3 13.6 %collective-permute-start.8 = (bf16[12,4,1024]{2,0,1:T(8,128)(2,1)S(1)}, bf16[12,4,1024]{2,0,1:T(8,128)(2,1)S(1)}, u32[]{:S(2)}, u32[]{:S(2)}) collective-permute-start(bf16[12,4,1024]{2,0,1:T(8,128)(2,1)S(1)} %copy.28), channel_id=1, source_target_pairs={{0,3},{1,2},{2,1},{3,0},{4,7},{5,6},{6,5},{7,4},{8,11},{9,10},{10,... | collective-permute-start | bytes 294920 | tf_op jit(solution)/shard_map/ppermute | solution.py:27
  36.2 36.0 %collective-permute-start.12 = (bf16[256,256]{1,0:T(8,128)(2,1)S(1)}, bf16[256,256]{1,0:T(8,128)(2,1)S(1)}, u32[]{:S(2)}, u32[]{:S(2)}) collective-permute-start(bf16[256,256]{1,0:T(8,128)(2,1)S(1)} %convert_element_type.96), channel_id=1, source_target_pairs={{0,0},{16,4},{4,8},{20,12},{8,16},{24,20},{12,24},{28,28},{1,1},{1... | collective-permute-start | bytes 393224 | tf_op jit(solution)/shard_map/ppermute | solution.py:605
  39.1 11.6 %all-to-all-start.1 = ((bf16[8,32,512]{2,1,0:T(8,128)(2,1)}), bf16[8,32,512]{2,1,0:T(8,128)(2,1)S(1)}, u32[]{:S(2)}, u32[]{:S(2)}) async-start(bf16[8,32,512]{2,1,0:T(8,128)(2,1)} %sum.1.refs_3_), calls=%async_computation.1 | async-start | bytes 524288 | tf_op jit(solution)/shard_map/all_to_all | solution.py:22
  47.7 12.8 %collective-permute-start.11 = (bf16[1,256,1024]{2,1,0:T(8,128)(2,1)S(1)}, bf16[1,256,1024]{2,1,0:T(8,128)(2,1)S(1)}, u32[]{:S(2)}, u32[]{:S(2)}) collective-permute-start(bf16[1,256,1024]{2,1,0:T(8,128)(2,1)S(1)} %fusion), channel_id=1, source_target_pairs={{0,2},{1,3},{2,0},{3,1},{4,6},{5,7},{6,4},{7,5},{8,10},{9,11},{10,... | collective-permute-start | bytes 1572872 | tf_op jit(solution)/shard_map/ppermute | solution.py:27
  56.1 19.8 %collective-permute-start.9 = (bf16[256,1024]{1,0:T(8,128)(2,1)}, bf16[256,1024]{1,0:T(8,128)(2,1)}, u32[]{:S(2)}, u32[]{:S(2)}) collective-permute-start(bf16[256,1024]{1,0:T(8,128)(2,1)} %get-tuple-element.49.refs_3_), channel_id=1, source_target_pairs={{0,1},{1,0},{2,3},{3,2},{4,5},{5,4},{6,7},{7,6},{8,9},{9,8},{10,11... | collective-permute-start | bytes 1572872 | tf_op jit(solution)/shard_map/ppermute | solution.py:27
  66.7 18.0 %all-to-all-start.2 = ((bf16[8,32,384]{2,1,0:T(8,128)(2,1)}), bf16[8,32,384]{2,1,0:T(8,128)(2,1)S(1)}, u32[]{:S(2)}, u32[]{:S(2)}) async-start(bf16[8,32,384]{2,1,0:T(8,128)(2,1)} %bitcast.54), calls=%async_computation.2 | async-start | bytes 393216 | tf_op jit(solution)/shard_map/all_to_all | solution.py:22
  72.2 19.7 %collective-permute-start.23 = (bf16[2,256,256]{2,1,0:T(8,128)(2,1)S(1)}, bf16[2,256,256]{2,1,0:T(8,128)(2,1)S(1)}, u32[]{:S(2)}, u32[]{:S(2)}) collective-permute-start(bf16[2,256,256]{2,1,0:T(8,128)(2,1)S(1)} %dynamic-slice_bitcast_fusion), channel_id=1, source_target_pairs={{0,8},{4,12},{8,0},{12,4},{16,24},{20,28},{24,16},{28,20},{1,9},{5... | collective-permute-start | bytes 786440 | tf_op jit(solution)/shard_map/ppermute | solution.py:27
  72.3 12.3 %collective-permute-start.13 = (bf16[1,256,256]{2,1,0:T(8,128)(2,1)S(1)}, bf16[1,256,256]{2,1,0:T(8,128)(2,1)S(1)}, u32[]{:S(2)}, u32[]{:S(2)}) collective-permute-start(bf16[1,256,256]{2,1,0:T(8,128)(2,1)S(1)} %bitcast.55), channel_id=1, source_target_pairs={{0,16},{4,20},{8,24},{12,28},{16,0},{20,4},{24,8},{28,12},{1,17},{... | collective-permute-start | bytes 393224 | tf_op jit(solution)/shard_map/ppermute | solution.py:27
  74.6 23.0 %collective-permute-start.15 = (bf16[256,1024]{1,0:T(8,128)(2,1)}, bf16[256,1024]{1,0:T(8,128)(2,1)S(1)}, u32[]{:S(2)}, u32[]{:S(2)}) collective-permute-start(bf16[256,1024]{1,0:T(8,128)(2,1)} %get-tuple-element.49.refs_3_), channel_id=1, source_target_pairs={{0,2},{1,3},{2,0},{3,1},{4,6},{5,7},{6,4},{7,5},{8,10},{9,11},{10,... | collective-permute-start | bytes 1572872 | tf_op jit(solution)/shard_map/ppermute | solution.py:27
  75.9 21.7 %collective-permute-start.16 = (bf16[256,1024]{1,0:T(8,128)(2,1)}, bf16[256,1024]{1,0:T(8,128)(2,1)S(1)}, u32[]{:S(2)}, u32[]{:S(2)}) collective-permute-start(bf16[256,1024]{1,0:T(8,128)(2,1)} %collective-permute-done.9.refs_4_), channel_id=1, source_target_pairs={{0,2},{1,3},{2,0},{3,1},{4,6},{5,7},{6,4},{7,5},{8,10},{9,11},{10,... | collective-permute-start | bytes 1572872 | tf_op jit(solution)/shard_map/ppermute | solution.py:27
  84.6 13.0 %collective-permute-start.14 = (bf16[2,256,256]{2,1,0:T(8,128)(2,1)S(1)}, bf16[2,256,256]{2,1,0:T(8,128)(2,1)S(1)}, u32[]{:S(2)}, u32[]{:S(2)}) collective-permute-start(bf16[2,256,256]{2,1,0:T(8,128)(2,1)S(1)} %pad_maximum_fusion.1.refs_8_), channel_id=1, source_target_pairs={{0,8},{4,12},{8,0},{12,4},{16,24},{20,28},{24,16},{28,20},{1,9},{5... | collective-permute-start | bytes 786440 | tf_op jit(solution)/shard_map/ppermute | solution.py:27
  87.2 15.4 %all-to-all-start.3 = ((bf16[8,32,384]{2,1,0:T(8,128)(2,1)}), bf16[8,32,384]{2,1,0:T(8,128)(2,1)S(1)}, u32[]{:S(2)}, u32[]{:S(2)}) async-start(bf16[8,32,384]{2,1,0:T(8,128)(2,1)} %sum_z.1), calls=%async_computation.3 | async-start | bytes 393216 | tf_op jit(solution)/shard_map/all_to_all | solution.py:22
  92.0 17.3 %collective-permute-start.24 = (bf16[1,256,256]{2,1,0:T(8,128)(2,1)S(1)}, bf16[1,256,256]{2,1,0:T(8,128)(2,1)S(1)}, u32[]{:S(2)}, u32[]{:S(2)}) collective-permute-start(bf16[1,256,256]{2,1,0:T(8,128)(2,1)S(1)} %constant_dynamic-slice_fusion), channel_id=1, source_target_pairs={{0,16},{4,20},{8,24},{12,28},{16,0},{20,4},{24,8},{28,12},{1,17},{... | collective-permute-start | bytes 393224 | tf_op jit(solution)/shard_map/ppermute | solution.py:27
  105.5 39.7 %all-to-all-start.4 = ((bf16[8,128,256]{2,1,0:T(8,128)(2,1)}), bf16[8,128,256]{2,1,0:T(8,128)(2,1)S(1)}, u32[]{:S(2)}, u32[]{:S(2)}) async-start(bf16[8,128,256]{2,1,0:T(8,128)(2,1)} %bitcast.22), calls=%async_computation.4 | async-start | bytes 1048576 | tf_op jit(solution)/shard_map/all_to_all | solution.py:22
  109.3 16.7 %collective-permute-start.25 = (bf16[256,256]{1,0:T(8,128)(2,1)S(1)}, bf16[256,256]{1,0:T(8,128)(2,1)S(1)}, u32[]{:S(2)}, u32[]{:S(2)}) collective-permute-start(bf16[256,256]{1,0:T(8,128)(2,1)S(1)} %fusion.3), channel_id=1, source_target_pairs={{0,0},{4,16},{8,4},{12,20},{16,8},{20,24},{24,12},{28,28},{1,1},{5... | collective-permute-start | bytes 393224 | tf_op jit(solution)/shard_map/ppermute | solution.py:621
  112.6 15.5 %collective-permute-start.17 = (bf16[4,12,1024]{2,1,0:T(8,128)(2,1)S(1)}, bf16[4,12,1024]{2,1,0:T(8,128)(2,1)S(1)}, u32[]{:S(2)}, u32[]{:S(2)}) collective-permute-start(bf16[4,12,1024]{2,1,0:T(8,128)(2,1)S(1)} %copy-done.28), channel_id=1, source_target_pairs={{0,1},{1,0},{2,3},{3,2},{4,5},{5,4},{6,7},{7,6},{8,9},{9,8},{10,11... | collective-permute-start | bytes 294920 | tf_op jit(solution)/shard_map/ppermute | solution.py:27
  118.1 13.5 %collective-permute-start.18 = (bf16[4,12,1024]{2,1,0:T(8,128)(2,1)S(1)}, bf16[4,12,1024]{2,1,0:T(8,128)(2,1)S(1)}, u32[]{:S(2)}, u32[]{:S(2)}) collective-permute-start(bf16[4,12,1024]{2,1,0:T(8,128)(2,1)S(1)} %copy-done.27), channel_id=1, source_target_pairs={{0,2},{1,3},{2,0},{3,1},{4,6},{5,7},{6,4},{7,5},{8,10},{9,11},{10,... | collective-permute-start | bytes 294920 | tf_op jit(solution)/shard_map/ppermute | solution.py:27
  119.3 12.3 %collective-permute-start.19 = (bf16[4,12,1024]{2,1,0:T(8,128)(2,1)S(1)}, bf16[4,12,1024]{2,1,0:T(8,128)(2,1)S(1)}, u32[]{:S(2)}, u32[]{:S(2)}) collective-permute-start(bf16[4,12,1024]{2,1,0:T(8,128)(2,1)S(1)} %copy-done.26), channel_id=1, source_target_pairs={{0,3},{1,2},{2,1},{3,0},{4,7},{5,6},{6,5},{7,4},{8,11},{9,10},{10,... | collective-permute-start | bytes 294920 | tf_op jit(solution)/shard_map/ppermute | solution.py:27
  119.8 21.9 %collective-permute-start.20 = (bf16[32,1024]{1,0:T(8,128)(2,1)S(1)}, bf16[32,1024]{1,0:T(8,128)(2,1)S(1)}, u32[]{:S(2)}, u32[]{:S(2)}) collective-permute-start(bf16[32,1024]{1,0:T(8,128)(2,1)S(1)} %convert_element_type.102.refs_4_), channel_id=1, source_target_pairs={{0,1},{1,0},{2,3},{3,2},{4,5},{5,4},{6,7},{7,6},{8,9},{9,8},{10,11... | collective-permute-start | bytes 196616 | tf_op jit(solution)/shard_map/ppermute | solution.py:27
  126.0 15.7 %collective-permute-start.21 = (bf16[32,1024]{1,0:T(8,128)(2,1)S(1)}, bf16[32,1024]{1,0:T(8,128)(2,1)S(1)}, u32[]{:S(2)}, u32[]{:S(2)}) collective-permute-start(bf16[32,1024]{1,0:T(8,128)(2,1)S(1)} %convert_element_type.102.refs_4_), channel_id=1, source_target_pairs={{0,2},{1,3},{2,0},{3,1},{4,6},{5,7},{6,4},{7,5},{8,10},{9,11},{10,... | collective-permute-start | bytes 196616 | tf_op jit(solution)/shard_map/ppermute | solution.py:27
  128.1 13.6 %collective-permute-start.22 = (bf16[32,1024]{1,0:T(8,128)(2,1)S(1)}, bf16[32,1024]{1,0:T(8,128)(2,1)S(1)}, u32[]{:S(2)}, u32[]{:S(2)}) collective-permute-start(bf16[32,1024]{1,0:T(8,128)(2,1)S(1)} %convert_element_type.102.refs_4_), channel_id=1, source_target_pairs={{0,3},{1,2},{2,1},{3,0},{4,7},{5,6},{6,5},{7,4},{8,11},{9,10},{10,... | collective-permute-start | bytes 196616 | tf_op jit(solution)/shard_map/ppermute | solution.py:27
  (36 other events, 158.6 us)

commit v3 on v2

v3 whole, which is shorter than its diff:
```python
import functools
import math

import jax
import jax.numpy as jnp
from jax import lax
from jax.experimental import pallas as pl
from jax.experimental.pallas import tpu as pltpu
from jax.sharding import PartitionSpec as P

D = 1024
HEADS = 16
HS = D // HEADS
GROUP = 2048
F32 = jnp.float32
BF16 = jnp.bfloat16
NEG = -1e30
SCALE = 1.0 / math.sqrt(HS)


def exchange(x, axis):
    return lax.all_to_all(x, axis, 0, 0, tiled=True)


def flip(x, axis, bit):
    n = lax.axis_size(axis)
    return lax.ppermute(x, axis, [(i, i ^ bit) for i in range(n)])


def gate(x, after):
    return lax.optimization_barrier((x, after))[0]


def gather_var(x, last):
    n = lax.axis_size("var")
    blocks = {0: x}
    bit = n // 2
    while bit:
        for k, block in list(blocks.items()):
            blocks[k | bit] = flip(last(block) if bit == 1 and k else block, "var", bit)
        bit //= 2
    return [blocks[k] for k in range(n)]


def halve(x, bit, step):
    pair = x.reshape(x.shape[0] // 2, 2, *x.shape[1:])
    send = lax.dynamic_index_in_dim(pair, 1 - bit, 1, False)
    keep = lax.dynamic_index_in_dim(pair, bit, 1, False)
    return (keep.astype(F32) + flip(send, "patch", step).astype(F32)).astype(BF16)


def nt(a, b):
    return lax.dot_general(a, b, (((1,), (1,)), ((), ())), preferred_element_type=F32)


def tn(a, b):
    return lax.dot_general(a, b, (((0,), (0,)), ((), ())), preferred_element_type=F32)


def nn(a, b):
    return jnp.dot(a, b, preferred_element_type=F32)


def pad16(n):
    return -(-n // 16) * 16


def split(value):
    hi = value.astype(BF16).astype(F32)
    return hi, value - hi


def put_pair(ref, row, lanes, value):
    ref[row : row + 1, :lanes], ref[row : row + 1, lanes : 2 * lanes] = split(value)


def put_rows(ref, block, row, lanes, value):
    ref[block, row : row + 1, :lanes], ref[block, row + 1 : row + 2, :lanes] = split(value)


def rows_kernel(length_ref, lead_ref, cot_ref, pix_ref, out_ref, sums_ref, tmp_ref):
    rows, cw = cot_ref.shape
    vl = pix_ref.shape[0]
    vp = tmp_ref.shape[0] // 4
    row0 = lax.axis_index("patch") * rows
    sample = row0 // GROUP
    pos = row0 % GROUP + lax.broadcasted_iota(jnp.int32, cot_ref.shape, 0)
    kept = jnp.where(pos < length_ref[sample], cot_ref[...].astype(F32), 0.0)
    out_ref[:rows] = kept.astype(BF16)
    total = jnp.sum(kept, axis=0, keepdims=True)
    sums_ref[0:1, :] = total
    sums_ref[1:2, :] = total * (lead_ref[sample].astype(F32) / 100.0)
    tmp_ref[...] = jnp.zeros_like(tmp_ref)
    for v in range(vl):
        x = pix_ref[v].astype(F32)
        for p in range(4):
            tmp_ref[p * vp + v : p * vp + v + 1, :] = x[p : p + 1]
    for b in range(rows // cw):
        out_ref[rows + b * 4 * vp : rows + (b + 1) * 4 * vp, :] = tmp_ref[:, b * cw : (b + 1) * cw].astype(BF16)


def pack_kernel(eb, v_ref, k_ref, wq_ref, q_ref, e_ref, b_ref, l_ref, *refs):
    outs, tmp_ref = refs[:-1], refs[-1]
    cw = outs[0].shape[1]
    rl = v_ref.shape[0]
    _, vl, dp = e_ref.shape
    spare = 5 * vl
    j = lax.axis_index("var")
    q = jnp.broadcast_to(q_ref[...].astype(BF16), (16, rl))
    tmp_ref[...] = jnp.zeros_like(tmp_ref)
    for p in range(5):
        tmp_ref[p * vl : (p + 1) * vl, :dp] = e_ref[p]
    own = lax.broadcasted_iota(jnp.int32, (1, dp), 1) // rl == j
    for i, ref in enumerate((b_ref, l_ref)):
        tiled = jnp.concatenate([ref[...]] * (dp // rl), axis=1)
        tmp_ref[spare + 2 + i : spare + 3 + i, :dp] = jnp.where(own, tiled, 0.0)
    for k, out_ref in enumerate(outs):
        cols = pl.ds(pl.multiple_of((j ^ k) * cw, 128), cw)
        hi, lo = split(nn(q, wq_ref[:, cols].astype(BF16))[0:1])
        tmp_ref[spare : spare + 1, :] = hi
        tmp_ref[spare + 1 : spare + 2, :] = lo
        tmp_ref[eb : eb + rl, :] = k_ref[:, cols]
        for m in range(len(outs)):
            at = eb + (m + 1) * rl
            tmp_ref[at : at + rl, :] = v_ref[:, pl.ds(pl.multiple_of((j ^ k ^ m) * cw, 128), cw)]
        out_ref[...] = tmp_ref[...].astype(BF16)


def place(ref, at, j, size, parts, lanes):
    if size % 16 == 0:
        for k, part in enumerate(parts):
            ref[pl.ds(pl.multiple_of((j ^ k) * size, size), size), lanes] = part
        return
    for s in range(len(parts)):
        value = parts[0]
        for k in range(1, len(parts)):
            value = jnp.where(j ^ k == s, parts[k], value)
        ref[s * size : (s + 1) * size, lanes] = value


def product_kernel(eb, vl, rl, dp, *refs):
    n = len(refs) - 7
    got, (sums_ref, out_ref, e_ref, kb_ref, vb_ref, w_ref, p_ref) = refs[:n], refs[n:]
    cw = got[0].shape[1]
    spare = 5 * vl
    p_id = lax.axis_index("patch")
    j = lax.axis_index("var")
    live = lax.broadcasted_iota(jnp.int32, (eb, dp), 0) < spare
    small = jnp.zeros((4, cw), F32)
    gs = [got[k][...].astype(F32) for k in range(n)]
    for k in range(n):
        small = small + gs[k][spare : spare + 4]
        e_ref[pl.ds(pl.multiple_of((j ^ k) * eb, eb), eb), :] = jnp.where(live, gs[k][:eb, :dp], 0.0).astype(BF16)
    for m in range(n + 1):
        at = eb + m * rl
        place(w_ref, 0, j, rl, [g[at : at + rl] for g in gs], slice(m * cw, (m + 1) * cw))
    vb_ref[...] = w_ref[:, cw:].astype(BF16)
    w = jnp.concatenate([vb_ref[:, :cw], w_ref[:, :cw].astype(BF16)], axis=1)
    kb_ref[...] = w[:, cw:]
    p_ref[...] = nn(e_ref[...], w)
    put_pair(p_ref, spare, cw, small[0:1] + small[1:2])
    put_pair(p_ref, spare + 1, cw, sums_ref[0:1])
    put_pair(p_ref, spare + 2, cw, sums_ref[1:2])
    per = cw // dp
    here = (lax.broadcasted_iota(jnp.int32, (1, cw), 1) // dp == p_id % per) & (p_id // per == j)
    for i in range(2):
        tiled = jnp.concatenate([small[2 + i : 3 + i, :dp]] * per, axis=1)
        p_ref[spare + 3 : spare + 4, i * cw : (i + 1) * cw] = jnp.where(here, tiled, 0.0)
    out_ref[...] = p_ref[...].astype(BF16)


def sum_kernel(vl, got_ref, out_ref):
    n_p, rc, lanes = got_ref.shape
    cw = lanes // 2
    total = got_ref[0].astype(F32)
    for s in range(1, n_p):
        total = total + got_ref[s].astype(F32)
    row = lax.axis_index("patch") * rc + lax.broadcasted_iota(jnp.int32, (rc, cw), 0)
    paired = (row >= 5 * vl) & (row < 5 * vl + 3)
    a, b = total[:, :cw], total[:, cw:]
    hi, lo = split(a + b)
    a, b = jnp.where(paired, hi, a).astype(BF16), jnp.where(paired, lo, b).astype(BF16)
    for s in range(n_p):
        out_ref[s, :, :cw] = a
        out_ref[s, :, cw:] = b


def forward_kernel(tile, eb, vk_ref, x_ref, avail_ref, att_ref, prob_ref, ef_ref, vw_ref, s_ref, vs_ref):
    nv, rows = x_ref.shape[1:]
    heads = prob_ref.shape[0]
    cw = att_ref.shape[0]
    n_j = vk_ref.shape[0] // eb
    vl = nv // n_j
    spare = 5 * vl
    j = lax.axis_index("var")
    for s in range(n_j):
        s_ref[s] = vk_ref[s * eb : (s + 1) * eb, :].astype(F32)
    q = (s_ref[0, spare : spare + 1, :cw] + s_ref[0, spare : spare + 1, cw:]) * SCALE
    for k in range(n_j):
        for p in range(5):
            vs_ref[p * nv + k * vl : p * nv + (k + 1) * vl, :] = s_ref[j ^ k, p * vl : (p + 1) * vl, :]
    vw_ref[...] = vs_ref[:, :cw].astype(BF16)
    for p in range(5):
        kq = vs_ref[p * nv : (p + 1) * nv, cw:] * q
        ef_ref[p] = jnp.concatenate(
            [jnp.sum(kq[:, h * HS : (h + 1) * HS], axis=1, keepdims=True) for h in range(heads)], axis=1
        )
    sample = lax.axis_index("patch") * rows // GROUP
    row = lax.broadcasted_iota(jnp.int32, (nv, nv), 0)
    shift = jnp.zeros((nv, nv), jnp.int32)
    for k in range(n_j):
        shift = jnp.where((row >= k * vl) & (row < (k + 1) * vl), ((j ^ k) - k) * vl, shift)
    same = row + shift == lax.broadcasted_iota(jnp.int32, (nv, nv), 1)
    flags = jnp.broadcast_to(avail_ref[pl.ds(sample, 1), :], (nv, nv))
    present = jnp.sum(jnp.where(same, flags.astype(F32), 0.0), axis=1, keepdims=True) > 0.5
    vw = [vw_ref[:, h * HS : (h + 1) * HS] for h in range(heads)]

    def step(i, carry):
        cols = pl.ds(pl.multiple_of(i * tile, tile), tile)
        xs = [x_ref[p, :, cols].astype(F32) for p in range(4)]
        for h in range(heads):
            s = jnp.broadcast_to(ef_ref[4, :, h : h + 1], (nv, tile))
            for p in range(4):
                s = s + ef_ref[p, :, h : h + 1] * xs[p]
            s = jnp.where(present, s, NEG)
            w = jnp.where(present, jnp.exp(s - jnp.max(s, axis=0, keepdims=True)), 0.0)
            prob = w / jnp.sum(w, axis=0, keepdims=True)
            prob_ref[h, :, cols] = prob
            a = jnp.concatenate([(prob * x).astype(BF16) for x in xs] + [prob.astype(BF16)], axis=0)
            att_ref[h * HS : (h + 1) * HS, cols] = tn(vw[h], a).astype(BF16)
        return carry

    lax.fori_loop(0, rows // tile, step, 0)


def reversed_bits(x, bits):
    out = 0
    for b in range(bits):
        out = out | (((x >> b) & 1) << (bits - 1 - b))
    return out


def pixel_kernel(vl, cw, *refs):
    bufs, (out_ref, x_ref) = refs[:-2], refs[-2:]
    rows = out_ref.shape[2]
    vp = (bufs[0].shape[0] - rows) // (4 * (rows // cw))
    for k, buf in enumerate(bufs):
        for b in range(rows // cw):
            at = rows + b * 4 * vp
            x = buf[at : at + 4 * vp, :].astype(F32)
            for p in range(4):
                x_ref[p, k * vl : (k + 1) * vl, b * cw : (b + 1) * cw] = x[p * vp : p * vp + vl]
    for p in range(4):
        out_ref[p] = x_ref[p].astype(BF16)


def weight_kernel(n_j, vl, lo_ref, hi_ref, *refs):
    bufs, (full_ref, *chunks), (pix_ref, x_ref) = refs[:n_j], refs[n_j : 2 * n_j], refs[2 * n_j :]
    pixel_kernel(vl, full_ref.shape[1], *bufs, pix_ref, x_ref)
    half, dp, cw = lo_ref.shape
    p_id = lax.axis_index("patch")
    j = lax.axis_index("var")
    for q in range(2 * half):
        block = reversed_bits(q ^ p_id, (2 * half).bit_length() - 1)
        at = slice(q * dp, (q + 1) * dp)

        @pl.when(block < half)
        def _(at=at, block=block):
            full_ref[at, :] = lo_ref[block]

        @pl.when(block >= half)
        def _(at=at, block=block):
            full_ref[at, :] = hi_ref[block - half]

    for k, ref in enumerate(chunks):
        ref[...] = full_ref[pl.ds(pl.multiple_of((j ^ (k + 1)) * cw, cw), cw), :]


def grad_kernel(n_j, full_ref, *refs):
    ws, cots, (out_ref,) = refs[: n_j - 1], refs[n_j - 1 : -1], refs[-1:]
    cw, rows = out_ref.shape
    j = lax.axis_index("var")
    own = full_ref[pl.ds(pl.multiple_of(j * cw, cw), cw), :]
    tile = 256
    for i in range(rows // tile):
        at = slice(i * tile, (i + 1) * tile)
        total = nt(own, cots[0][at, :])
        for k in range(1, n_j):
            total = total + nt(ws[k - 1][...], cots[k][at, :])
        out_ref[:, at] = total.astype(BF16)


def weight_grad_kernel(n_j, buf_ref, *refs):
    atts, (send_ref, keep_ref, tmp_ref) = refs[:n_j], refs[n_j:]
    cw, rows = atts[0].shape
    half, dp, _ = send_ref.shape
    j = lax.axis_index("var")
    per = cw // dp
    for k in range(n_j):
        g = nn(atts[k][...], buf_ref[:rows, :]).astype(BF16)
        for t in range(per):
            tmp_ref[(j ^ k) * per + t] = g[t * dp : (t + 1) * dp]
    own = lax.axis_index("patch") & 1
    for b in range(half):
        send_ref[b] = tmp_ref[2 * b + 1 - own]
        keep_ref[b] = tmp_ref[2 * b + own]


def halve_kernel(bit, keep_ref, got_ref, send_ref, next_ref):
    own = jnp.where(lax.axis_index("patch") & bit, 1, 0)
    for b in range(send_ref.shape[0]):
        for ref, i in ((send_ref, 1 - own), (next_ref, own)):
            ref[b] = (keep_ref[2 * b + i].astype(F32) + got_ref[2 * b + i].astype(F32)).astype(BF16)


def mixed_kernel(vl, n_j, length_ref, lead_ref, w_ref, vk_ref, plo_ref, phi_ref, *refs):
    atts, (out_ref, pos_ref) = refs[:n_j], refs[n_j:]
    rows, cw = out_ref.shape
    spare = 5 * vl
    base = pad16(spare) - 16
    row0 = lax.axis_index("patch") * rows
    sample = row0 // GROUP
    me = lax.axis_index("patch") // (GROUP // rows)
    j = lax.axis_index("var")
    half, per, _ = plo_ref.shape
    pos_ref[:half] = plo_ref[...]
    pos_ref[half:] = phi_ref[...]
    bl = vk_ref[base : base + 32, :].astype(F32)[spare - base + 3 : spare - base + 4]
    add = bl[:, :cw] + lead_ref[sample].astype(F32) / 100.0 * bl[:, cw:]
    for b in range(2 * half):
        at = slice(b * per, (b + 1) * per)
        total = add + pos_ref[reversed_bits(b ^ me, (2 * half).bit_length() - 1)].astype(F32)
        for k in range(n_j):
            w = w_ref[pl.ds(pl.multiple_of((j ^ k) * cw, cw), cw), :]
            total = total + tn(atts[k][:, at], w)
        pos = row0 % GROUP + b * per + lax.broadcasted_iota(jnp.int32, (per, cw), 0)
        out_ref[at, :] = jnp.where(pos < length_ref[sample], total, 0.0).astype(BF16)


def backward_kernel(tile, eb, n_j, vp, x_ref, ef_ref, vw_ref, prob_ref, grad_ref, *refs):
    outs, (z_ref, gv_ref, acc_ref, s_ref) = refs[:-4], refs[-4:]
    nv, rows = x_ref.shape[1:]
    heads = prob_ref.shape[0]
    vl = nv // n_j
    cw = gv_ref.shape[1]
    j = lax.axis_index("var")
    gv_ref[...] = jnp.zeros_like(gv_ref)
    acc_ref[...] = jnp.zeros_like(acc_ref)
    blank = jnp.zeros((vp - vl, tile), F32)

    def step(i, carry):
        cols = pl.ds(pl.multiple_of(i * tile, tile), tile)
        xs = [x_ref[p, :, cols].astype(F32) for p in range(4)]
        gx = [jnp.zeros((nv, tile), F32) for _ in range(4)]
        for h in range(heads):
            hc = slice(h * HS, (h + 1) * HS)
            prob = prob_ref[h, :, cols]
            gh = grad_ref[hc, cols]
            g = nn(vw_ref[:, hc], gh)
            gp = [g[p * nv : (p + 1) * nv] for p in range(5)]
            gprob = gp[4]
            for p in range(4):
                gprob = gprob + xs[p] * gp[p]
            inner = jnp.sum(prob * gprob, axis=0, keepdims=True)
            gs = prob * (gprob - inner)
            for p in range(4):
                gx[p] = gx[p] + prob * gp[p] + ef_ref[p, :, h : h + 1] * gs
            a = jnp.concatenate([(prob * x).astype(BF16) for x in xs] + [prob.astype(BF16)], axis=0)
            gv_ref[:, hc] += nt(a, gh)
            for p in range(5):
                t = gs if p == 4 else gs * xs[p]
                part = t[:, :128]
                for k in range(1, tile // 128):
                    part = part + t[:, k * 128 : (k + 1) * 128]
                acc_ref[p * heads + h] += part
        for k, ref in enumerate(outs):
            piece = jnp.concatenate([t for p in range(4) for t in (gx[p][k * vl : (k + 1) * vl], blank)], axis=0)
            ref[:, cols] = piece.astype(BF16)
        return carry

    lax.fori_loop(0, rows // tile, step, 0)
    s_ref[...] = jnp.zeros_like(s_ref)
    for p in range(5):
        gs = jnp.concatenate(
            [jnp.sum(acc_ref[p * heads + h], axis=1, keepdims=True) for h in range(heads)], axis=1
        )
        hi, lo = split(gs)
        pair = jnp.concatenate([hi, lo, jnp.zeros((nv, 128 - 2 * heads), F32)], axis=1)
        for k in range(n_j):
            at = slice(p * nv + k * vl, p * nv + (k + 1) * vl)
            s_ref[j ^ k, p * vl : (p + 1) * vl, :cw] = gv_ref[at, :]
            s_ref[j ^ k, p * vl : (p + 1) * vl, cw:] = pair[k * vl : (k + 1) * vl]
    for s in range(n_j):
        z_ref[s * eb : (s + 1) * eb, :] = s_ref[s].astype(BF16)


def sum_z_kernel(heads, got_ref, out_ref):
    n_p, rc, lanes = got_ref.shape
    cw = lanes - 128
    total = got_ref[0].astype(F32)
    for s in range(1, n_p):
        total = total + got_ref[s].astype(F32)
    main = total[:, :cw].astype(BF16)
    hi, lo = split(total[:, cw : cw + heads] + total[:, cw + heads : cw + 2 * heads])
    pair = jnp.concatenate([hi, lo, jnp.zeros((rc, 128 - 2 * heads), F32)], axis=1).astype(BF16)
    for s in range(n_p):
        out_ref[s, :, :cw] = main
        out_ref[s, :, cw:] = pair


def middle_kernel(eb, vl, n_j, z_ref, vk_ref, kb_ref, e_ref, v_ref, *refs):
    chunks, (g_ref, ge_ref, s_ref) = refs[:n_j], refs[n_j:]
    dp, cw = kb_ref.shape
    rl = dp // n_j
    heads = cw // HS
    spare = 5 * vl
    half = eb // 2
    j = lax.axis_index("var")
    base = pad16(spare) - 16
    small = vk_ref[base : base + 32, :].astype(F32)[spare - base : spare - base + 3]
    small = small[:, :cw] + small[:, cw:]
    qvec = small[0:1] * SCALE
    g = tn(e_ref[...], z_ref[...])
    gfold = g[:, cw : cw + heads] + g[:, cw + heads : cw + 2 * heads]
    g_ref[:, :cw] = g[:, :cw]
    g_ref[:, cw:] = jnp.concatenate(
        [gfold[:, h : h + 1] * qvec[:, h * HS : (h + 1) * HS] for h in range(heads)], axis=1
    )
    pair = z_ref[:, cw:].astype(F32)
    gs = pair[:, :heads] + pair[:, heads : 2 * heads]
    live = lax.broadcasted_iota(jnp.int32, (n_j * eb, 1), 0) % eb < spare
    ke = jnp.where(live, vk_ref[:, cw:].astype(F32), 0.0)
    gq = jnp.concatenate(
        [jnp.sum(ke[:, h * HS : (h + 1) * HS] * gs[:, h : h + 1], axis=0, keepdims=True) for h in range(heads)], axis=1
    ) * SCALE
    head = lax.broadcasted_iota(jnp.int32, (8, cw), 0) == lax.broadcasted_iota(jnp.int32, (8, cw), 1) // HS
    hi, lo = split(jnp.where(head, qvec, 0.0))
    fold = nt(hi.astype(BF16), kb_ref[...]) + nt(lo.astype(BF16), kb_ref[...])
    ge = nt(z_ref[:, :cw], v_ref[:, :cw])
    for h in range(heads):
        ge = ge + gs[:, h : h + 1] * fold[h : h + 1, :]
    ge_ref[...] = ge
    s_ref[...] = jnp.zeros_like(s_ref)
    at = 2 * rl + half
    for i, row in enumerate((gq, small[1:2], small[2:3])):
        s_ref[at + 2 * i : at + 2 * i + 1, :], s_ref[at + 2 * i + 1 : at + 2 * i + 2, :] = split(row)
    for k in range(n_j):
        rows = own_rows(g_ref, j ^ k, rl)
        s_ref[:rl, :] = rows[:, :cw]
        s_ref[rl : 2 * rl, :] = rows[:, cw:]
        block = ge_ref[pl.ds(pl.multiple_of((j ^ k) * eb, eb), eb), :]
        s_ref[2 * rl : 2 * rl + half, :dp] = block[:half]
        s_ref[2 * rl : 2 * rl + half, cw // 2 : cw // 2 + dp] = block[half:]
        chunks[k][...] = s_ref[...].astype(BF16)


def own_rows(ref, index, size):
    if size % 8 == 0:
        return ref[pl.ds(pl.multiple_of(index * size, size), size), :]
    out = ref[:size, :]
    for k in range(1, ref.shape[0] // size):
        out = jnp.where(index == k, ref[k * size : (k + 1) * size, :], out)
    return out


def final_kernel(eb, vl, rl, dp, n_j, wq_ref, q_ref, *refs):
    chunks, (gwv_ref, gwk_ref, gwq_ref, gq_ref, ge_ref, gb_ref, gl_ref, f_ref, r_ref) = refs[:n_j], refs[n_j:]
    cw = chunks[0].shape[1]
    half = eb // 2
    j = lax.axis_index("var")
    at_out = lax.axis_index("patch") * n_j + j
    at = 2 * rl + half
    ge = jnp.zeros((half, cw), F32)
    gb = jnp.zeros((1, rl), F32)
    gl = jnp.zeros((1, rl), F32)
    for k in range(n_j):
        c = chunks[k][...].astype(F32)
        cols = pl.ds(pl.multiple_of((j ^ k) * cw, 128), cw)
        gwv_ref[:, cols] = c[:rl]
        gwk_ref[:, cols] = c[rl : 2 * rl]
        ge = ge + c[2 * rl : at]
        r_ref[0:1, cols] = c[at : at + 1] + c[at + 1 : at + 2]
        bias = c[at + 2 : at + 3] + c[at + 3 : at + 4]
        lead = c[at + 4 : at + 5] + c[at + 5 : at + 6]
        for g in range(cw // rl):
            here = at_out == (j ^ k) * (cw // rl) + g
            gb = gb + jnp.where(here, bias[:, g * rl : (g + 1) * rl], 0.0)
            gl = gl + jnp.where(here, lead[:, g * rl : (g + 1) * rl], 0.0)
    f_ref[:half, :] = ge[:, :dp]
    f_ref[half:, :] = ge[:, cw // 2 : cw // 2 + dp]
    for p in range(5):
        ge_ref[p] = f_ref[p * vl : (p + 1) * vl, :]
    gq = r_ref[0:1, :]
    gwq_ref[...] = q_ref[...].astype(BF16).astype(F32) * gq
    hi, lo = split(gq)
    wq = wq_ref[...].astype(BF16)
    both = jnp.concatenate([jnp.broadcast_to(hi, (8, D)), jnp.broadcast_to(lo, (8, D))], axis=0).astype(BF16)
    two = nt(both, wq)
    gq_ref[...] = two[0:1] + two[8:9]
    gb_ref[...] = gb
    gl_ref[...] = gl


def call(kernel, name, out_shape, args, scratch=(), us=1.0, smem=0, after=(), first=False, spill=(), hbm=0):
    n = len(args)
    in_vmem = pl.BlockSpec(memory_space=pltpu.VMEM)
    specs = [pl.BlockSpec(memory_space=pltpu.SMEM)] * smem + [pl.BlockSpec() if first else in_vmem] * (n - smem)
    specs[n - hbm :] = [pl.BlockSpec(memory_space=pl.ANY)] * hbm
    specs += [pl.BlockSpec(memory_space=pl.ANY)] * len(after)
    shapes = list(out_shape) if isinstance(out_shape, (list, tuple)) else [out_shape]
    outs = [pl.BlockSpec(memory_space=pltpu.HBM) if i in spill else in_vmem for i in range(len(shapes))]
    extra = [pltpu.VMEM(shapes[i].shape, shapes[i].dtype) for i in spill]
    if spill:
        extra.append(pltpu.SemaphoreType.DMA((len(spill),)))

    def body(*refs):
        ins, rest = refs[:n], refs[n + len(after) :]
        results, rest = list(rest[: len(shapes)]), rest[len(shapes) :]
        local, sems = rest[: len(spill)], rest[len(extra) - 1 : len(extra)]
        rest = rest[len(extra) :]
        copies = []
        for c, i in enumerate(spill):
            copies.append(pltpu.make_async_copy(local[c], results[i], sems[0].at[c]))
            results[i] = local[c]
        kernel(*ins, *results, *rest)
        for copy in copies:
            copy.start()
        for copy in copies:
            copy.wait()

    result = pl.pallas_call(
        body,
        out_shape=shapes,
        in_specs=specs,
        out_specs=outs,
        scratch_shapes=[*extra, *scratch],
        name=name,
        compiler_params=None if first else pltpu.CompilerParams(vmem_limit_bytes=12 << 20),
        cost_estimate=pl.CostEstimate(flops=int(us * 1.153e9), bytes_accessed=1 << 16, transcendentals=0),
    )(*args, *after)
    return result if isinstance(out_shape, (list, tuple)) else result[0]


def shape(dims, kind=F32):
    return jax.ShapeDtypeStruct(dims, kind)


def shards(pixels, embed, query, w_query, w_key, w_value, w_out, b_out, pos_embed, w_lead, avail, lengths, lead_hours, cotangent):
    n_p = lax.axis_size("patch")
    n_j = lax.axis_size("var")
    p_id = lax.axis_index("patch")
    vl, _, rows = pixels.shape
    nv = vl * n_j
    cw = w_out.shape[1]
    hl = cw // HS
    dp = embed.shape[2]
    rl = w_value.shape[0]
    eb = pad16(5 * vl + 4)
    nr = n_j * eb
    ch = pad16(eb + (n_j + 1) * rl)
    vp = -(-vl // 8) * 8
    rc = nr // n_p
    others = range(1, n_j)

    pack = call(
        functools.partial(pack_kernel, eb),
        "pack",
        [shape((ch, cw), BF16)] * n_j,
        (w_value, w_key, w_query, query[None, :], embed.transpose(1, 0, 2), b_out[None, :], w_lead[None, :]),
        [pltpu.VMEM((ch, cw), F32)],
        first=True,
    )
    got = [pack[0]] + [flip(pack[k], "var", k) for k in others]

    buf, sums = call(
        rows_kernel,
        "rows",
        (shape((rows + 4 * vp * (rows // cw), cw), BF16), shape((2, cw))),
        (lengths, lead_hours, cotangent, pixels),
        [pltpu.VMEM((4 * vp, rows), F32)],
        smem=2,
        after=(pack[0],),
    )

    wo_lo = gate(w_out, pack[0]).astype(BF16)[None]
    bit = n_p // 2
    wo_hi = flip(wo_lo, "patch", bit)
    wo_steps = [wo_hi]
    while bit > 1:
        bit //= 2
        wo_lo = jnp.concatenate([gate(wo_lo, got[-1]), wo_hi], axis=0)
        wo_hi = flip(wo_lo, "patch", bit)
        wo_steps.append(wo_hi)

    part, e_all, k_blk, v_blk = call(
        functools.partial(product_kernel, eb, vl, rl, dp),
        "product",
        (shape((nr, 2 * cw), BF16), shape((nr, dp), BF16), shape((dp, cw), BF16), shape((dp, D), BF16)),
        (*got, sums),
        [pltpu.VMEM((dp, (n_j + 1) * cw), F32), pltpu.VMEM((nr, 2 * cw), F32)],
        us=1.0,
        spill=(1, 2, 3),
    )
    got2 = exchange(gate(part, wo_steps[-2]), "patch").reshape(n_p, rc, 2 * cw)
    copies = call(functools.partial(sum_kernel, vl), "sum", shape((n_p, rc, 2 * cw), BF16), (got2,), after=(wo_hi,))
    vk = exchange(copies.reshape(nr, 2 * cw), "patch")

    bufs = gather_var(gate(buf, part), lambda x: gate(x, copies))

    wo, *chunks, pix = call(
        functools.partial(weight_kernel, n_j, vl),
        "weight",
        [shape((D, cw), BF16)] + [shape((cw, cw), BF16)] * (n_j - 1) + [shape((4, nv, rows), BF16)],
        (wo_lo, wo_hi, *bufs),
        [pltpu.VMEM((4, nv, rows), F32)],
        after=(copies,),
    )
    chunks = [flip(c, "var", k + 1) for k, c in enumerate(chunks)]
    grad_att = call(
        functools.partial(grad_kernel, n_j), "grad_att", shape((cw, rows), BF16), (wo, *chunks, *bufs)
    )

    parts = GROUP // rows
    owners = n_p // parts
    per = pos_embed.shape[0]
    me = p_id // parts
    there = [(k * owners + i, parts * i + k) for i in range(owners) for k in range(parts)]
    back = [(b, a) for a, b in there]
    pos_lo = lax.ppermute(gate(pos_embed, wo).astype(BF16), "patch", there)[None]
    gpos = gate(buf, wo)[:rows].reshape(owners, per, cw)
    gpos = halve(gpos, me % 2, parts)

    att, prob, ef, vw = call(
        functools.partial(forward_kernel, 256, eb),
        "attention_forward",
        (
            shape((cw, rows), BF16),
            shape((hl, nv, rows)),
            shape((5, nv, hl)),
            shape((5 * nv, cw), BF16),
        ),
        (vk, pix, avail),
        [pltpu.VMEM((n_j, eb, 2 * cw), F32), pltpu.VMEM((5 * nv, 2 * cw), F32)],
        after=(*chunks, gpos),
    )

    *gx, z = call(
        functools.partial(backward_kernel, 256, eb, n_j, vp),
        "attention_backward",
        [shape((4 * vp, rows), BF16)] * n_j + [shape((nr, cw + 128), BF16)],
        (pix, ef, vw, prob, grad_att),
        [pltpu.VMEM((5 * nv, cw), F32), pltpu.VMEM((5 * hl, nv, 128), F32), pltpu.VMEM((n_j, eb, cw + 128), F32)],
        spill=tuple(range(1, n_j + 1)),
    )

    bit = n_p // 2
    pos_hi = flip(gate(pos_lo, z), "patch", bit)
    step = 2
    while step < owners:
        gpos = halve(gate(gpos, z), (me // step) % 2, parts * step)
        step *= 2

    got3 = exchange(z, "patch").reshape(n_p, rc, cw + 128)
    gx = [gx[0]] + [flip(gx[k], "var", k) for k in others]
    grad_pixels = sum(g.astype(F32) for g in gx).astype(BF16).reshape(4, vp, rows)[:, :vl].transpose(1, 0, 2)
    atts = gather_var(att, lambda x: gate(x, z))
    size = n_p // 2
    send, keep = call(
        functools.partial(weight_grad_kernel, n_j), "weight_grad", [shape((size, dp, cw), BF16)] * 2, (buf, *atts), [pltpu.VMEM((n_p, dp, cw), BF16)]
    )
    copies_z = call(
        functools.partial(sum_z_kernel, hl), "sum_z", shape((n_p, rc, cw + 128), BF16), (got3,), after=(send, *gx[1:])
    )
    z = exchange(copies_z.reshape(nr, cw + 128), "patch")

    step = 1
    halves = []
    while size > 1:
        size //= 2
        send, keep = call(
            functools.partial(halve_kernel, 2 * step),
            "halve",
            [shape((size, dp, cw), BF16)] * 2,
            (keep, flip(send, "patch", step)),
        )
        halves.append(send)
        step *= 2
    grad_w_out = (keep.astype(F32) + flip(send, "patch", step).astype(F32)).reshape(dp, cw)
    while bit > parts:
        bit //= 2
        pos_lo = jnp.concatenate([gate(pos_lo, copies_z), pos_hi], axis=0)
        pos_hi = flip(pos_lo, "patch", bit)
    grad_pos = lax.ppermute(gate(gpos, copies_z).reshape(per, cw), "patch", back)
    mixed = call(
        functools.partial(mixed_kernel, vl, n_j),
        "mixed",
        shape((rows, cw), BF16),
        (lengths, lead_hours, wo, vk, pos_lo, pos_hi, *atts),
        [pltpu.VMEM((owners, per, cw), BF16)],
        smem=2,
        after=(copies_z,),
    )
    fh = pad16(2 * rl + eb // 2 + 6)
    last = call(
        functools.partial(middle_kernel, eb, vl, n_j),
        "middle",
        [shape((fh, cw), BF16)] * n_j,
        (z, vk, k_blk, e_all, v_blk),
        [pltpu.VMEM((dp, 2 * cw), F32), pltpu.VMEM((nr, dp), F32), pltpu.VMEM((fh, cw), F32)],
        after=(halves[0],),
    )
    last = [last[0]] + [flip(last[k], "var", k) for k in others]
    gwv, gwk, gwq, gq, ge, gb, gl = call(
        functools.partial(final_kernel, eb, vl, rl, dp, n_j),
        "final",
        (
            shape((rl, D)),
            shape((rl, D)),
            shape((rl, D)),
            shape((1, rl)),
            shape((5, vl, dp)),
            shape((1, rl)),
            shape((1, rl)),
        ),
        (w_query, query[:, None], *last),
        [pltpu.VMEM((eb, dp), F32), pltpu.VMEM((8, D), F32)],
    )
    return (
        mixed,
        grad_pixels,
        ge.transpose(1, 0, 2),
        gq.reshape(rl),
        gwq,
        gwk,
        gwv,
        grad_w_out,
        gb.reshape(rl),
        grad_pos.astype(F32),
        gl.reshape(rl),
    )


def solution(mesh):
    both = P(("patch", "var"))
    rows2 = P(("patch", "var"), None)
    return jax.shard_map(
        shards,
        mesh=mesh,
        in_specs=(
            P("var", None, "patch"),
            P("var", None, "patch"),
            both,
            rows2,
            rows2,
            rows2,
            P("patch", "var"),
            both,
            P("patch", "var"),
            both,
            P(),
            P(),
            P(),
            P("patch", "var"),
        ),
        out_specs=(
            P("patch", "var"),
            P("var", None, "patch"),
            P("var", None, "patch"),
            both,
            rows2,
            rows2,
            rows2,
            P("patch", "var"),
            both,
            P("patch", "var"),
            both,
        ),
        check_vma=False,
    )
```

time: 147 us -> 130 us (0.88)
  the two profiles are of different devices: /device:TPU:9 before, /device:TPU:0 now
where the time goes in v3:
time: 130 us
  starting transfers between devices  58.1 us (45%)
  waiting for transfers between devices  35.4 us (27%)
  Pallas kernels  22.2 us (17%)
  local copies, waits for them, and re-layouts  9.39 us (7%)
  other arithmetic  3.52 us (3%)
    ppermute x28, starting transfers between devices, flip(): return lax.ppermute(x, axis, [(i, i ^ bit) for i in range(n)])  37.6 us
    ppermute x28, waiting for transfers between devices, flip(): return lax.ppermute(x, axis, [(i, i ^ bit) for i in range(n)])  31.4 us
    pallas_call x15, Pallas kernels, call(): pl.pallas_call(body, out_shape=shapes, in_specs=specs, out_specs=outs, sc...  22.2 us
    all_to_all x4, starting transfers between devices, exchange(): return lax.all_to_all(x, axis, 0, 0, tiled=True)  19.2 us
    unnamed x52, local copies, waits for them, and re-layouts  8.31 us
    all_to_all x4, waiting for transfers between devices, exchange(): return lax.all_to_all(x, axis, 0, 0, tiled=True)  4.08 us
  transfers between devices with their start and end apart: 34, of which 11 were waited for; matrix products, arithmetic and copies ran while one was open for 4% of the time, Pallas kernels for 12%

profile of v3, /device:TPU:0, one launch (start us, length us, event | category | flops | bytes accessed | tf_op | source)
XLA Modules:
  0.0 129.6 jit_solution(11690400337459888391)
XLA Ops:
  0.7 2.0 %pack.1 = (bf16[224,256]{1,0:T(8,128)(2,1)}, bf16[224,256]{1,0:T(8,128)(2,1)}, bf16[224,256]{1,0:T(8,128)(2,1)}, bf16[224,256]{1,0:T(8,128)(2,1)}) custom-call(f32[32,1024]{1,0:T(8,128)} %refs_0_.4, f32[32,1024]{1,0:T(8,128)} %refs_1_.3, f32[32,1024]{1,0:T(8,128)} %refs_0_.7, f32[1,32]{1,0:T(1,128)} %bitcast.43, f32[5,12,128]{2,1,0:T(8,128)} %bitcast.45, ...), custom_call_target="tpu_custom_call" | custom-call | flops 1152999936 | bytes 65536 | tf_op jit(solution)/shard_map/pack/pallas_call | solution.py:531
  2.7 2.4 %collective-permute-start = (bf16[224,256]{1,0:T(8,128)(2,1)}, bf16[224,256]{1,0:T(8,128)(2,1)S(1)}, u32[]{:S(2)}, u32[]{:S(2)}) collective-permute-start(bf16[224,256]{1,0:T(8,128)(2,1)} %get-tuple-element.67), channel_id=1, source_target_pairs={{0,3},{1,2},{2,1},{3,0},{4,7},{5,6},{6,5},{7,4},{8,11},{9,10},{10,... | collective-permute-start | bytes 344072 | tf_op jit(solution)/shard_map/ppermute | solution.py:27
  5.8 3.1 %collective-permute-start.1 = (bf16[1,128,256]{2,1,0:T(8,128)(2,1)S(1)}, bf16[1,128,256]{2,1,0:T(8,128)(2,1)S(1)}, u32[]{:S(2)}, u32[]{:S(2)}) collective-permute-start(bf16[1,128,256]{2,1,0:T(8,128)(2,1)S(1)} %convert_bitcast_fusion), channel_id=1, source_target_pairs={{0,16},{4,20},{8,24},{12,28},{16,0},{20,4},{24,8},{28,12},{1,17},{... | collective-permute-start | bytes 196616 | tf_op jit(solution)/shard_map/ppermute | solution.py:27
  10.8 1.8 %collective-permute-done.1 = bf16[1,128,256]{2,1,0:T(8,128)(2,1)S(1)} collective-permute-done((bf16[1,128,256]{2,1,0:T(8,128)(2,1)S(1)}, bf16[1,128,256]{2,1,0:T(8,128)(2,1)S(1)}, u32[]{:S(2)}, u32[]{:S(2)}) %collective-permute-start.1) | collective-permute-done | bytes 65568 | tf_op jit(solution)/shard_map/ppermute | solution.py:27
  18.0 5.4 %all-to-all-start = ((bf16[8,32,512]{2,1,0:T(8,128)(2,1)}), bf16[8,32,512]{2,1,0:T(8,128)(2,1)S(1)}, u32[]{:S(2)}, u32[]{:S(2)}) async-start(bf16[8,32,512]{2,1,0:T(8,128)(2,1)} %bitcast.5), calls=%async_computation | async-start | bytes 524288 | tf_op jit(solution)/shard_map/all_to_all | solution.py:22
  23.4 2.1 %collective-permute-start.3 = (bf16[4,128,256]{2,1,0:T(8,128)(2,1)S(1)}, bf16[4,128,256]{2,1,0:T(8,128)(2,1)S(1)}, u32[]{:S(2)}, u32[]{:S(2)}) collective-permute-start(bf16[4,128,256]{2,1,0:T(8,128)(2,1)S(1)} %constant_dynamic-update-slice_fusion.2.refs_0_), channel_id=1, source_target_pairs={{0,4},{4,0},{8,12},{12,8},{16,20},{20,16},{24,28},{28,24},{1,5},{5... | collective-permute-start | bytes 786440 | tf_op jit(solution)/shard_map/ppermute | solution.py:27
  25.5 8.0 %collective-permute-done.3.refs_1_ = bf16[4,128,256]{2,1,0:T(8,128)(2,1)S(1)} collective-permute-done((bf16[4,128,256]{2,1,0:T(8,128)(2,1)S(1)}, bf16[4,128,256]{2,1,0:T(8,128)(2,1)S(1)}, u32[]{:S(2)}, u32[]{:S(2)}) %collective-permute-start.3) | collective-permute-done | bytes 262176 | tf_op jit(solution)/shard_map/ppermute | solution.py:27
  34.3 2.1 %collective-permute-done.8.refs_5_.refs_7_ = bf16[1280,256]{1,0:T(8,128)(2,1)S(1)} collective-permute-done((bf16[1280,256]{1,0:T(8,128)(2,1)S(1)}, bf16[1280,256]{1,0:T(8,128)(2,1)S(1)}, u32[]{:S(2)}, u32[]{:S(2)}) %collective-permute-start.8) | collective-permute-done | bytes 655392 | tf_op jit(solution)/shard_map/ppermute | solution.py:27
  41.2 3.8 %all-to-all-start.1 = ((bf16[8,32,512]{2,1,0:T(8,128)(2,1)}), bf16[8,32,512]{2,1,0:T(8,128)(2,1)S(1)}, u32[]{:S(2)}, u32[]{:S(2)}) async-start(bf16[8,32,512]{2,1,0:T(8,128)(2,1)} %sum.1.refs_6_), calls=%async_computation.1 | async-start | bytes 524288 | tf_op jit(solution)/shard_map/all_to_all | solution.py:22
  46.9 1.9 %collective-permute-done.13 = bf16[2,256,256]{2,1,0:T(8,128)(2,1)} collective-permute-done((bf16[2,256,256]{2,1,0:T(8,128)(2,1)S(1)}, bf16[2,256,256]{2,1,0:T(8,128)(2,1)}, u32[]{:S(2)}, u32[]{:S(2)}) %collective-permute-start.13) | collective-permute-done | bytes 262176 | tf_op jit(solution)/shard_map/ppermute | solution.py:27
  49.9 4.1 %all-to-all-done.1 = bf16[8,32,512]{2,1,0:T(8,128)(2,1)S(1)} async-done(((bf16[8,32,512]{2,1,0:T(8,128)(2,1)}), bf16[8,32,512]{2,1,0:T(8,128)(2,1)S(1)}, u32[]{:S(2)}, u32[]{:S(2)}) %all-to-all-start.1) | async-done | bytes 262176 | tf_op jit(solution)/shard_map/all_to_all | solution.py:22
  55.0 3.6 %attention_forward.1 = (bf16[256,1024]{1,0:T(8,128)(2,1)}, f32[4,48,1024]{2,1,0:T(8,128)S(1)}, f32[5,48,4]{2,1,0:T(8,128)S(1)}, bf16[240,256]{1,0:T(8,128)(2,1)S(1)}) custom-call(bf16[256,512]{1,0:T(8,128)(2,1)S(1)} %bitcast.32, bf16[4,48,1024]{2,1,0:T(8,128)(2,1)S(1)} %copy-done.10, s32[4,48]{1,0:T(4,128)S(1)} %copy-done.3, ...), custom_call_target="tpu_custom_call" | custom-call | flops 1152999936 | bytes 65536 | tf_op jit(solution)/shard_map/attention_forward/pallas_call | solution.py:531
  61.4 3.9 %attention_backward.1 = (bf16[64,1024]{1,0:T(8,128)(2,1)S(1)}, bf16[64,1024]{1,0:T(8,128)(2,1)}, bf16[64,1024]{1,0:T(8,128)(2,1)S(1)}, bf16[64,1024]{1,0:T(8,128)(2,1)S(1)}, bf16[256,384]{1,0:T(8,128)(2,1)}) custom-call(bf16[4,48,1024]{2,1,0:T(8,128)(2,1)S(1)} %copy-done.10, f32[5,48,4]{2,1,0:T(8,128)S(1)} %get-tuple-element.85.refs_1_, ...), custom_call_target="tpu_custom_call" | custom-call | flops 1152999936 | bytes 65536 | tf_op jit(solution)/shard_map/attention_backward/pallas_call | solution.py:531
  65.3 7.5 %collective-permute-done.15.refs_3_.refs_8_ = bf16[256,1024]{1,0:T(8,128)(2,1)} collective-permute-done((bf16[256,1024]{1,0:T(8,128)(2,1)}, bf16[256,1024]{1,0:T(8,128)(2,1)}, u32[]{:S(2)}, u32[]{:S(2)}) %collective-permute-start.15) | collective-permute-done | bytes 524320 | tf_op jit(solution)/shard_map/ppermute | solution.py:27
  73.6 5.5 %collective-permute-start.28 = (bf16[1,256,256]{2,1,0:T(8,128)(2,1)S(1)}, bf16[1,256,256]{2,1,0:T(8,128)(2,1)}, u32[]{:S(2)}, u32[]{:S(2)}) collective-permute-start(bf16[1,256,256]{2,1,0:T(8,128)(2,1)S(1)} %constant_dynamic-slice_fusion), channel_id=1, source_target_pairs={{0,16},{4,20},{8,24},{12,28},{16,0},{20,4},{24,8},{28,12},{1,17},{... | collective-permute-start | bytes 393224 | tf_op jit(solution)/shard_map/ppermute | solution.py:27
  79.1 4.5 %all-to-all-start.2 = ((bf16[8,32,384]{2,1,0:T(8,128)(2,1)}), bf16[8,32,384]{2,1,0:T(8,128)(2,1)S(1)}, u32[]{:S(2)}, u32[]{:S(2)}) async-start(bf16[8,32,384]{2,1,0:T(8,128)(2,1)} %bitcast.11), calls=%async_computation.2 | async-start | bytes 393216 | tf_op jit(solution)/shard_map/all_to_all | solution.py:22
  85.5 4.8 %collective-permute-done.28 = bf16[1,256,256]{2,1,0:T(8,128)(2,1)} collective-permute-done((bf16[1,256,256]{2,1,0:T(8,128)(2,1)S(1)}, bf16[1,256,256]{2,1,0:T(8,128)(2,1)}, u32[]{:S(2)}, u32[]{:S(2)}) %collective-permute-start.28) | collective-permute-done | bytes 131104 | tf_op jit(solution)/shard_map/ppermute | solution.py:27
  91.3 2.0 %weight_grad.1 = (bf16[4,128,256]{2,1,0:T(8,128)(2,1)S(1)}, bf16[4,128,256]{2,1,0:T(8,128)(2,1)S(1)}) custom-call(bf16[1280,256]{1,0:T(8,128)(2,1)S(1)} %get-tuple-element.84.refs_2_.refs_4_.refs_0_, bf16[256,1024]{1,0:T(8,128)(2,1)} %get-tuple-element.89.refs_1_.refs_6_, bf16[256,1024]{1,0:T(8,128)(2,1)S(1)} %collective-permute-done.14.refs_2_.refs_7_, ...), custom_call_target="tpu_custom_call" | custom-call | flops 1152999936 | bytes 65536 | tf_op jit(solution)/shard_map/weight_grad/pallas_call | solution.py:531
  96.5 5.4 %all-to-all-start.3 = ((bf16[8,32,384]{2,1,0:T(8,128)(2,1)}), bf16[8,32,384]{2,1,0:T(8,128)(2,1)S(1)}, u32[]{:S(2)}, u32[]{:S(2)}) async-start(bf16[8,32,384]{2,1,0:T(8,128)(2,1)} %sum_z.1.refs_10_), calls=%async_computation.3 | async-start | bytes 393216 | tf_op jit(solution)/shard_map/all_to_all | solution.py:22
  103.5 4.8 %collective-permute-start.21 = (bf16[2,256,256]{2,1,0:T(8,128)(2,1)S(1)}, bf16[2,256,256]{2,1,0:T(8,128)(2,1)S(1)}, u32[]{:S(2)}, u32[]{:S(2)}) collective-permute-start(bf16[2,256,256]{2,1,0:T(8,128)(2,1)S(1)} %constant_dynamic-update-slice_fusion.4.refs_4_), channel_id=1, source_target_pairs={{0,8},{4,12},{8,0},{12,4},{16,24},{20,28},{24,16},{28,20},{1,9},{5... | collective-permute-start | bytes 786440 | tf_op jit(solution)/shard_map/ppermute | solution.py:27
  109.9 6.8 %collective-permute-start.26 = (bf16[2,128,256]{2,1,0:T(8,128)(2,1)S(1)}, bf16[2,128,256]{2,1,0:T(8,128)(2,1)S(1)}, u32[]{:S(2)}, u32[]{:S(2)}) collective-permute-start(bf16[2,128,256]{2,1,0:T(8,128)(2,1)S(1)} %get-tuple-element.102.refs_5_), channel_id=1, source_target_pairs={{0,8},{4,12},{8,0},{12,4},{16,24},{20,28},{24,16},{28,20},{1,9},{5... | collective-permute-start | bytes 393224 | tf_op jit(solution)/shard_map/ppermute | solution.py:27
  116.8 2.9 %mixed.1 = bf16[1024,256]{1,0:T(8,128)(2,1)} custom-call(s32[4]{0:T(128)S(1)} %copy-done.4, s32[4]{0:T(128)S(1)} %copy-done.5, bf16[1024,256]{1,0:T(8,128)(2,1)S(1)} %copy-done.8, bf16[256,512]{1,0:T(8,128)(2,1)S(1)} %bitcast.33, bf16[2,256,256]{2,1,0:T(8,128)(2,1)S(1)} %constant_dynamic-update-slice_fusion.4.refs_4_, ...), custom_call_target="tpu_custom_call" | custom-call | flops 1152999936 | bytes 65536 | tf_op jit(solution)/shard_map/mixed/pallas_call | solution.py:531
  122.3 2.0 %collective-permute-start.27 = (bf16[1,128,256]{2,1,0:T(8,128)(2,1)S(1)}, bf16[1,128,256]{2,1,0:T(8,128)(2,1)S(1)}, u32[]{:S(2)}, u32[]{:S(2)}) collective-permute-start(bf16[1,128,256]{2,1,0:T(8,128)(2,1)S(1)} %get-tuple-element.114), channel_id=1, source_target_pairs={{0,16},{4,20},{8,24},{12,28},{16,0},{20,4},{24,8},{28,12},{1,17},{... | collective-permute-start | bytes 196616 | tf_op jit(solution)/shard_map/ppermute | solution.py:27
  126.4 2.5 %collective-permute-done.27 = bf16[1,128,256]{2,1,0:T(8,128)(2,1)S(1)} collective-permute-done((bf16[1,128,256]{2,1,0:T(8,128)(2,1)S(1)}, bf16[1,128,256]{2,1,0:T(8,128)(2,1)S(1)}, u32[]{:S(2)}, u32[]{:S(2)}) %collective-permute-start.27) | collective-permute-done | bytes 65568 | tf_op jit(solution)/shard_map/ppermute | solution.py:27
  (125 shorter events, 35.5 us)
Async XLA Ops:
  2.7 8.1 %collective-permute-start = (bf16[224,256]{1,0:T(8,128)(2,1)}, bf16[224,256]{1,0:T(8,128)(2,1)S(1)}, u32[]{:S(2)}, u32[]{:S(2)}) collective-permute-start(bf16[224,256]{1,0:T(8,128)(2,1)} %get-tuple-element.67), channel_id=1, source_target_pairs={{0,3},{1,2},{2,1},{3,0},{4,7},{5,6},{6,5},{7,4},{8,11},{9,10},{10,... | collective-permute-start | bytes 344072 | tf_op jit(solution)/shard_map/ppermute | solution.py:27
  5.1 8.0 %collective-permute-start.4 = (bf16[224,256]{1,0:T(8,128)(2,1)}, bf16[224,256]{1,0:T(8,128)(2,1)S(1)}, u32[]{:S(2)}, u32[]{:S(2)}) collective-permute-start(bf16[224,256]{1,0:T(8,128)(2,1)} %get-tuple-element.71), channel_id=1, source_target_pairs={{0,1},{1,0},{2,3},{3,2},{4,5},{5,4},{6,7},{7,6},{8,9},{9,8},{10,11... | collective-permute-start | bytes 344072 | tf_op jit(solution)/shard_map/ppermute | solution.py:27
  16.3 18.0 %collective-permute-start.7 = (bf16[1280,256]{1,0:T(8,128)(2,1)S(1)}, bf16[1280,256]{1,0:T(8,128)(2,1)S(1)}, u32[]{:S(2)}, u32[]{:S(2)}) collective-permute-start(bf16[1280,256]{1,0:T(8,128)(2,1)S(1)} %get-tuple-element.84.refs_2_.refs_4_.refs_0_), channel_id=1, source_target_pairs={{0,2},{1,3},{2,0},{3,1},{4,6},{5,7},{6,4},{7,5},{8,10},{9,11},{10,... | collective-permute-start | bytes 1966088 | tf_op jit(solution)/shard_map/ppermute | solution.py:27
  18.0 15.6 %all-to-all-start = ((bf16[8,32,512]{2,1,0:T(8,128)(2,1)}), bf16[8,32,512]{2,1,0:T(8,128)(2,1)S(1)}, u32[]{:S(2)}, u32[]{:S(2)}) async-start(bf16[8,32,512]{2,1,0:T(8,128)(2,1)} %bitcast.5), calls=%async_computation | async-start | bytes 524288 | tf_op jit(solution)/shard_map/all_to_all | solution.py:22
  23.4 10.1 %collective-permute-start.3 = (bf16[4,128,256]{2,1,0:T(8,128)(2,1)S(1)}, bf16[4,128,256]{2,1,0:T(8,128)(2,1)S(1)}, u32[]{:S(2)}, u32[]{:S(2)}) collective-permute-start(bf16[4,128,256]{2,1,0:T(8,128)(2,1)S(1)} %constant_dynamic-update-slice_fusion.2.refs_0_), channel_id=1, source_target_pairs={{0,4},{4,0},{8,12},{12,8},{16,20},{20,16},{24,28},{28,24},{1,5},{5... | collective-permute-start | bytes 786440 | tf_op jit(solution)/shard_map/ppermute | solution.py:27
  25.5 8.8 %collective-permute-start.6 = (bf16[1280,256]{1,0:T(8,128)(2,1)S(1)}, bf16[1280,256]{1,0:T(8,128)(2,1)S(1)}, u32[]{:S(2)}, u32[]{:S(2)}) collective-permute-start(bf16[1280,256]{1,0:T(8,128)(2,1)S(1)} %get-tuple-element.84.refs_2_.refs_4_.refs_0_), channel_id=1, source_target_pairs={{0,1},{1,0},{2,3},{3,2},{4,5},{5,4},{6,7},{7,6},{8,9},{9,8},{10,11... | collective-permute-start | bytes 1966088 | tf_op jit(solution)/shard_map/ppermute | solution.py:27
  39.7 9.1 %collective-permute-start.13 = (bf16[2,256,256]{2,1,0:T(8,128)(2,1)S(1)}, bf16[2,256,256]{2,1,0:T(8,128)(2,1)}, u32[]{:S(2)}, u32[]{:S(2)}) collective-permute-start(bf16[2,256,256]{2,1,0:T(8,128)(2,1)S(1)} %dynamic-slice_bitcast_fusion), channel_id=1, source_target_pairs={{0,8},{4,12},{8,0},{12,4},{16,24},{20,28},{24,16},{28,20},{1,9},{5... | collective-permute-start | bytes 786440 | tf_op jit(solution)/shard_map/ppermute | solution.py:27
  41.2 12.8 %all-to-all-start.1 = ((bf16[8,32,512]{2,1,0:T(8,128)(2,1)}), bf16[8,32,512]{2,1,0:T(8,128)(2,1)S(1)}, u32[]{:S(2)}, u32[]{:S(2)}) async-start(bf16[8,32,512]{2,1,0:T(8,128)(2,1)} %sum.1.refs_6_), calls=%async_computation.1 | async-start | bytes 524288 | tf_op jit(solution)/shard_map/all_to_all | solution.py:22
  45.1 8.9 %collective-permute-start.10 = (bf16[256,256]{1,0:T(8,128)(2,1)}, bf16[256,256]{1,0:T(8,128)(2,1)S(1)}, u32[]{:S(2)}, u32[]{:S(2)}) collective-permute-start(bf16[256,256]{1,0:T(8,128)(2,1)} %get-tuple-element.81), channel_id=1, source_target_pairs={{0,1},{1,0},{2,3},{3,2},{4,5},{5,4},{6,7},{7,6},{8,9},{9,8},{10,11... | collective-permute-start | bytes 393224 | tf_op jit(solution)/shard_map/ppermute | solution.py:27
  45.1 8.9 %collective-permute-start.11 = (bf16[256,256]{1,0:T(8,128)(2,1)}, bf16[256,256]{1,0:T(8,128)(2,1)S(1)}, u32[]{:S(2)}, u32[]{:S(2)}) collective-permute-start(bf16[256,256]{1,0:T(8,128)(2,1)} %get-tuple-element.82), channel_id=1, source_target_pairs={{0,2},{1,3},{2,0},{3,1},{4,6},{5,7},{6,4},{7,5},{8,10},{9,11},{10,... | collective-permute-start | bytes 393224 | tf_op jit(solution)/shard_map/ppermute | solution.py:27
  46.2 7.8 %collective-permute-start.12 = (bf16[256,256]{1,0:T(8,128)(2,1)S(1)}, bf16[256,256]{1,0:T(8,128)(2,1)}, u32[]{:S(2)}, u32[]{:S(2)}) collective-permute-start(bf16[256,256]{1,0:T(8,128)(2,1)S(1)} %get-tuple-element.83), channel_id=1, source_target_pairs={{0,3},{1,2},{2,1},{3,0},{4,7},{5,6},{6,5},{7,4},{8,11},{9,10},{10,... | collective-permute-start | bytes 393224 | tf_op jit(solution)/shard_map/ppermute | solution.py:27
  58.6 14.2 %collective-permute-start.15 = (bf16[256,1024]{1,0:T(8,128)(2,1)}, bf16[256,1024]{1,0:T(8,128)(2,1)}, u32[]{:S(2)}, u32[]{:S(2)}) collective-permute-start(bf16[256,1024]{1,0:T(8,128)(2,1)} %get-tuple-element.89.refs_1_.refs_6_), channel_id=1, source_target_pairs={{0,2},{1,3},{2,0},{3,1},{4,6},{5,7},{6,4},{7,5},{8,10},{9,11},{10,... | collective-permute-start | bytes 1572872 | tf_op jit(solution)/shard_map/ppermute | solution.py:27
  61.3 29.9 %collective-permute-start.14 = (bf16[256,1024]{1,0:T(8,128)(2,1)}, bf16[256,1024]{1,0:T(8,128)(2,1)S(1)}, u32[]{:S(2)}, u32[]{:S(2)}) collective-permute-start(bf16[256,1024]{1,0:T(8,128)(2,1)} %get-tuple-element.89.refs_1_.refs_6_), channel_id=1, source_target_pairs={{0,1},{1,0},{2,3},{3,2},{4,5},{5,4},{6,7},{7,6},{8,9},{9,8},{10,11... | collective-permute-start | bytes 1572872 | tf_op jit(solution)/shard_map/ppermute | solution.py:27
  72.8 18.5 %collective-permute-start.16 = (bf16[256,1024]{1,0:T(8,128)(2,1)}, bf16[256,1024]{1,0:T(8,128)(2,1)S(1)}, u32[]{:S(2)}, u32[]{:S(2)}) collective-permute-start(bf16[256,1024]{1,0:T(8,128)(2,1)} %collective-permute-done.15.refs_3_.refs_8_), channel_id=1, source_target_pairs={{0,1},{1,0},{2,3},{3,2},{4,5},{5,4},{6,7},{7,6},{8,9},{9,8},{10,11... | collective-permute-start | bytes 1572872 | tf_op jit(solution)/shard_map/ppermute | solution.py:27
  72.9 11.5 %collective-permute-start.9 = (bf16[256,256]{1,0:T(8,128)(2,1)S(1)}, bf16[256,256]{1,0:T(8,128)(2,1)S(1)}, u32[]{:S(2)}, u32[]{:S(2)}) collective-permute-start(bf16[256,256]{1,0:T(8,128)(2,1)S(1)} %convert_element_type.54), channel_id=1, source_target_pairs={{0,0},{16,4},{4,8},{20,12},{8,16},{24,20},{12,24},{28,28},{1,1},{1... | collective-permute-start | bytes 393224 | tf_op jit(solution)/shard_map/ppermute | solution.py:629
  73.6 16.7 %collective-permute-start.28 = (bf16[1,256,256]{2,1,0:T(8,128)(2,1)S(1)}, bf16[1,256,256]{2,1,0:T(8,128)(2,1)}, u32[]{:S(2)}, u32[]{:S(2)}) collective-permute-start(bf16[1,256,256]{2,1,0:T(8,128)(2,1)S(1)} %constant_dynamic-slice_fusion), channel_id=1, source_target_pairs={{0,16},{4,20},{8,24},{12,28},{16,0},{20,4},{24,8},{28,12},{1,17},{... | collective-permute-start | bytes 393224 | tf_op jit(solution)/shard_map/ppermute | solution.py:27
  79.1 16.6 %all-to-all-start.2 = ((bf16[8,32,384]{2,1,0:T(8,128)(2,1)}), bf16[8,32,384]{2,1,0:T(8,128)(2,1)S(1)}, u32[]{:S(2)}, u32[]{:S(2)}) async-start(bf16[8,32,384]{2,1,0:T(8,128)(2,1)} %bitcast.11), calls=%async_computation.2 | async-start | bytes 393216 | tf_op jit(solution)/shard_map/all_to_all | solution.py:22
  84.3 10.0 %collective-permute-start.17 = (bf16[64,1024]{1,0:T(8,128)(2,1)}, bf16[64,1024]{1,0:T(8,128)(2,1)S(1)}, u32[]{:S(2)}, u32[]{:S(2)}) collective-permute-start(bf16[64,1024]{1,0:T(8,128)(2,1)} %get-tuple-element.92), channel_id=1, source_target_pairs={{0,1},{1,0},{2,3},{3,2},{4,5},{5,4},{6,7},{7,6},{8,9},{9,8},{10,11... | collective-permute-start | bytes 393224 | tf_op jit(solution)/shard_map/ppermute | solution.py:27
  84.4 10.0 %collective-permute-start.18 = (bf16[64,1024]{1,0:T(8,128)(2,1)S(1)}, bf16[64,1024]{1,0:T(8,128)(2,1)S(1)}, u32[]{:S(2)}, u32[]{:S(2)}) collective-permute-start(bf16[64,1024]{1,0:T(8,128)(2,1)S(1)} %get-tuple-element.93), channel_id=1, source_target_pairs={{0,2},{1,3},{2,0},{3,1},{4,6},{5,7},{6,4},{7,5},{8,10},{9,11},{10,... | collective-permute-start | bytes 393224 | tf_op jit(solution)/shard_map/ppermute | solution.py:27
  91.2 11.3 %collective-permute-start.20 = (bf16[1,256,256]{2,1,0:T(8,128)(2,1)S(1)}, bf16[1,256,256]{2,1,0:T(8,128)(2,1)}, u32[]{:S(2)}, u32[]{:S(2)}) collective-permute-start(bf16[1,256,256]{2,1,0:T(8,128)(2,1)S(1)} %bitcast.39), channel_id=1, source_target_pairs={{0,16},{4,20},{8,24},{12,28},{16,0},{20,4},{24,8},{28,12},{1,17},{... | collective-permute-start | bytes 393224 | tf_op jit(solution)/shard_map/ppermute | solution.py:27
  94.0 15.8 %collective-permute-start.22 = (bf16[4,128,256]{2,1,0:T(8,128)(2,1)S(1)}, bf16[4,128,256]{2,1,0:T(8,128)(2,1)S(1)}, u32[]{:S(2)}, u32[]{:S(2)}) collective-permute-start(bf16[4,128,256]{2,1,0:T(8,128)(2,1)S(1)} %get-tuple-element.91.refs_1_), channel_id=1, source_target_pairs={{0,4},{4,0},{8,12},{12,8},{16,20},{20,16},{24,28},{28,24},{1,5},{5... | collective-permute-start | bytes 786440 | tf_op jit(solution)/shard_map/ppermute | solution.py:27
  96.5 23.2 %all-to-all-start.3 = ((bf16[8,32,384]{2,1,0:T(8,128)(2,1)}), bf16[8,32,384]{2,1,0:T(8,128)(2,1)S(1)}, u32[]{:S(2)}, u32[]{:S(2)}) async-start(bf16[8,32,384]{2,1,0:T(8,128)(2,1)} %sum_z.1.refs_10_), calls=%async_computation.3 | async-start | bytes 393216 | tf_op jit(solution)/shard_map/all_to_all | solution.py:22
  103.5 13.3 %collective-permute-start.21 = (bf16[2,256,256]{2,1,0:T(8,128)(2,1)S(1)}, bf16[2,256,256]{2,1,0:T(8,128)(2,1)S(1)}, u32[]{:S(2)}, u32[]{:S(2)}) collective-permute-start(bf16[2,256,256]{2,1,0:T(8,128)(2,1)S(1)} %constant_dynamic-update-slice_fusion.4.refs_4_), channel_id=1, source_target_pairs={{0,8},{4,12},{8,0},{12,4},{16,24},{20,28},{24,16},{28,20},{1,9},{5... | collective-permute-start | bytes 786440 | tf_op jit(solution)/shard_map/ppermute | solution.py:27
  109.9 12.3 %collective-permute-start.26 = (bf16[2,128,256]{2,1,0:T(8,128)(2,1)S(1)}, bf16[2,128,256]{2,1,0:T(8,128)(2,1)S(1)}, u32[]{:S(2)}, u32[]{:S(2)}) collective-permute-start(bf16[2,128,256]{2,1,0:T(8,128)(2,1)S(1)} %get-tuple-element.102.refs_5_), channel_id=1, source_target_pairs={{0,8},{4,12},{8,0},{12,4},{16,24},{20,28},{24,16},{28,20},{1,9},{5... | collective-permute-start | bytes 393224 | tf_op jit(solution)/shard_map/ppermute | solution.py:27
  (34 other events, 145.9 us)

commit v4 on v3

--- a/solution.py
+++ b/solution.py
@@ -46,7 +46,11 @@
     pair = x.reshape(x.shape[0] // 2, 2, *x.shape[1:])
     send = lax.dynamic_index_in_dim(pair, 1 - bit, 1, False)
     keep = lax.dynamic_index_in_dim(pair, bit, 1, False)
-    return (keep.astype(F32) + flip(send, "patch", step).astype(F32)).astype(BF16)
+    return keep, flip(send, "patch", step)
+
+
+def joined(keep, got):
+    return (keep.astype(F32) + got.astype(F32)).astype(BF16)
 
 
 def nt(a, b):
@@ -99,8 +103,9 @@
         out_ref[rows + b * 4 * vp : rows + (b + 1) * 4 * vp, :] = tmp_ref[:, b * cw : (b + 1) * cw].astype(BF16)
 
 
-def pack_kernel(eb, v_ref, k_ref, wq_ref, q_ref, e_ref, b_ref, l_ref, *refs):
-    outs, tmp_ref = refs[:-1], refs[-1]
+def pack_kernel(eb, v_ref, k_ref, wq_ref, q_ref, e_ref, b_ref, l_ref, wo_ref, *refs):
+    outs, wo_low_ref, tmp_ref = refs[:-2], refs[-2], refs[-1]
+    wo_low_ref[0] = wo_ref[...].astype(BF16)
     cw = outs[0].shape[1]
     rl = v_ref.shape[0]
     _, vl, dp = e_ref.shape
@@ -120,9 +125,7 @@
         tmp_ref[spare : spare + 1, :] = hi
         tmp_ref[spare + 1 : spare + 2, :] = lo
         tmp_ref[eb : eb + rl, :] = k_ref[:, cols]
-        for m in range(len(outs)):
-            at = eb + (m + 1) * rl
-            tmp_ref[at : at + rl, :] = v_ref[:, pl.ds(pl.multiple_of((j ^ k ^ m) * cw, 128), cw)]
+        tmp_ref[eb + rl : eb + 2 * rl, :] = v_ref[:, cols]
         out_ref[...] = tmp_ref[...].astype(BF16)
 
 
@@ -139,10 +142,11 @@
 
 
 def product_kernel(eb, vl, rl, dp, *refs):
-    n = len(refs) - 7
-    got, (sums_ref, out_ref, e_ref, kb_ref, vb_ref, w_ref, p_ref) = refs[:n], refs[n:]
+    n = len(refs) - 5
+    got, (sums_ref, out_ref, ekv_ref, w_ref, p_ref) = refs[:n], refs[n:]
     cw = got[0].shape[1]
     spare = 5 * vl
+    lanes = -(-dp // 128) * 128
     p_id = lax.axis_index("patch")
     j = lax.axis_index("var")
     live = lax.broadcasted_iota(jnp.int32, (eb, dp), 0) < spare
@@ -150,14 +154,15 @@
     gs = [got[k][...].astype(F32) for k in range(n)]
     for k in range(n):
         small = small + gs[k][spare : spare + 4]
-        e_ref[pl.ds(pl.multiple_of((j ^ k) * eb, eb), eb), :] = jnp.where(live, gs[k][:eb, :dp], 0.0).astype(BF16)
-    for m in range(n + 1):
+        at = pl.ds(pl.multiple_of((j ^ k) * eb, eb), eb)
+        ekv_ref[at, :dp] = jnp.where(live, gs[k][:eb, :dp], 0.0).astype(BF16)
+    for m in range(2):
         at = eb + m * rl
         place(w_ref, 0, j, rl, [g[at : at + rl] for g in gs], slice(m * cw, (m + 1) * cw))
-    vb_ref[...] = w_ref[:, cw:].astype(BF16)
-    w = jnp.concatenate([vb_ref[:, :cw], w_ref[:, :cw].astype(BF16)], axis=1)
-    kb_ref[...] = w[:, cw:]
-    p_ref[...] = nn(e_ref[...], w)
+    key, value = w_ref[:, :cw].astype(BF16), w_ref[:, cw:].astype(BF16)
+    ekv_ref[:dp, lanes : lanes + cw] = key
+    ekv_ref[dp : 2 * dp, lanes : lanes + cw] = value
+    p_ref[...] = nn(ekv_ref[:, :dp], jnp.concatenate([value, key], axis=1))
     put_pair(p_ref, spare, cw, small[0:1] + small[1:2])
     put_pair(p_ref, spare + 1, cw, sums_ref[0:1])
     put_pair(p_ref, spare + 2, cw, sums_ref[1:2])
@@ -254,9 +259,7 @@
         out_ref[p] = x_ref[p].astype(BF16)
 
 
-def weight_kernel(n_j, vl, lo_ref, hi_ref, *refs):
-    bufs, (full_ref, *chunks), (pix_ref, x_ref) = refs[:n_j], refs[n_j : 2 * n_j], refs[2 * n_j :]
-    pixel_kernel(vl, full_ref.shape[1], *bufs, pix_ref, x_ref)
+def weight_kernel(lo_ref, hi_ref, full_ref, *chunks):
     half, dp, cw = lo_ref.shape
     p_id = lax.axis_index("patch")
     j = lax.axis_index("var")
@@ -293,7 +296,7 @@
 def weight_grad_kernel(n_j, buf_ref, *refs):
     atts, (send_ref, keep_ref, tmp_ref) = refs[:n_j], refs[n_j:]
     cw, rows = atts[0].shape
-    half, dp, _ = send_ref.shape
+    half, dp, _ = keep_ref.shape
     j = lax.axis_index("var")
     per = cw // dp
     for k in range(n_j):
@@ -302,19 +305,44 @@
             tmp_ref[(j ^ k) * per + t] = g[t * dp : (t + 1) * dp]
     own = lax.axis_index("patch") & 1
     for b in range(half):
-        send_ref[b] = tmp_ref[2 * b + 1 - own]
+        send_ref[b * dp : (b + 1) * dp, :] = tmp_ref[2 * b + 1 - own]
         keep_ref[b] = tmp_ref[2 * b + own]
 
 
-def halve_kernel(bit, keep_ref, got_ref, send_ref, next_ref):
-    own = jnp.where(lax.axis_index("patch") & bit, 1, 0)
-    for b in range(send_ref.shape[0]):
-        for ref, i in ((send_ref, 1 - own), (next_ref, own)):
-            ref[b] = (keep_ref[2 * b + i].astype(F32) + got_ref[2 * b + i].astype(F32)).astype(BF16)
-
-
-def mixed_kernel(vl, n_j, length_ref, lead_ref, w_ref, vk_ref, plo_ref, phi_ref, *refs):
-    atts, (out_ref, pos_ref) = refs[:n_j], refs[n_j:]
+def halve_kernel(bit, g_ref, got_ref, *refs):
+    count, dp, cw = g_ref.shape
+    own = jnp.where(lax.axis_index("patch") & (2 * bit), 1, 0)
+
+    def g_sum(b):
+        at = pl.ds(pl.multiple_of(b * dp, dp), dp)
+        return g_ref[b].astype(F32) + got_ref[at, :].astype(F32)
+
+    if count == 1:
+        pos_ref, out_ref, pos_out_ref = refs
+        out_ref[...] = g_sum(0)
+        pos_out_ref[...] = pos_ref[...].astype(F32)
+        return
+    send_ref, g_next = refs
+    for b in range(g_next.shape[0]):
+        send_ref[b * dp : (b + 1) * dp, :] = g_sum(2 * b + 1 - own).astype(BF16)
+        g_next[b] = g_sum(2 * b + own).astype(BF16)
+
+
+def pixel_add_kernel(keep_ref, got_ref, next_ref, send_ref):
+    for i in range(next_ref.shape[0]):
+        next_ref[i] = (keep_ref[2 * i].astype(F32) + got_ref[2 * i].astype(F32)).astype(BF16)
+        send_ref[i] = (keep_ref[2 * i + 1].astype(F32) + got_ref[2 * i + 1].astype(F32)).astype(BF16)
+
+
+def mixed_kernel(vl, n_j, length_ref, lead_ref, w_ref, vk_ref, plo_ref, phi_ref, pk_ref, pg_ref, *refs):
+    atts, (out_ref, px_ref, pos_ref, s_ref, x_ref) = refs[:n_j], refs[n_j:]
+    s_ref[...] = pk_ref[0].astype(F32) + pg_ref[0].astype(F32)
+    vp = s_ref.shape[0] // 4
+    for v in range(vl):
+        for p in range(4):
+            x_ref[4 * v + p : 4 * v + p + 1, :] = s_ref[p * vp + v : p * vp + v + 1, :]
+    for v in range(vl):
+        px_ref[v] = x_ref[4 * v : 4 * v + 4, :].astype(BF16)
     rows, cw = out_ref.shape
     spare = 5 * vl
     base = pad16(spare) - 16
@@ -373,7 +401,8 @@
                 for k in range(1, tile // 128):
                     part = part + t[:, k * 128 : (k + 1) * 128]
                 acc_ref[p * heads + h] += part
-        for k, ref in enumerate(outs):
+        for k in range(n_j):
+            ref = outs[k & 1].at[k >> 1]
             piece = jnp.concatenate([t for p in range(4) for t in (gx[p][k * vl : (k + 1) * vl], blank)], axis=0)
             ref[:, cols] = piece.astype(BF16)
         return carry
@@ -408,9 +437,11 @@
         out_ref[s, :, cw:] = pair
 
 
-def middle_kernel(eb, vl, n_j, z_ref, vk_ref, kb_ref, e_ref, v_ref, *refs):
+def middle_kernel(eb, vl, n_j, dp, z_ref, vk_ref, ekv_ref, *refs):
     chunks, (g_ref, ge_ref, s_ref) = refs[:n_j], refs[n_j:]
-    dp, cw = kb_ref.shape
+    cw = z_ref.shape[1] - 128
+    lanes = -(-dp // 128) * 128
+    key, value = ekv_ref[:dp, lanes : lanes + cw], ekv_ref[dp : 2 * dp, lanes : lanes + cw]
     rl = dp // n_j
     heads = cw // HS
     spare = 5 * vl
@@ -420,7 +451,7 @@
     small = vk_ref[base : base + 32, :].astype(F32)[spare - base : spare - base + 3]
     small = small[:, :cw] + small[:, cw:]
     qvec = small[0:1] * SCALE
-    g = tn(e_ref[...], z_ref[...])
+    g = tn(ekv_ref[:, :dp], z_ref[...])
     gfold = g[:, cw : cw + heads] + g[:, cw + heads : cw + 2 * heads]
     g_ref[:, :cw] = g[:, :cw]
     g_ref[:, cw:] = jnp.concatenate(
@@ -435,8 +466,8 @@
     ) * SCALE
     head = lax.broadcasted_iota(jnp.int32, (8, cw), 0) == lax.broadcasted_iota(jnp.int32, (8, cw), 1) // HS
     hi, lo = split(jnp.where(head, qvec, 0.0))
-    fold = nt(hi.astype(BF16), kb_ref[...]) + nt(lo.astype(BF16), kb_ref[...])
-    ge = nt(z_ref[:, :cw], v_ref[:, :cw])
+    fold = nt(hi.astype(BF16), key) + nt(lo.astype(BF16), key)
+    ge = nt(z_ref[:, :cw], value)
     for h in range(heads):
         ge = ge + gs[:, h : h + 1] * fold[h : h + 1, :]
     ge_ref[...] = ge
@@ -501,7 +532,7 @@
     gl_ref[...] = gl
 
 
-def call(kernel, name, out_shape, args, scratch=(), us=1.0, smem=0, after=(), first=False, spill=(), hbm=0):
+def call(kernel, name, out_shape, args, scratch=(), us=0.01, smem=0, after=(), first=False, spill=(), hbm=0):
     n = len(args)
     in_vmem = pl.BlockSpec(memory_space=pltpu.VMEM)
     specs = [pl.BlockSpec(memory_space=pltpu.SMEM)] * smem + [pl.BlockSpec() if first else in_vmem] * (n - smem)
@@ -557,16 +588,16 @@
     rl = w_value.shape[0]
     eb = pad16(5 * vl + 4)
     nr = n_j * eb
-    ch = pad16(eb + (n_j + 1) * rl)
+    ch = pad16(eb + 2 * rl)
     vp = -(-vl // 8) * 8
     rc = nr // n_p
     others = range(1, n_j)
 
-    pack = call(
+    *pack, wo_lo = call(
         functools.partial(pack_kernel, eb),
         "pack",
-        [shape((ch, cw), BF16)] * n_j,
-        (w_value, w_key, w_query, query[None, :], embed.transpose(1, 0, 2), b_out[None, :], w_lead[None, :]),
+        [shape((ch, cw), BF16)] * n_j + [shape((1, dp, cw), BF16)],
+        (w_value, w_key, w_query, query[None, :], embed.transpose(1, 0, 2), b_out[None, :], w_lead[None, :], w_out),
         [pltpu.VMEM((ch, cw), F32)],
         first=True,
     )
@@ -582,7 +613,6 @@
         after=(pack[0],),
     )
 
-    wo_lo = gate(w_out, pack[0]).astype(BF16)[None]
     bit = n_p // 2
     wo_hi = flip(wo_lo, "patch", bit)
     wo_steps = [wo_hi]
@@ -592,123 +622,144 @@
         wo_hi = flip(wo_lo, "patch", bit)
         wo_steps.append(wo_hi)
 
-    part, e_all, k_blk, v_blk = call(
+    part, ekv = call(
         functools.partial(product_kernel, eb, vl, rl, dp),
         "product",
-        (shape((nr, 2 * cw), BF16), shape((nr, dp), BF16), shape((dp, cw), BF16), shape((dp, D), BF16)),
+        (shape((nr, 2 * cw), BF16), shape((nr, -(-dp // 128) * 128 + cw), BF16)),
         (*got, sums),
-        [pltpu.VMEM((dp, (n_j + 1) * cw), F32), pltpu.VMEM((nr, 2 * cw), F32)],
-        us=1.0,
-        spill=(1, 2, 3),
-    )
-    got2 = exchange(gate(part, wo_steps[-2]), "patch").reshape(n_p, rc, 2 * cw)
-    copies = call(functools.partial(sum_kernel, vl), "sum", shape((n_p, rc, 2 * cw), BF16), (got2,), after=(wo_hi,))
+        [pltpu.VMEM((dp, 2 * cw), F32), pltpu.VMEM((nr, 2 * cw), F32)],
+        us=0.01,
+    )
+    got2 = exchange(part, "patch").reshape(n_p, rc, 2 * cw)
+    wo, *chunks = call(
+        weight_kernel, "weight", [shape((D, cw), BF16)] + [shape((cw, cw), BF16)] * (n_j - 1), (wo_lo, wo_hi)
+    )
+    copies = call(functools.partial(sum_kernel, vl), "sum", shape((n_p, rc, 2 * cw), BF16), (got2,), after=(wo,))
     vk = exchange(copies.reshape(nr, 2 * cw), "patch")
 
     bufs = gather_var(gate(buf, part), lambda x: gate(x, copies))
-
-    wo, *chunks, pix = call(
-        functools.partial(weight_kernel, n_j, vl),
-        "weight",
-        [shape((D, cw), BF16)] + [shape((cw, cw), BF16)] * (n_j - 1) + [shape((4, nv, rows), BF16)],
-        (wo_lo, wo_hi, *bufs),
+    pix = call(
+        functools.partial(pixel_kernel, vl, cw),
+        "pixels",
+        shape((4, nv, rows), BF16),
+        bufs,
         [pltpu.VMEM((4, nv, rows), F32)],
-        after=(copies,),
-    )
+    )
+
     chunks = [flip(c, "var", k + 1) for k, c in enumerate(chunks)]
     grad_att = call(
-        functools.partial(grad_kernel, n_j), "grad_att", shape((cw, rows), BF16), (wo, *chunks, *bufs)
+        functools.partial(grad_kernel, n_j), "grad_att", shape((cw, rows), BF16), (wo, *chunks, *bufs), after=(vk,)
     )
 
     parts = GROUP // rows
     owners = n_p // parts
     per = pos_embed.shape[0]
-    me = p_id // parts
     there = [(k * owners + i, parts * i + k) for i in range(owners) for k in range(parts)]
     back = [(b, a) for a, b in there]
-    pos_lo = lax.ppermute(gate(pos_embed, wo).astype(BF16), "patch", there)[None]
-    gpos = gate(buf, wo)[:rows].reshape(owners, per, cw)
-    gpos = halve(gpos, me % 2, parts)
-
+    pos_lo = lax.ppermute(gate(pos_embed, chunks[0]).astype(BF16), "patch", there)[None]
     att, prob, ef, vw = call(
         functools.partial(forward_kernel, 256, eb),
         "attention_forward",
-        (
-            shape((cw, rows), BF16),
-            shape((hl, nv, rows)),
-            shape((5, nv, hl)),
-            shape((5 * nv, cw), BF16),
-        ),
+        (shape((cw, rows), BF16), shape((hl, nv, rows)), shape((5, nv, hl)), shape((5 * nv, cw), BF16)),
         (vk, pix, avail),
         [pltpu.VMEM((n_j, eb, 2 * cw), F32), pltpu.VMEM((5 * nv, 2 * cw), F32)],
-        after=(*chunks, gpos),
-    )
-
-    *gx, z = call(
+        after=(grad_att, pos_lo),
+    )
+    px_keep, px_send, z = call(
         functools.partial(backward_kernel, 256, eb, n_j, vp),
         "attention_backward",
-        [shape((4 * vp, rows), BF16)] * n_j + [shape((nr, cw + 128), BF16)],
+        [shape((n_j // 2, 4 * vp, rows), BF16)] * 2 + [shape((nr, cw + 128), BF16)],
         (pix, ef, vw, prob, grad_att),
         [pltpu.VMEM((5 * nv, cw), F32), pltpu.VMEM((5 * hl, nv, 128), F32), pltpu.VMEM((n_j, eb, cw + 128), F32)],
-        spill=tuple(range(1, n_j + 1)),
-    )
-
+    )
+
+    got3 = exchange(z, "patch").reshape(n_p, rc, cw + 128)
+    me = p_id // parts
+    pos_hi = flip(gate(pos_lo, z), "patch", n_p // 2)
+    g_rows = halve(gate(buf, z)[:rows].reshape(owners, per, cw), me % 2, parts)
+    atts = [att] + [flip(gate(att, z), "var", k) for k in others]
+    copies_z = call(functools.partial(sum_z_kernel, hl), "sum_z", shape((n_p, rc, cw + 128), BF16), (got3,), after=(g_rows[1],))
+    zs = exchange(copies_z.reshape(nr, cw + 128), "patch")
+
+    size = n_p // 2
+    send, g_keep = call(
+        functools.partial(weight_grad_kernel, n_j),
+        "weight_grad",
+        [shape((size * dp, cw), BF16), shape((size, dp, cw), BF16)],
+        (buf, *atts),
+        [pltpu.VMEM((n_p, dp, cw), BF16)],
+        after=(copies_z,),
+    )
+    step = 1
+    size //= 2
+    send, g_keep = call(
+        functools.partial(halve_kernel, step),
+        "halve",
+        [shape((size * dp, cw), BF16), shape((size, dp, cw), BF16)],
+        (g_keep, flip(send, "patch", step)),
+    )
     bit = n_p // 2
-    pos_hi = flip(gate(pos_lo, z), "patch", bit)
-    step = 2
-    while step < owners:
-        gpos = halve(gate(gpos, z), (me // step) % 2, parts * step)
-        step *= 2
-
-    got3 = exchange(z, "patch").reshape(n_p, rc, cw + 128)
-    gx = [gx[0]] + [flip(gx[k], "var", k) for k in others]
-    grad_pixels = sum(g.astype(F32) for g in gx).astype(BF16).reshape(4, vp, rows)[:, :vl].transpose(1, 0, 2)
-    atts = gather_var(att, lambda x: gate(x, z))
-    size = n_p // 2
-    send, keep = call(
-        functools.partial(weight_grad_kernel, n_j), "weight_grad", [shape((size, dp, cw), BF16)] * 2, (buf, *atts), [pltpu.VMEM((n_p, dp, cw), BF16)]
-    )
-    copies_z = call(
-        functools.partial(sum_z_kernel, hl), "sum_z", shape((n_p, rc, cw + 128), BF16), (got3,), after=(send, *gx[1:])
-    )
-    z = exchange(copies_z.reshape(nr, cw + 128), "patch")
-
-    step = 1
-    halves = []
-    while size > 1:
-        size //= 2
-        send, keep = call(
-            functools.partial(halve_kernel, 2 * step),
-            "halve",
-            [shape((size, dp, cw), BF16)] * 2,
-            (keep, flip(send, "patch", step)),
-        )
-        halves.append(send)
-        step *= 2
-    grad_w_out = (keep.astype(F32) + flip(send, "patch", step).astype(F32)).reshape(dp, cw)
     while bit > parts:
         bit //= 2
         pos_lo = jnp.concatenate([gate(pos_lo, copies_z), pos_hi], axis=0)
         pos_hi = flip(pos_lo, "patch", bit)
-    grad_pos = lax.ppermute(gate(gpos, copies_z).reshape(per, cw), "patch", back)
-    mixed = call(
+    turn = 2
+    while turn < owners:
+        g_rows = halve(gate(joined(*g_rows), copies_z), (me // turn) % 2, parts * turn)
+        turn *= 2
+    px_got = flip(gate(px_send, copies_z), "var", 1)
+    fh = pad16(2 * rl + eb // 2 + 6)
+    last = call(
+        functools.partial(middle_kernel, eb, vl, n_j, dp),
+        "middle",
+        [shape((fh, cw), BF16)] * n_j,
+        (zs, vk, ekv),
+        [pltpu.VMEM((dp, 2 * cw), F32), pltpu.VMEM((nr, dp), F32), pltpu.VMEM((fh, cw), F32)],
+        after=(send,),
+    )
+
+    def late(x):
+        return gate(x, last[0])
+
+    while size > 1:
+        size //= 2
+        step *= 2
+        send, g_keep = call(
+            functools.partial(halve_kernel, step),
+            "halve",
+            [shape((size * dp, cw), BF16), shape((size, dp, cw), BF16)],
+            (g_keep, flip(send, "patch", step)),
+            after=(last[0],),
+        )
+    grad_pos = lax.ppermute(joined(g_rows[0], late(g_rows[1])).reshape(per, cw), "patch", back)
+    grad_w_out, grad_pos = call(
+        functools.partial(halve_kernel, 2 * step),
+        "halve",
+        (shape((dp, cw)), shape((per, cw))),
+        (g_keep, flip(send, "patch", 2 * step), grad_pos),
+    )
+
+    bit = 1
+    while 2 * bit < n_j:
+        bit *= 2
+        px_keep, px_send = call(
+            pixel_add_kernel,
+            "pixel_add",
+            [shape((n_j // (2 * bit), 4 * vp, rows), BF16)] * 2,
+            (px_keep, px_got),
+            after=(send,),
+        )
+        px_got = flip(px_send, "var", bit)
+    mixed, grad_pixels = call(
         functools.partial(mixed_kernel, vl, n_j),
         "mixed",
-        shape((rows, cw), BF16),
-        (lengths, lead_hours, wo, vk, pos_lo, pos_hi, *atts),
-        [pltpu.VMEM((owners, per, cw), BF16)],
+        (shape((rows, cw), BF16), shape((vl, 4, rows), BF16)),
+        (lengths, lead_hours, wo, vk, pos_lo, pos_hi, px_keep, px_got, *atts),
+        [pltpu.VMEM((owners, per, cw), BF16), pltpu.VMEM((4 * vp, rows), F32), pltpu.VMEM((4 * vl, rows), F32)],
         smem=2,
-        after=(copies_z,),
-    )
-    fh = pad16(2 * rl + eb // 2 + 6)
-    last = call(
-        functools.partial(middle_kernel, eb, vl, n_j),
-        "middle",
-        [shape((fh, cw), BF16)] * n_j,
-        (z, vk, k_blk, e_all, v_blk),
-        [pltpu.VMEM((dp, 2 * cw), F32), pltpu.VMEM((nr, dp), F32), pltpu.VMEM((fh, cw), F32)],
-        after=(halves[0],),
-    )
+        after=(send,),
+    )
+
     last = [last[0]] + [flip(last[k], "var", k) for k in others]
     gwv, gwk, gwq, gq, ge, gb, gl = call(
         functools.partial(final_kernel, eb, vl, rl, dp, n_j),
@@ -724,6 +775,7 @@
         ),
         (w_query, query[:, None], *last),
         [pltpu.VMEM((eb, dp), F32), pltpu.VMEM((8, D), F32)],
+        after=(mixed,),
     )
     return (
         mixed,
@@ -735,7 +787,7 @@
         gwv,
         grad_w_out,
         gb.reshape(rl),
-        grad_pos.astype(F32),
+        grad_pos,
         gl.reshape(rl),
     )
 

time: 130 us -> 119 us (0.915)
  starting transfers between devices: 58.1 us -> 47.8 us
  Pallas kernels: 22.2 us -> 27.8 us
  waiting for transfers between devices: 35.4 us -> 30.6 us
  local copies, waits for them, and re-layouts: 9.39 us -> 7.12 us
    ppermute x28 -> x27, waiting for transfers between devices: 31.4 us -> 22.6 us  [flip(): return lax.ppermute(x, axis, [(i, i ^ bit) for i in range(n)])]
    ppermute x28 -> x27, starting transfers between devices: 37.6 us -> 29.6 us  [flip(): return lax.ppermute(x, axis, [(i, i ^ bit) for i in range(n)])]
    pallas_call x15 -> x18, Pallas kernels: 22.2 us -> 27.8 us  [call(): pl.pallas_call(body, out_shape=shapes, in_specs=specs, out_specs=outs, sc...]
    all_to_all x4, waiting for transfers between devices: 4.08 us -> 8.01 us  [exchange(): return lax.all_to_all(x, axis, 0, 0, tiled=True)]
    all_to_all x4, starting transfers between devices: 19.2 us -> 16 us  [exchange(): return lax.all_to_all(x, axis, 0, 0, tiled=True)]
    unnamed x52 -> x49, local copies, waits for them, and re-layouts: 8.31 us -> 5.57 us
    squeeze x2, local copies, waits for them, and re-layouts: 0.04 us -> 1.39 us  [halve(): send = lax.dynamic_index_in_dim(pair, 1 - bit, 1, False)]
    convert_element_type x5 -> x2, other arithmetic: 2.84 us -> 2.38 us  [the longest x1 1.71 us: joined(): return (keep.astype(F32) + got.astype(F32)).astype(BF16)]
  transfers between devices with their start and end apart: 34 -> 33, of which waited for: 11 -> 8; matrix products, arithmetic and copies ran while one was open for 4% -> 4% of each run, Pallas kernels for 12% -> 15%
where the time goes in v4:
time: 119 us; the launch traced here: 118 us
  starting transfers between devices  47.8 us (40%)
  waiting for transfers between devices  30.6 us (26%)
  Pallas kernels  27.8 us (23%)
  local copies, waits for them, and re-layouts  7.12 us (6%)
  other arithmetic  3.37 us (3%)
    ppermute x27, starting transfers between devices, flip(): return lax.ppermute(x, axis, [(i, i ^ bit) for i in range(n)])  29.6 us
    pallas_call x18, Pallas kernels, call(): pl.pallas_call(body, out_shape=shapes, in_specs=specs, out_specs=outs, sc...  27.8 us
    ppermute x27, waiting for transfers between devices, flip(): return lax.ppermute(x, axis, [(i, i ^ bit) for i in range(n)])  22.6 us
    all_to_all x4, starting transfers between devices, exchange(): return lax.all_to_all(x, axis, 0, 0, tiled=True)  16 us
    all_to_all x4, waiting for transfers between devices, exchange(): return lax.all_to_all(x, axis, 0, 0, tiled=True)  8.01 us
    unnamed x49, local copies, waits for them, and re-layouts  5.57 us
  transfers between devices with their start and end apart: 33, of which 8 were waited for; matrix products, arithmetic and copies ran while one was open for 4% of the time, Pallas kernels for 15%

profile of v4, /device:TPU:0, one launch (start us, length us, event | category | flops | bytes accessed | tf_op | source)
XLA Modules:
  0.0 117.7 jit_solution(17911732990364699492)
XLA Ops:
  0.7 2.1 %pack.1 = (bf16[128,256]{1,0:T(8,128)(2,1)}, bf16[128,256]{1,0:T(8,128)(2,1)}, bf16[128,256]{1,0:T(8,128)(2,1)}, bf16[128,256]{1,0:T(8,128)(2,1)}, bf16[1,128,256]{2,1,0:T(8,128)(2,1)}) custom-call(f32[32,1024]{1,0:T(8,128)} %refs_0_.4, f32[32,1024]{1,0:T(8,128)} %refs_1_.3, f32[32,1024]{1,0:T(8,128)} %refs_0_.7, f32[1,32]{1,0:T(1,128)} %bitcast.36, ...), custom_call_target="tpu_custom_call" | custom-call | flops 11530000 | bytes 65536 | tf_op jit(solution)/shard_map/pack/pallas_call | solution.py:562
  2.7 2.4 %collective-permute-start = (bf16[128,256]{1,0:T(8,128)(2,1)}, bf16[128,256]{1,0:T(8,128)(2,1)S(1)}, u32[]{:S(2)}, u32[]{:S(2)}) collective-permute-start(bf16[128,256]{1,0:T(8,128)(2,1)} %get-tuple-element.67), channel_id=1, source_target_pairs={{0,3},{1,2},{2,1},{3,0},{4,7},{5,6},{6,5},{7,4},{8,11},{9,10},{10,... | collective-permute-start | bytes 196616 | tf_op jit(solution)/shard_map/ppermute | solution.py:27
  5.8 3.1 %collective-permute-start.1 = (bf16[1,128,256]{2,1,0:T(8,128)(2,1)}, bf16[1,128,256]{2,1,0:T(8,128)(2,1)S(1)}, u32[]{:S(2)}, u32[]{:S(2)}) collective-permute-start(bf16[1,128,256]{2,1,0:T(8,128)(2,1)} %get-tuple-element.68), channel_id=1, source_target_pairs={{0,16},{4,20},{8,24},{12,28},{16,0},{20,4},{24,8},{28,12},{1,17},{... | collective-permute-start | bytes 196616 | tf_op jit(solution)/shard_map/ppermute | solution.py:27
  15.8 3.4 %all-to-all-start = ((bf16[8,32,512]{2,1,0:T(8,128)(2,1)}), bf16[8,32,512]{2,1,0:T(8,128)(2,1)S(1)}, u32[]{:S(2)}, u32[]{:S(2)}) async-start(bf16[8,32,512]{2,1,0:T(8,128)(2,1)} %bitcast.4), calls=%async_computation | async-start | bytes 524288 | tf_op jit(solution)/shard_map/all_to_all | solution.py:22
  19.3 2.0 %collective-permute-start.3 = (bf16[4,128,256]{2,1,0:T(8,128)(2,1)S(1)}, bf16[4,128,256]{2,1,0:T(8,128)(2,1)S(1)}, u32[]{:S(2)}, u32[]{:S(2)}) collective-permute-start(bf16[4,128,256]{2,1,0:T(8,128)(2,1)S(1)} %constant_dynamic-update-slice_fusion.2.refs_0_), channel_id=1, source_target_pairs={{0,4},{4,0},{8,12},{12,8},{16,20},{20,16},{24,28},{28,24},{1,5},{5... | collective-permute-start | bytes 786440 | tf_op jit(solution)/shard_map/ppermute | solution.py:27
  21.3 8.4 %collective-permute-done.3.refs_1_ = bf16[4,128,256]{2,1,0:T(8,128)(2,1)S(1)} collective-permute-done((bf16[4,128,256]{2,1,0:T(8,128)(2,1)S(1)}, bf16[4,128,256]{2,1,0:T(8,128)(2,1)S(1)}, u32[]{:S(2)}, u32[]{:S(2)}) %collective-permute-start.3) | collective-permute-done | bytes 262176 | tf_op jit(solution)/shard_map/ppermute | solution.py:27
  31.2 4.7 %all-to-all-start.1 = ((bf16[8,32,512]{2,1,0:T(8,128)(2,1)}), bf16[8,32,512]{2,1,0:T(8,128)(2,1)S(1)}, u32[]{:S(2)}, u32[]{:S(2)}) async-start(bf16[8,32,512]{2,1,0:T(8,128)(2,1)} %sum.1), calls=%async_computation.1 | async-start | bytes 524288 | tf_op jit(solution)/shard_map/all_to_all | solution.py:22
  42.6 2.0 %collective-permute-done.12.refs_3_ = bf16[256,256]{1,0:T(8,128)(2,1)} collective-permute-done((bf16[256,256]{1,0:T(8,128)(2,1)}, bf16[256,256]{1,0:T(8,128)(2,1)}, u32[]{:S(2)}, u32[]{:S(2)}) %collective-permute-start.12) | collective-permute-done | bytes 131104 | tf_op jit(solution)/shard_map/ppermute | solution.py:27
  45.4 1.9 %grad_att.1.refs_3_.refs_4_ = bf16[256,1024]{1,0:T(8,128)(2,1)S(1)} custom-call(bf16[1024,256]{1,0:T(8,128)(2,1)S(1)} %get-tuple-element.70.refs_1_.refs_0_.refs_2_, bf16[256,256]{1,0:T(8,128)(2,1)S(1)} %collective-permute-done.6.refs_1_, bf16[256,256]{1,0:T(8,128)(2,1)S(1)} %collective-permute-done.11.refs_2_, ...), custom_call_target="tpu_custom_call" | custom-call | flops 11530000 | bytes 65536 | tf_op jit(solution)/shard_map/grad_att/pallas_call | solution.py:562
  47.3 2.7 %attention_forward.1 = (bf16[256,1024]{1,0:T(8,128)(2,1)S(1)}, f32[4,48,1024]{2,1,0:T(8,128)S(1)}, f32[5,48,4]{2,1,0:T(8,128)S(1)}, bf16[240,256]{1,0:T(8,128)(2,1)S(1)}) custom-call(bf16[256,512]{1,0:T(8,128)(2,1)S(1)} %bitcast.25, bf16[4,48,1024]{2,1,0:T(8,128)(2,1)S(1)} %pixels.1.refs_1_.refs_0_, s32[4,48]{1,0:T(4,128)S(1)} %copy-done.12, ...), custom_call_target="tpu_custom_call" | custom-call | flops 11530000 | bytes 65536 | tf_op jit(solution)/shard_map/attention_forward/pallas_call | solution.py:562
  50.1 3.1 %attention_backward.1 = (bf16[2,64,1024]{2,1,0:T(8,128)(2,1)S(1)}, bf16[2,64,1024]{2,1,0:T(8,128)(2,1)}, bf16[256,384]{1,0:T(8,128)(2,1)S(1)}) custom-call(bf16[4,48,1024]{2,1,0:T(8,128)(2,1)S(1)} %pixels.1.refs_1_.refs_0_, f32[5,48,4]{2,1,0:T(8,128)S(1)} %get-tuple-element.83.refs_1_, bf16[240,256]{1,0:T(8,128)(2,1)S(1)} %get-tuple-element.84.refs_2_, ...), custom_call_target="tpu_custom_call" | custom-call | flops 11530000 | bytes 65536 | tf_op jit(solution)/shard_map/attention_backward/pallas_call | solution.py:562
  56.6 1.9 %collective-permute-start.13 = (bf16[2,256,256]{2,1,0:T(8,128)(2,1)}, bf16[2,256,256]{2,1,0:T(8,128)(2,1)S(1)}, u32[]{:S(2)}, u32[]{:S(2)}) collective-permute-start(bf16[2,256,256]{2,1,0:T(8,128)(2,1)} %dynamic-slice_bitcast_fusion), channel_id=1, source_target_pairs={{0,8},{4,12},{8,0},{12,4},{16,24},{20,28},{24,16},{28,20},{1,9},{5... | collective-permute-start | bytes 786440 | tf_op jit(solution)/shard_map/ppermute | solution.py:27
  58.6 4.5 %all-to-all-start.2 = ((bf16[8,32,384]{2,1,0:T(8,128)(2,1)}), bf16[8,32,384]{2,1,0:T(8,128)(2,1)}, u32[]{:S(2)}, u32[]{:S(2)}) async-start(bf16[8,32,384]{2,1,0:T(8,128)(2,1)} %bitcast.32), calls=%async_computation.2 | async-start | bytes 393216 | tf_op jit(solution)/shard_map/all_to_all | solution.py:22
  63.0 2.9 %collective-permute-start.14 = (bf16[1,256,256]{2,1,0:T(8,128)(2,1)S(1)}, bf16[1,256,256]{2,1,0:T(8,128)(2,1)S(1)}, u32[]{:S(2)}, u32[]{:S(2)}) collective-permute-start(bf16[1,256,256]{2,1,0:T(8,128)(2,1)S(1)} %bitcast.30), channel_id=1, source_target_pairs={{0,16},{4,20},{8,24},{12,28},{16,0},{20,4},{24,8},{28,12},{1,17},{... | collective-permute-start | bytes 393224 | tf_op jit(solution)/shard_map/ppermute | solution.py:27
  67.7 7.1 %all-to-all-done.2.refs_0_ = bf16[8,32,384]{2,1,0:T(8,128)(2,1)} async-done(((bf16[8,32,384]{2,1,0:T(8,128)(2,1)}), bf16[8,32,384]{2,1,0:T(8,128)(2,1)}, u32[]{:S(2)}, u32[]{:S(2)}) %all-to-all-start.2) | async-done | bytes 196640 | tf_op jit(solution)/shard_map/all_to_all | solution.py:22
  74.8 1.8 %sum_z.1.refs_5_ = bf16[8,32,384]{2,1,0:T(8,128)(2,1)} custom-call(bf16[8,32,384]{2,1,0:T(8,128)(2,1)} %all-to-all-done.2.refs_0_, bf16[2,256,256]{2,1,0:T(8,128)(2,1)S(1)} %collective-permute-done.13.refs_1_), custom_call_target="tpu_custom_call" | custom-call | flops 11530000 | bytes 65536 | tf_op jit(solution)/shard_map/sum_z/pallas_call | solution.py:562
  76.6 3.4 %all-to-all-start.3 = ((bf16[8,32,384]{2,1,0:T(8,128)(2,1)}), bf16[8,32,384]{2,1,0:T(8,128)(2,1)S(1)}, u32[]{:S(2)}, u32[]{:S(2)}) async-start(bf16[8,32,384]{2,1,0:T(8,128)(2,1)} %sum_z.1.refs_5_), calls=%async_computation.3 | async-start | bytes 393216 | tf_op jit(solution)/shard_map/all_to_all | solution.py:22
  80.0 1.8 %weight_grad.1 = (bf16[512,256]{1,0:T(8,128)(2,1)S(1)}, bf16[4,128,256]{2,1,0:T(8,128)(2,1)S(1)}) custom-call(bf16[1280,256]{1,0:T(8,128)(2,1)S(1)} %get-tuple-element.87.refs_0_.refs_4_, bf16[256,1024]{1,0:T(8,128)(2,1)S(1)} %get-tuple-element.94.refs_1_.refs_8_, bf16[256,1024]{1,0:T(8,128)(2,1)S(1)} %collective-permute-done.17.refs_2_.refs_9_, ...), custom_call_target="tpu_custom_call" | custom-call | flops 11530000 | bytes 65536 | tf_op jit(solution)/shard_map/weight_grad/pallas_call | solution.py:562
  81.9 2.0 %collective-permute-start.20 = (bf16[512,256]{1,0:T(8,128)(2,1)S(1)}, bf16[512,256]{1,0:T(8,128)(2,1)S(1)}, u32[]{:S(2)}, u32[]{:S(2)}) collective-permute-start(bf16[512,256]{1,0:T(8,128)(2,1)S(1)} %get-tuple-element.96), channel_id=1, source_target_pairs={{0,4},{4,0},{8,12},{12,8},{16,20},{20,16},{24,28},{28,24},{1,5},{5... | collective-permute-start | bytes 786440 | tf_op jit(solution)/shard_map/ppermute | solution.py:27
  84.5 2.4 %collective-permute-start.27 = (bf16[1,256,256]{2,1,0:T(8,128)(2,1)}, bf16[1,256,256]{2,1,0:T(8,128)(2,1)}, u32[]{:S(2)}, u32[]{:S(2)}) collective-permute-start(bf16[1,256,256]{2,1,0:T(8,128)(2,1)} %constant_dynamic-slice_fusion), channel_id=1, source_target_pairs={{0,16},{4,20},{8,24},{12,28},{16,0},{20,4},{24,8},{28,12},{1,17},{... | collective-permute-start | bytes 393224 | tf_op jit(solution)/shard_map/ppermute | solution.py:27
  88.5 2.1 %collective-permute-done.20.refs_1_ = bf16[512,256]{1,0:T(8,128)(2,1)S(1)} collective-permute-done((bf16[512,256]{1,0:T(8,128)(2,1)S(1)}, bf16[512,256]{1,0:T(8,128)(2,1)S(1)}, u32[]{:S(2)}, u32[]{:S(2)}) %collective-permute-start.20) | collective-permute-done | bytes 262176 | tf_op jit(solution)/shard_map/ppermute | solution.py:27
  95.3 4.7 %collective-permute-done.21.refs_1_ = bf16[256,256]{1,0:T(8,128)(2,1)} collective-permute-done((bf16[256,256]{1,0:T(8,128)(2,1)}, bf16[256,256]{1,0:T(8,128)(2,1)}, u32[]{:S(2)}, u32[]{:S(2)}) %collective-permute-start.21) | collective-permute-done | bytes 131104 | tf_op jit(solution)/shard_map/ppermute | solution.py:27
  105.9 4.1 %collective-permute-done.26.refs_1_ = bf16[128,256]{1,0:T(8,128)(2,1)S(1)} collective-permute-done((bf16[128,256]{1,0:T(8,128)(2,1)S(1)}, bf16[128,256]{1,0:T(8,128)(2,1)S(1)}, u32[]{:S(2)}, u32[]{:S(2)}) %collective-permute-start.26) | collective-permute-done | bytes 65568 | tf_op jit(solution)/shard_map/ppermute | solution.py:27
  112.2 2.8 %mixed.1 = (bf16[1024,256]{1,0:T(8,128)(2,1)}, bf16[12,4,1024]{2,1,0:T(4,128)(2,1)}) custom-call(s32[4]{0:T(128)S(1)} %copy-done.14, s32[4]{0:T(128)S(1)} %copy-done.16, bf16[1024,256]{1,0:T(8,128)(2,1)S(1)} %get-tuple-element.70.refs_1_.refs_0_.refs_2_, bf16[256,512]{1,0:T(8,128)(2,1)S(1)} %bitcast.27, ...), custom_call_target="tpu_custom_call" | custom-call | flops 11530000 | bytes 65536 | tf_op jit(solution)/shard_map/mixed/pallas_call | solution.py:562
  (119 shorter events, 39.4 us)
Async XLA Ops:
  2.7 8.9 %collective-permute-start = (bf16[128,256]{1,0:T(8,128)(2,1)}, bf16[128,256]{1,0:T(8,128)(2,1)S(1)}, u32[]{:S(2)}, u32[]{:S(2)}) collective-permute-start(bf16[128,256]{1,0:T(8,128)(2,1)} %get-tuple-element.67), channel_id=1, source_target_pairs={{0,3},{1,2},{2,1},{3,0},{4,7},{5,6},{6,5},{7,4},{8,11},{9,10},{10,... | collective-permute-start | bytes 196616 | tf_op jit(solution)/shard_map/ppermute | solution.py:27
  5.8 8.3 %collective-permute-start.1 = (bf16[1,128,256]{2,1,0:T(8,128)(2,1)}, bf16[1,128,256]{2,1,0:T(8,128)(2,1)S(1)}, u32[]{:S(2)}, u32[]{:S(2)}) collective-permute-start(bf16[1,128,256]{2,1,0:T(8,128)(2,1)} %get-tuple-element.68), channel_id=1, source_target_pairs={{0,16},{4,20},{8,24},{12,28},{16,0},{20,4},{24,8},{28,12},{1,17},{... | collective-permute-start | bytes 196616 | tf_op jit(solution)/shard_map/ppermute | solution.py:27
  12.6 18.6 %collective-permute-start.9 = (bf16[1280,256]{1,0:T(8,128)(2,1)S(1)}, bf16[1280,256]{1,0:T(8,128)(2,1)S(1)}, u32[]{:S(2)}, u32[]{:S(2)}) collective-permute-start(bf16[1280,256]{1,0:T(8,128)(2,1)S(1)} %get-tuple-element.87.refs_0_.refs_4_), channel_id=1, source_target_pairs={{0,2},{1,3},{2,0},{3,1},{4,6},{5,7},{6,4},{7,5},{8,10},{9,11},{10,... | collective-permute-start | bytes 1966088 | tf_op jit(solution)/shard_map/ppermute | solution.py:27
  15.8 14.7 %all-to-all-start = ((bf16[8,32,512]{2,1,0:T(8,128)(2,1)}), bf16[8,32,512]{2,1,0:T(8,128)(2,1)S(1)}, u32[]{:S(2)}, u32[]{:S(2)}) async-start(bf16[8,32,512]{2,1,0:T(8,128)(2,1)} %bitcast.4), calls=%async_computation | async-start | bytes 524288 | tf_op jit(solution)/shard_map/all_to_all | solution.py:22
  19.3 10.4 %collective-permute-start.3 = (bf16[4,128,256]{2,1,0:T(8,128)(2,1)S(1)}, bf16[4,128,256]{2,1,0:T(8,128)(2,1)S(1)}, u32[]{:S(2)}, u32[]{:S(2)}) collective-permute-start(bf16[4,128,256]{2,1,0:T(8,128)(2,1)S(1)} %constant_dynamic-update-slice_fusion.2.refs_0_), channel_id=1, source_target_pairs={{0,4},{4,0},{8,12},{12,8},{16,20},{20,16},{24,28},{28,24},{1,5},{5... | collective-permute-start | bytes 786440 | tf_op jit(solution)/shard_map/ppermute | solution.py:27
  21.3 18.8 %collective-permute-start.8 = (bf16[1280,256]{1,0:T(8,128)(2,1)S(1)}, bf16[1280,256]{1,0:T(8,128)(2,1)S(1)}, u32[]{:S(2)}, u32[]{:S(2)}) collective-permute-start(bf16[1280,256]{1,0:T(8,128)(2,1)S(1)} %get-tuple-element.87.refs_0_.refs_4_), channel_id=1, source_target_pairs={{0,1},{1,0},{2,3},{3,2},{4,5},{5,4},{6,7},{7,6},{8,9},{9,8},{10,11... | collective-permute-start | bytes 1966088 | tf_op jit(solution)/shard_map/ppermute | solution.py:27
  31.2 8.8 %collective-permute-start.10 = (bf16[1280,256]{1,0:T(8,128)(2,1)S(1)}, bf16[1280,256]{1,0:T(8,128)(2,1)}, u32[]{:S(2)}, u32[]{:S(2)}) collective-permute-start(bf16[1280,256]{1,0:T(8,128)(2,1)S(1)} %collective-permute-done.9.refs_2_.refs_6_), channel_id=1, source_target_pairs={{0,1},{1,0},{2,3},{3,2},{4,5},{5,4},{6,7},{7,6},{8,9},{9,8},{10,11... | collective-permute-start | bytes 1966088 | tf_op jit(solution)/shard_map/ppermute | solution.py:27
  31.2 14.2 %all-to-all-start.1 = ((bf16[8,32,512]{2,1,0:T(8,128)(2,1)}), bf16[8,32,512]{2,1,0:T(8,128)(2,1)S(1)}, u32[]{:S(2)}, u32[]{:S(2)}) async-start(bf16[8,32,512]{2,1,0:T(8,128)(2,1)} %sum.1), calls=%async_computation.1 | async-start | bytes 524288 | tf_op jit(solution)/shard_map/all_to_all | solution.py:22
  38.5 8.8 %collective-permute-start.7 = (bf16[256,256]{1,0:T(8,128)(2,1)}, bf16[256,256]{1,0:T(8,128)(2,1)S(1)}, u32[]{:S(2)}, u32[]{:S(2)}) collective-permute-start(bf16[256,256]{1,0:T(8,128)(2,1)} %convert_element_type.26), channel_id=1, source_target_pairs={{0,0},{16,4},{4,8},{20,12},{8,16},{24,20},{12,24},{28,28},{1,1},{1... | collective-permute-start | bytes 393224 | tf_op jit(solution)/shard_map/ppermute | solution.py:659
  53.2 26.8 %collective-permute-start.17 = (bf16[256,1024]{1,0:T(8,128)(2,1)S(1)}, bf16[256,1024]{1,0:T(8,128)(2,1)S(1)}, u32[]{:S(2)}, u32[]{:S(2)}) collective-permute-start(bf16[256,1024]{1,0:T(8,128)(2,1)S(1)} %get-tuple-element.94.refs_1_.refs_8_), channel_id=1, source_target_pairs={{0,1},{1,0},{2,3},{3,2},{4,5},{5,4},{6,7},{7,6},{8,9},{9,8},{10,11... | collective-permute-start | bytes 1572872 | tf_op jit(solution)/shard_map/ppermute | solution.py:27
  53.2 26.8 %collective-permute-start.18 = (bf16[256,1024]{1,0:T(8,128)(2,1)S(1)}, bf16[256,1024]{1,0:T(8,128)(2,1)S(1)}, u32[]{:S(2)}, u32[]{:S(2)}) collective-permute-start(bf16[256,1024]{1,0:T(8,128)(2,1)S(1)} %get-tuple-element.94.refs_1_.refs_8_), channel_id=1, source_target_pairs={{0,2},{1,3},{2,0},{3,1},{4,6},{5,7},{6,4},{7,5},{8,10},{9,11},{10,... | collective-permute-start | bytes 1572872 | tf_op jit(solution)/shard_map/ppermute | solution.py:27
  54.0 26.0 %collective-permute-start.19 = (bf16[256,1024]{1,0:T(8,128)(2,1)S(1)}, bf16[256,1024]{1,0:T(8,128)(2,1)}, u32[]{:S(2)}, u32[]{:S(2)}) collective-permute-start(bf16[256,1024]{1,0:T(8,128)(2,1)S(1)} %get-tuple-element.94.refs_1_.refs_8_), channel_id=1, source_target_pairs={{0,3},{1,2},{2,1},{3,0},{4,7},{5,6},{6,5},{7,4},{8,11},{9,10},{10,... | collective-permute-start | bytes 1572872 | tf_op jit(solution)/shard_map/ppermute | solution.py:27
  56.6 9.3 %collective-permute-start.13 = (bf16[2,256,256]{2,1,0:T(8,128)(2,1)}, bf16[2,256,256]{2,1,0:T(8,128)(2,1)S(1)}, u32[]{:S(2)}, u32[]{:S(2)}) collective-permute-start(bf16[2,256,256]{2,1,0:T(8,128)(2,1)} %dynamic-slice_bitcast_fusion), channel_id=1, source_target_pairs={{0,8},{4,12},{8,0},{12,4},{16,24},{20,28},{24,16},{28,20},{1,9},{5... | collective-permute-start | bytes 786440 | tf_op jit(solution)/shard_map/ppermute | solution.py:27
  58.6 16.3 %all-to-all-start.2 = ((bf16[8,32,384]{2,1,0:T(8,128)(2,1)}), bf16[8,32,384]{2,1,0:T(8,128)(2,1)}, u32[]{:S(2)}, u32[]{:S(2)}) async-start(bf16[8,32,384]{2,1,0:T(8,128)(2,1)} %bitcast.32), calls=%async_computation.2 | async-start | bytes 393216 | tf_op jit(solution)/shard_map/all_to_all | solution.py:22
  63.0 23.9 %collective-permute-start.14 = (bf16[1,256,256]{2,1,0:T(8,128)(2,1)S(1)}, bf16[1,256,256]{2,1,0:T(8,128)(2,1)S(1)}, u32[]{:S(2)}, u32[]{:S(2)}) collective-permute-start(bf16[1,256,256]{2,1,0:T(8,128)(2,1)S(1)} %bitcast.30), channel_id=1, source_target_pairs={{0,16},{4,20},{8,24},{12,28},{16,0},{20,4},{24,8},{28,12},{1,17},{... | collective-permute-start | bytes 393224 | tf_op jit(solution)/shard_map/ppermute | solution.py:27
  76.6 15.9 %all-to-all-start.3 = ((bf16[8,32,384]{2,1,0:T(8,128)(2,1)}), bf16[8,32,384]{2,1,0:T(8,128)(2,1)S(1)}, u32[]{:S(2)}, u32[]{:S(2)}) async-start(bf16[8,32,384]{2,1,0:T(8,128)(2,1)} %sum_z.1.refs_5_), calls=%async_computation.3 | async-start | bytes 393216 | tf_op jit(solution)/shard_map/all_to_all | solution.py:22
  81.9 8.7 %collective-permute-start.20 = (bf16[512,256]{1,0:T(8,128)(2,1)S(1)}, bf16[512,256]{1,0:T(8,128)(2,1)S(1)}, u32[]{:S(2)}, u32[]{:S(2)}) collective-permute-start(bf16[512,256]{1,0:T(8,128)(2,1)S(1)} %get-tuple-element.96), channel_id=1, source_target_pairs={{0,4},{4,0},{8,12},{12,8},{16,20},{20,16},{24,28},{28,24},{1,5},{5... | collective-permute-start | bytes 786440 | tf_op jit(solution)/shard_map/ppermute | solution.py:27
  84.5 9.1 %collective-permute-start.27 = (bf16[1,256,256]{2,1,0:T(8,128)(2,1)}, bf16[1,256,256]{2,1,0:T(8,128)(2,1)}, u32[]{:S(2)}, u32[]{:S(2)}) collective-permute-start(bf16[1,256,256]{2,1,0:T(8,128)(2,1)} %constant_dynamic-slice_fusion), channel_id=1, source_target_pairs={{0,16},{4,20},{8,24},{12,28},{16,0},{20,4},{24,8},{28,12},{1,17},{... | collective-permute-start | bytes 393224 | tf_op jit(solution)/shard_map/ppermute | solution.py:27
  86.9 14.7 %collective-permute-start.16 = (bf16[2,64,1024]{2,1,0:T(8,128)(2,1)}, bf16[2,64,1024]{2,1,0:T(8,128)(2,1)}, u32[]{:S(2)}, u32[]{:S(2)}) collective-permute-start(bf16[2,64,1024]{2,1,0:T(8,128)(2,1)} %get-tuple-element.92), channel_id=1, source_target_pairs={{0,1},{1,0},{2,3},{3,2},{4,5},{5,4},{6,7},{7,6},{8,9},{9,8},{10,11... | collective-permute-start | bytes 786440 | tf_op jit(solution)/shard_map/ppermute | solution.py:27
  86.9 24.6 %collective-permute-start.15 = (bf16[2,256,256]{2,1,0:T(8,128)(2,1)S(1)}, bf16[2,256,256]{2,1,0:T(8,128)(2,1)S(1)}, u32[]{:S(2)}, u32[]{:S(2)}) collective-permute-start(bf16[2,256,256]{2,1,0:T(8,128)(2,1)S(1)} %constant_dynamic-update-slice_fusion.4.refs_4_), channel_id=1, source_target_pairs={{0,8},{4,12},{8,0},{12,4},{16,24},{20,28},{24,16},{28,20},{1,9},{5... | collective-permute-start | bytes 786440 | tf_op jit(solution)/shard_map/ppermute | solution.py:27
  91.3 8.8 %collective-permute-start.21 = (bf16[256,256]{1,0:T(8,128)(2,1)}, bf16[256,256]{1,0:T(8,128)(2,1)}, u32[]{:S(2)}, u32[]{:S(2)}) collective-permute-start(bf16[256,256]{1,0:T(8,128)(2,1)} %get-tuple-element.98.refs_3_), channel_id=1, source_target_pairs={{0,8},{4,12},{8,0},{12,4},{16,24},{20,28},{24,16},{28,20},{1,9},{5... | collective-permute-start | bytes 393224 | tf_op jit(solution)/shard_map/ppermute | solution.py:27
  94.6 10.1 %collective-permute-start.28 = (bf16[256,256]{1,0:T(8,128)(2,1)S(1)}, bf16[256,256]{1,0:T(8,128)(2,1)S(1)}, u32[]{:S(2)}, u32[]{:S(2)}) collective-permute-start(bf16[256,256]{1,0:T(8,128)(2,1)S(1)} %fusion.1), channel_id=1, source_target_pairs={{0,0},{4,16},{8,4},{12,20},{16,8},{20,24},{24,12},{28,28},{1,1},{5... | collective-permute-start | bytes 393224 | tf_op jit(solution)/shard_map/ppermute | solution.py:734
  104.7 10.3 %collective-permute-start.23 = (bf16[112,256]{1,0:T(8,128)(2,1)}, bf16[112,256]{1,0:T(8,128)(2,1)}, u32[]{:S(2)}, u32[]{:S(2)}) collective-permute-start(bf16[112,256]{1,0:T(8,128)(2,1)} %get-tuple-element.106), channel_id=1, source_target_pairs={{0,1},{1,0},{2,3},{3,2},{4,5},{5,4},{6,7},{7,6},{8,9},{9,8},{10,11... | collective-permute-start | bytes 172040 | tf_op jit(solution)/shard_map/ppermute | solution.py:27
  104.7 10.3 %collective-permute-start.24 = (bf16[112,256]{1,0:T(8,128)(2,1)}, bf16[112,256]{1,0:T(8,128)(2,1)}, u32[]{:S(2)}, u32[]{:S(2)}) collective-permute-start(bf16[112,256]{1,0:T(8,128)(2,1)} %get-tuple-element.107), channel_id=1, source_target_pairs={{0,2},{1,3},{2,0},{3,1},{4,6},{5,7},{6,4},{7,5},{8,10},{9,11},{10,... | collective-permute-start | bytes 172040 | tf_op jit(solution)/shard_map/ppermute | solution.py:27
  (32 other events, 118.0 us)

commit v5 on v4

--- a/solution.py
+++ b/solution.py
@@ -334,15 +334,8 @@
         send_ref[i] = (keep_ref[2 * i + 1].astype(F32) + got_ref[2 * i + 1].astype(F32)).astype(BF16)
 
 
-def mixed_kernel(vl, n_j, length_ref, lead_ref, w_ref, vk_ref, plo_ref, phi_ref, pk_ref, pg_ref, *refs):
-    atts, (out_ref, px_ref, pos_ref, s_ref, x_ref) = refs[:n_j], refs[n_j:]
-    s_ref[...] = pk_ref[0].astype(F32) + pg_ref[0].astype(F32)
-    vp = s_ref.shape[0] // 4
-    for v in range(vl):
-        for p in range(4):
-            x_ref[4 * v + p : 4 * v + p + 1, :] = s_ref[p * vp + v : p * vp + v + 1, :]
-    for v in range(vl):
-        px_ref[v] = x_ref[4 * v : 4 * v + 4, :].astype(BF16)
+def mixed_kernel(vl, n_j, length_ref, lead_ref, w_ref, vk_ref, plo_ref, phi_ref, *refs):
+    atts, (out_ref, pos_ref) = refs[:n_j], refs[n_j:]
     rows, cw = out_ref.shape
     spare = 5 * vl
     base = pad16(spare) - 16
@@ -494,8 +487,15 @@
     return out
 
 
-def final_kernel(eb, vl, rl, dp, n_j, wq_ref, q_ref, *refs):
-    chunks, (gwv_ref, gwk_ref, gwq_ref, gq_ref, ge_ref, gb_ref, gl_ref, f_ref, r_ref) = refs[:n_j], refs[n_j:]
+def final_kernel(eb, vl, rl, dp, n_j, wq_ref, q_ref, pk_ref, pg_ref, *refs):
+    chunks, (gwv_ref, gwk_ref, gwq_ref, gq_ref, ge_ref, gb_ref, gl_ref, px_ref, f_ref, r_ref, s_ref, x_ref) = refs[:n_j], refs[n_j:]
+    s_ref[...] = pk_ref[0].astype(F32) + pg_ref[0].astype(F32)
+    vp = s_ref.shape[0] // 4
+    for v in range(vl):
+        for p in range(4):
+            x_ref[4 * v + p : 4 * v + p + 1, :] = s_ref[p * vp + v : p * vp + v + 1, :]
+    for v in range(vl):
+        px_ref[v] = x_ref[4 * v : 4 * v + 4, :].astype(BF16)
     cw = chunks[0].shape[1]
     half = eb // 2
     j = lax.axis_index("var")
@@ -698,6 +698,7 @@
         [shape((size * dp, cw), BF16), shape((size, dp, cw), BF16)],
         (g_keep, flip(send, "patch", step)),
     )
+    first = send
     bit = n_p // 2
     while bit > parts:
         bit //= 2
@@ -715,7 +716,7 @@
         [shape((fh, cw), BF16)] * n_j,
         (zs, vk, ekv),
         [pltpu.VMEM((dp, 2 * cw), F32), pltpu.VMEM((nr, dp), F32), pltpu.VMEM((fh, cw), F32)],
-        after=(send,),
+        after=(),
     )
 
     def late(x):
@@ -731,7 +732,7 @@
             (g_keep, flip(send, "patch", step)),
             after=(last[0],),
         )
-    grad_pos = lax.ppermute(joined(g_rows[0], late(g_rows[1])).reshape(per, cw), "patch", back)
+    grad_pos = lax.ppermute(joined(g_rows[0], gate(g_rows[1], first)).reshape(per, cw), "patch", back)
     grad_w_out, grad_pos = call(
         functools.partial(halve_kernel, 2 * step),
         "halve",
@@ -747,21 +748,21 @@
             "pixel_add",
             [shape((n_j // (2 * bit), 4 * vp, rows), BF16)] * 2,
             (px_keep, px_got),
-            after=(send,),
+            after=(first,),
         )
         px_got = flip(px_send, "var", bit)
-    mixed, grad_pixels = call(
+    mixed = call(
         functools.partial(mixed_kernel, vl, n_j),
         "mixed",
-        (shape((rows, cw), BF16), shape((vl, 4, rows), BF16)),
-        (lengths, lead_hours, wo, vk, pos_lo, pos_hi, px_keep, px_got, *atts),
-        [pltpu.VMEM((owners, per, cw), BF16), pltpu.VMEM((4 * vp, rows), F32), pltpu.VMEM((4 * vl, rows), F32)],
+        shape((rows, cw), BF16),
+        (lengths, lead_hours, wo, vk, pos_lo, pos_hi, *atts),
+        [pltpu.VMEM((owners, per, cw), BF16)],
         smem=2,
-        after=(send,),
+        after=(first,),
     )
 
     last = [last[0]] + [flip(last[k], "var", k) for k in others]
-    gwv, gwk, gwq, gq, ge, gb, gl = call(
+    gwv, gwk, gwq, gq, ge, gb, gl, grad_pixels = call(
         functools.partial(final_kernel, eb, vl, rl, dp, n_j),
         "final",
         (
@@ -772,10 +773,11 @@
             shape((5, vl, dp)),
             shape((1, rl)),
             shape((1, rl)),
+            shape((vl, 4, rows), BF16),
         ),
-        (w_query, query[:, None], *last),
-        [pltpu.VMEM((eb, dp), F32), pltpu.VMEM((8, D), F32)],
-        after=(mixed,),
+        (w_query, query[:, None], px_keep, px_got, *last),
+        [pltpu.VMEM((eb, dp), F32), pltpu.VMEM((8, D), F32), pltpu.VMEM((4 * vp, rows), F32), pltpu.VMEM((4 * vl, rows), F32)],
+        after=(send,),
     )
     return (
         mixed,

time: 119 us -> 112 us (0.941)
  waiting for transfers between devices: 30.6 us -> 24 us
  starting transfers between devices: 47.8 us -> 51.4 us
  local copies, waits for them, and re-layouts: 7.12 us -> 4.41 us
    ppermute x27, waiting for transfers between devices: 22.6 us -> 16 us  [flip(): return lax.ppermute(x, axis, [(i, i ^ bit) for i in range(n)])]
    ppermute x27, starting transfers between devices: 29.6 us -> 31.7 us  [flip(): return lax.ppermute(x, axis, [(i, i ^ bit) for i in range(n)])]
    unnamed x49 -> x47, local copies, waits for them, and re-layouts: 5.57 us -> 3.53 us
    ppermute x1, starting transfers between devices: 0.67 us -> 2.15 us  [shards(): lax.ppermute(joined(g_rows[0], gate(g_rows[1], first)).reshape(per, cw),...]
  transfers between devices with their start and end apart: 33 -> 33, of which waited for: 8 -> 8; matrix products, arithmetic and copies ran while one was open for 4% -> 4% of each run, Pallas kernels for 15% -> 16%
where the time goes in v5:
time: 112 us; the launch traced here: 111 us
  starting transfers between devices  51.4 us (46%)
  Pallas kernels  27 us (24%)
  waiting for transfers between devices  24 us (21%)
  local copies, waits for them, and re-layouts  4.41 us (4%)
  other arithmetic  3.09 us (3%)
    ppermute x27, starting transfers between devices, flip(): return lax.ppermute(x, axis, [(i, i ^ bit) for i in range(n)])  31.7 us
    pallas_call x18, Pallas kernels, call(): pl.pallas_call(body, out_shape=shapes, in_specs=specs, out_specs=outs, sc...  27 us
    ppermute x27, waiting for transfers between devices, flip(): return lax.ppermute(x, axis, [(i, i ^ bit) for i in range(n)])  16 us
    all_to_all x4, starting transfers between devices, exchange(): return lax.all_to_all(x, axis, 0, 0, tiled=True)  16 us
    all_to_all x4, waiting for transfers between devices, exchange(): return lax.all_to_all(x, axis, 0, 0, tiled=True)  7.99 us
    unnamed x47, local copies, waits for them, and re-layouts  3.53 us
  transfers between devices with their start and end apart: 33, of which 8 were waited for; matrix products, arithmetic and copies ran while one was open for 4% of the time, Pallas kernels for 16%

profile of v5, /device:TPU:0, one launch (start us, length us, event | category | flops | bytes accessed | tf_op | source)
XLA Modules:
  0.0 110.9 jit_solution(1868961183867186655)
XLA Ops:
  0.7 2.1 %pack.1 = (bf16[128,256]{1,0:T(8,128)(2,1)}, bf16[128,256]{1,0:T(8,128)(2,1)}, bf16[128,256]{1,0:T(8,128)(2,1)}, bf16[128,256]{1,0:T(8,128)(2,1)}, bf16[1,128,256]{2,1,0:T(8,128)(2,1)}) custom-call(f32[32,1024]{1,0:T(8,128)} %refs_0_.4, f32[32,1024]{1,0:T(8,128)} %refs_1_.3, f32[32,1024]{1,0:T(8,128)} %refs_0_.7, f32[1,32]{1,0:T(1,128)} %bitcast.36, ...), custom_call_target="tpu_custom_call" | custom-call | flops 11530000 | bytes 65536 | tf_op jit(solution)/shard_map/pack/pallas_call | solution.py:562
  2.7 2.4 %collective-permute-start = (bf16[128,256]{1,0:T(8,128)(2,1)}, bf16[128,256]{1,0:T(8,128)(2,1)S(1)}, u32[]{:S(2)}, u32[]{:S(2)}) collective-permute-start(bf16[128,256]{1,0:T(8,128)(2,1)} %get-tuple-element.66), channel_id=1, source_target_pairs={{0,3},{1,2},{2,1},{3,0},{4,7},{5,6},{6,5},{7,4},{8,11},{9,10},{10,... | collective-permute-start | bytes 196616 | tf_op jit(solution)/shard_map/ppermute | solution.py:27
  5.8 3.1 %collective-permute-start.1 = (bf16[1,128,256]{2,1,0:T(8,128)(2,1)}, bf16[1,128,256]{2,1,0:T(8,128)(2,1)S(1)}, u32[]{:S(2)}, u32[]{:S(2)}) collective-permute-start(bf16[1,128,256]{2,1,0:T(8,128)(2,1)} %get-tuple-element.67), channel_id=1, source_target_pairs={{0,16},{4,20},{8,24},{12,28},{16,0},{20,4},{24,8},{28,12},{1,17},{... | collective-permute-start | bytes 196616 | tf_op jit(solution)/shard_map/ppermute | solution.py:27
  15.8 3.4 %all-to-all-start = ((bf16[8,32,512]{2,1,0:T(8,128)(2,1)}), bf16[8,32,512]{2,1,0:T(8,128)(2,1)S(1)}, u32[]{:S(2)}, u32[]{:S(2)}) async-start(bf16[8,32,512]{2,1,0:T(8,128)(2,1)} %bitcast.4), calls=%async_computation | async-start | bytes 524288 | tf_op jit(solution)/shard_map/all_to_all | solution.py:22
  19.3 2.0 %collective-permute-start.3 = (bf16[4,128,256]{2,1,0:T(8,128)(2,1)S(1)}, bf16[4,128,256]{2,1,0:T(8,128)(2,1)S(1)}, u32[]{:S(2)}, u32[]{:S(2)}) collective-permute-start(bf16[4,128,256]{2,1,0:T(8,128)(2,1)S(1)} %constant_dynamic-update-slice_fusion.2.refs_0_), channel_id=1, source_target_pairs={{0,4},{4,0},{8,12},{12,8},{16,20},{20,16},{24,28},{28,24},{1,5},{5... | collective-permute-start | bytes 786440 | tf_op jit(solution)/shard_map/ppermute | solution.py:27
  21.3 8.4 %collective-permute-done.3.refs_1_ = bf16[4,128,256]{2,1,0:T(8,128)(2,1)S(1)} collective-permute-done((bf16[4,128,256]{2,1,0:T(8,128)(2,1)S(1)}, bf16[4,128,256]{2,1,0:T(8,128)(2,1)S(1)}, u32[]{:S(2)}, u32[]{:S(2)}) %collective-permute-start.3) | collective-permute-done | bytes 262176 | tf_op jit(solution)/shard_map/ppermute | solution.py:27
  31.2 4.7 %all-to-all-start.1 = ((bf16[8,32,512]{2,1,0:T(8,128)(2,1)}), bf16[8,32,512]{2,1,0:T(8,128)(2,1)S(1)}, u32[]{:S(2)}, u32[]{:S(2)}) async-start(bf16[8,32,512]{2,1,0:T(8,128)(2,1)} %sum.1), calls=%async_computation.1 | async-start | bytes 524288 | tf_op jit(solution)/shard_map/all_to_all | solution.py:22
  42.6 2.0 %collective-permute-done.12.refs_3_ = bf16[256,256]{1,0:T(8,128)(2,1)} collective-permute-done((bf16[256,256]{1,0:T(8,128)(2,1)}, bf16[256,256]{1,0:T(8,128)(2,1)}, u32[]{:S(2)}, u32[]{:S(2)}) %collective-permute-start.12) | collective-permute-done | bytes 131104 | tf_op jit(solution)/shard_map/ppermute | solution.py:27
  45.4 1.9 %grad_att.1.refs_3_.refs_4_ = bf16[256,1024]{1,0:T(8,128)(2,1)S(1)} custom-call(bf16[1024,256]{1,0:T(8,128)(2,1)S(1)} %get-tuple-element.69.refs_1_.refs_0_.refs_2_, bf16[256,256]{1,0:T(8,128)(2,1)S(1)} %collective-permute-done.6.refs_1_, bf16[256,256]{1,0:T(8,128)(2,1)S(1)} %collective-permute-done.11.refs_2_, ...), custom_call_target="tpu_custom_call" | custom-call | flops 11530000 | bytes 65536 | tf_op jit(solution)/shard_map/grad_att/pallas_call | solution.py:562
  47.3 2.8 %attention_forward.1 = (bf16[256,1024]{1,0:T(8,128)(2,1)S(1)}, f32[4,48,1024]{2,1,0:T(8,128)S(1)}, f32[5,48,4]{2,1,0:T(8,128)S(1)}, bf16[240,256]{1,0:T(8,128)(2,1)S(1)}) custom-call(bf16[256,512]{1,0:T(8,128)(2,1)S(1)} %bitcast.25, bf16[4,48,1024]{2,1,0:T(8,128)(2,1)S(1)} %pixels.1.refs_1_.refs_0_, s32[4,48]{1,0:T(4,128)S(1)} %copy-done.13, ...), custom_call_target="tpu_custom_call" | custom-call | flops 11530000 | bytes 65536 | tf_op jit(solution)/shard_map/attention_forward/pallas_call | solution.py:562
  50.1 2.9 %attention_backward.1 = (bf16[2,64,1024]{2,1,0:T(8,128)(2,1)S(1)}, bf16[2,64,1024]{2,1,0:T(8,128)(2,1)S(1)}, bf16[256,384]{1,0:T(8,128)(2,1)S(1)}) custom-call(bf16[4,48,1024]{2,1,0:T(8,128)(2,1)S(1)} %pixels.1.refs_1_.refs_0_, f32[5,48,4]{2,1,0:T(8,128)S(1)} %get-tuple-element.82.refs_1_, bf16[240,256]{1,0:T(8,128)(2,1)S(1)} %get-tuple-element.83.refs_2_, ...), custom_call_target="tpu_custom_call" | custom-call | flops 11530000 | bytes 65536 | tf_op jit(solution)/shard_map/attention_backward/pallas_call | solution.py:562
  56.5 1.9 %collective-permute-start.13 = (bf16[2,256,256]{2,1,0:T(8,128)(2,1)}, bf16[2,256,256]{2,1,0:T(8,128)(2,1)S(1)}, u32[]{:S(2)}, u32[]{:S(2)}) collective-permute-start(bf16[2,256,256]{2,1,0:T(8,128)(2,1)} %dynamic-slice_bitcast_fusion), channel_id=1, source_target_pairs={{0,8},{4,12},{8,0},{12,4},{16,24},{20,28},{24,16},{28,20},{1,9},{5... | collective-permute-start | bytes 786440 | tf_op jit(solution)/shard_map/ppermute | solution.py:27
  58.5 4.5 %all-to-all-start.2 = ((bf16[8,32,384]{2,1,0:T(8,128)(2,1)}), bf16[8,32,384]{2,1,0:T(8,128)(2,1)}, u32[]{:S(2)}, u32[]{:S(2)}) async-start(bf16[8,32,384]{2,1,0:T(8,128)(2,1)} %bitcast.32), calls=%async_computation.2 | async-start | bytes 393216 | tf_op jit(solution)/shard_map/all_to_all | solution.py:22
  62.9 2.9 %collective-permute-start.14 = (bf16[1,256,256]{2,1,0:T(8,128)(2,1)S(1)}, bf16[1,256,256]{2,1,0:T(8,128)(2,1)S(1)}, u32[]{:S(2)}, u32[]{:S(2)}) collective-permute-start(bf16[1,256,256]{2,1,0:T(8,128)(2,1)S(1)} %bitcast.30), channel_id=1, source_target_pairs={{0,16},{4,20},{8,24},{12,28},{16,0},{20,4},{24,8},{28,12},{1,17},{... | collective-permute-start | bytes 393224 | tf_op jit(solution)/shard_map/ppermute | solution.py:27
  67.6 7.1 %all-to-all-done.2.refs_0_ = bf16[8,32,384]{2,1,0:T(8,128)(2,1)} async-done(((bf16[8,32,384]{2,1,0:T(8,128)(2,1)}), bf16[8,32,384]{2,1,0:T(8,128)(2,1)}, u32[]{:S(2)}, u32[]{:S(2)}) %all-to-all-start.2) | async-done | bytes 196640 | tf_op jit(solution)/shard_map/all_to_all | solution.py:22
  76.5 3.4 %all-to-all-start.3 = ((bf16[8,32,384]{2,1,0:T(8,128)(2,1)}), bf16[8,32,384]{2,1,0:T(8,128)(2,1)S(1)}, u32[]{:S(2)}, u32[]{:S(2)}) async-start(bf16[8,32,384]{2,1,0:T(8,128)(2,1)} %sum_z.1.refs_5_), calls=%async_computation.3 | async-start | bytes 393216 | tf_op jit(solution)/shard_map/all_to_all | solution.py:22
  80.0 1.8 %weight_grad.1 = (bf16[512,256]{1,0:T(8,128)(2,1)S(1)}, bf16[4,128,256]{2,1,0:T(8,128)(2,1)S(1)}) custom-call(bf16[1280,256]{1,0:T(8,128)(2,1)S(1)} %get-tuple-element.86.refs_0_.refs_4_, bf16[256,1024]{1,0:T(8,128)(2,1)S(1)} %get-tuple-element.90.refs_1_.refs_6_, bf16[256,1024]{1,0:T(8,128)(2,1)S(1)} %collective-permute-done.16.refs_2_.refs_7_, ...), custom_call_target="tpu_custom_call" | custom-call | flops 11530000 | bytes 65536 | tf_op jit(solution)/shard_map/weight_grad/pallas_call | solution.py:562
  81.8 2.0 %collective-permute-start.19 = (bf16[512,256]{1,0:T(8,128)(2,1)S(1)}, bf16[512,256]{1,0:T(8,128)(2,1)S(1)}, u32[]{:S(2)}, u32[]{:S(2)}) collective-permute-start(bf16[512,256]{1,0:T(8,128)(2,1)S(1)} %get-tuple-element.92), channel_id=1, source_target_pairs={{0,4},{4,0},{8,12},{12,8},{16,20},{20,16},{24,28},{28,24},{1,5},{5... | collective-permute-start | bytes 786440 | tf_op jit(solution)/shard_map/ppermute | solution.py:27
  83.8 2.4 %collective-permute-start.27 = (bf16[1,256,256]{2,1,0:T(8,128)(2,1)S(1)}, bf16[1,256,256]{2,1,0:T(8,128)(2,1)S(1)}, u32[]{:S(2)}, u32[]{:S(2)}) collective-permute-start(bf16[1,256,256]{2,1,0:T(8,128)(2,1)S(1)} %constant_dynamic-slice_fusion), channel_id=1, source_target_pairs={{0,16},{4,20},{8,24},{12,28},{16,0},{20,4},{24,8},{28,12},{1,17},{... | collective-permute-start | bytes 393224 | tf_op jit(solution)/shard_map/ppermute | solution.py:27
  87.8 3.4 %collective-permute-done.19.refs_1_ = bf16[512,256]{1,0:T(8,128)(2,1)S(1)} collective-permute-done((bf16[512,256]{1,0:T(8,128)(2,1)S(1)}, bf16[512,256]{1,0:T(8,128)(2,1)S(1)}, u32[]{:S(2)}, u32[]{:S(2)}) %collective-permute-start.19) | collective-permute-done | bytes 262176 | tf_op jit(solution)/shard_map/ppermute | solution.py:27
  95.7 2.1 %collective-permute-start.28 = (bf16[256,256]{1,0:T(8,128)(2,1)}, bf16[256,256]{1,0:T(8,128)(2,1)}, u32[]{:S(2)}, u32[]{:S(2)}) collective-permute-start(bf16[256,256]{1,0:T(8,128)(2,1)} %fusion.1), channel_id=1, source_target_pairs={{0,0},{4,16},{8,4},{12,20},{16,8},{20,24},{24,12},{28,28},{1,1},{5... | collective-permute-start | bytes 393224 | tf_op jit(solution)/shard_map/ppermute | solution.py:735
  100.1 1.8 %collective-permute-start.26 = (bf16[128,256]{1,0:T(8,128)(2,1)S(1)}, bf16[128,256]{1,0:T(8,128)(2,1)S(1)}, u32[]{:S(2)}, u32[]{:S(2)}) collective-permute-start(bf16[128,256]{1,0:T(8,128)(2,1)S(1)} %get-tuple-element.105.refs_8_), channel_id=1, source_target_pairs={{0,16},{4,20},{8,24},{12,28},{16,0},{20,4},{24,8},{28,12},{1,17},{... | collective-permute-start | bytes 196616 | tf_op jit(solution)/shard_map/ppermute | solution.py:27
  103.9 2.8 %mixed.1 = bf16[1024,256]{1,0:T(8,128)(2,1)} custom-call(s32[4]{0:T(128)S(1)} %copy-done.14, s32[4]{0:T(128)S(1)} %copy-done.15, bf16[1024,256]{1,0:T(8,128)(2,1)S(1)} %get-tuple-element.69.refs_1_.refs_0_.refs_2_, bf16[256,512]{1,0:T(8,128)(2,1)S(1)} %bitcast.27, bf16[2,256,256]{2,1,0:T(8,128)(2,1)S(1)} %constant_dynamic-update-slice_fusion.4.refs_4_, ...), custom_call_target="tpu_custom_call" | custom-call | flops 11530000 | bytes 65536 | tf_op jit(solution)/shard_map/mixed/pallas_call | solution.py:562
  107.4 1.8 %final.1 = (f32[32,1024]{1,0:T(8,128)}, f32[32,1024]{1,0:T(8,128)}, f32[32,1024]{1,0:T(8,128)}, f32[1,32]{1,0:T(1,128)}, f32[5,12,128]{2,1,0:T(8,128)}, /*index=...) custom-call(f32[32,1024]{1,0:T(8,128)S(1)} %copy-done.1, f32[32,1]{1,0:T(8,128)S(1)} %copy.26.refs_1_, ...), custom_call_target="tpu_custom_call" | custom-call | flops 11530000 | bytes 65536 | tf_op jit(solution)/shard_map/final/pallas_call | solution.py:562
  (117 shorter events, 36.3 us)
Async XLA Ops:
  2.7 8.9 %collective-permute-start = (bf16[128,256]{1,0:T(8,128)(2,1)}, bf16[128,256]{1,0:T(8,128)(2,1)S(1)}, u32[]{:S(2)}, u32[]{:S(2)}) collective-permute-start(bf16[128,256]{1,0:T(8,128)(2,1)} %get-tuple-element.66), channel_id=1, source_target_pairs={{0,3},{1,2},{2,1},{3,0},{4,7},{5,6},{6,5},{7,4},{8,11},{9,10},{10,... | collective-permute-start | bytes 196616 | tf_op jit(solution)/shard_map/ppermute | solution.py:27
  5.8 8.3 %collective-permute-start.1 = (bf16[1,128,256]{2,1,0:T(8,128)(2,1)}, bf16[1,128,256]{2,1,0:T(8,128)(2,1)S(1)}, u32[]{:S(2)}, u32[]{:S(2)}) collective-permute-start(bf16[1,128,256]{2,1,0:T(8,128)(2,1)} %get-tuple-element.67), channel_id=1, source_target_pairs={{0,16},{4,20},{8,24},{12,28},{16,0},{20,4},{24,8},{28,12},{1,17},{... | collective-permute-start | bytes 196616 | tf_op jit(solution)/shard_map/ppermute | solution.py:27
  12.6 18.6 %collective-permute-start.9 = (bf16[1280,256]{1,0:T(8,128)(2,1)S(1)}, bf16[1280,256]{1,0:T(8,128)(2,1)S(1)}, u32[]{:S(2)}, u32[]{:S(2)}) collective-permute-start(bf16[1280,256]{1,0:T(8,128)(2,1)S(1)} %get-tuple-element.86.refs_0_.refs_4_), channel_id=1, source_target_pairs={{0,2},{1,3},{2,0},{3,1},{4,6},{5,7},{6,4},{7,5},{8,10},{9,11},{10,... | collective-permute-start | bytes 1966088 | tf_op jit(solution)/shard_map/ppermute | solution.py:27
  15.8 14.7 %all-to-all-start = ((bf16[8,32,512]{2,1,0:T(8,128)(2,1)}), bf16[8,32,512]{2,1,0:T(8,128)(2,1)S(1)}, u32[]{:S(2)}, u32[]{:S(2)}) async-start(bf16[8,32,512]{2,1,0:T(8,128)(2,1)} %bitcast.4), calls=%async_computation | async-start | bytes 524288 | tf_op jit(solution)/shard_map/all_to_all | solution.py:22
  19.3 10.4 %collective-permute-start.3 = (bf16[4,128,256]{2,1,0:T(8,128)(2,1)S(1)}, bf16[4,128,256]{2,1,0:T(8,128)(2,1)S(1)}, u32[]{:S(2)}, u32[]{:S(2)}) collective-permute-start(bf16[4,128,256]{2,1,0:T(8,128)(2,1)S(1)} %constant_dynamic-update-slice_fusion.2.refs_0_), channel_id=1, source_target_pairs={{0,4},{4,0},{8,12},{12,8},{16,20},{20,16},{24,28},{28,24},{1,5},{5... | collective-permute-start | bytes 786440 | tf_op jit(solution)/shard_map/ppermute | solution.py:27
  21.3 18.8 %collective-permute-start.8 = (bf16[1280,256]{1,0:T(8,128)(2,1)S(1)}, bf16[1280,256]{1,0:T(8,128)(2,1)S(1)}, u32[]{:S(2)}, u32[]{:S(2)}) collective-permute-start(bf16[1280,256]{1,0:T(8,128)(2,1)S(1)} %get-tuple-element.86.refs_0_.refs_4_), channel_id=1, source_target_pairs={{0,1},{1,0},{2,3},{3,2},{4,5},{5,4},{6,7},{7,6},{8,9},{9,8},{10,11... | collective-permute-start | bytes 1966088 | tf_op jit(solution)/shard_map/ppermute | solution.py:27
  31.2 8.8 %collective-permute-start.10 = (bf16[1280,256]{1,0:T(8,128)(2,1)S(1)}, bf16[1280,256]{1,0:T(8,128)(2,1)}, u32[]{:S(2)}, u32[]{:S(2)}) collective-permute-start(bf16[1280,256]{1,0:T(8,128)(2,1)S(1)} %collective-permute-done.9.refs_2_.refs_6_), channel_id=1, source_target_pairs={{0,1},{1,0},{2,3},{3,2},{4,5},{5,4},{6,7},{7,6},{8,9},{9,8},{10,11... | collective-permute-start | bytes 1966088 | tf_op jit(solution)/shard_map/ppermute | solution.py:27
  31.2 14.2 %all-to-all-start.1 = ((bf16[8,32,512]{2,1,0:T(8,128)(2,1)}), bf16[8,32,512]{2,1,0:T(8,128)(2,1)S(1)}, u32[]{:S(2)}, u32[]{:S(2)}) async-start(bf16[8,32,512]{2,1,0:T(8,128)(2,1)} %sum.1), calls=%async_computation.1 | async-start | bytes 524288 | tf_op jit(solution)/shard_map/all_to_all | solution.py:22
  36.9 7.7 %collective-permute-start.12 = (bf16[256,256]{1,0:T(8,128)(2,1)}, bf16[256,256]{1,0:T(8,128)(2,1)}, u32[]{:S(2)}, u32[]{:S(2)}) collective-permute-start(bf16[256,256]{1,0:T(8,128)(2,1)} %get-tuple-element.81), channel_id=1, source_target_pairs={{0,3},{1,2},{2,1},{3,0},{4,7},{5,6},{6,5},{7,4},{8,11},{9,10},{10,... | collective-permute-start | bytes 393224 | tf_op jit(solution)/shard_map/ppermute | solution.py:27
  38.5 8.8 %collective-permute-start.7 = (bf16[256,256]{1,0:T(8,128)(2,1)}, bf16[256,256]{1,0:T(8,128)(2,1)S(1)}, u32[]{:S(2)}, u32[]{:S(2)}) collective-permute-start(bf16[256,256]{1,0:T(8,128)(2,1)} %convert_element_type.26), channel_id=1, source_target_pairs={{0,0},{16,4},{4,8},{20,12},{8,16},{24,20},{12,24},{28,28},{1,1},{1... | collective-permute-start | bytes 393224 | tf_op jit(solution)/shard_map/ppermute | solution.py:659
  53.0 27.0 %collective-permute-start.16 = (bf16[256,1024]{1,0:T(8,128)(2,1)S(1)}, bf16[256,1024]{1,0:T(8,128)(2,1)S(1)}, u32[]{:S(2)}, u32[]{:S(2)}) collective-permute-start(bf16[256,1024]{1,0:T(8,128)(2,1)S(1)} %get-tuple-element.90.refs_1_.refs_6_), channel_id=1, source_target_pairs={{0,1},{1,0},{2,3},{3,2},{4,5},{5,4},{6,7},{7,6},{8,9},{9,8},{10,11... | collective-permute-start | bytes 1572872 | tf_op jit(solution)/shard_map/ppermute | solution.py:27
  53.1 26.9 %collective-permute-start.17 = (bf16[256,1024]{1,0:T(8,128)(2,1)S(1)}, bf16[256,1024]{1,0:T(8,128)(2,1)S(1)}, u32[]{:S(2)}, u32[]{:S(2)}) collective-permute-start(bf16[256,1024]{1,0:T(8,128)(2,1)S(1)} %get-tuple-element.90.refs_1_.refs_6_), channel_id=1, source_target_pairs={{0,2},{1,3},{2,0},{3,1},{4,6},{5,7},{6,4},{7,5},{8,10},{9,11},{10,... | collective-permute-start | bytes 1572872 | tf_op jit(solution)/shard_map/ppermute | solution.py:27
  54.0 26.0 %collective-permute-start.18 = (bf16[256,1024]{1,0:T(8,128)(2,1)S(1)}, bf16[256,1024]{1,0:T(8,128)(2,1)}, u32[]{:S(2)}, u32[]{:S(2)}) collective-permute-start(bf16[256,1024]{1,0:T(8,128)(2,1)S(1)} %get-tuple-element.90.refs_1_.refs_6_), channel_id=1, source_target_pairs={{0,3},{1,2},{2,1},{3,0},{4,7},{5,6},{6,5},{7,4},{8,11},{9,10},{10,... | collective-permute-start | bytes 1572872 | tf_op jit(solution)/shard_map/ppermute | solution.py:27
  56.5 9.3 %collective-permute-start.13 = (bf16[2,256,256]{2,1,0:T(8,128)(2,1)}, bf16[2,256,256]{2,1,0:T(8,128)(2,1)S(1)}, u32[]{:S(2)}, u32[]{:S(2)}) collective-permute-start(bf16[2,256,256]{2,1,0:T(8,128)(2,1)} %dynamic-slice_bitcast_fusion), channel_id=1, source_target_pairs={{0,8},{4,12},{8,0},{12,4},{16,24},{20,28},{24,16},{28,20},{1,9},{5... | collective-permute-start | bytes 786440 | tf_op jit(solution)/shard_map/ppermute | solution.py:27
  58.5 16.3 %all-to-all-start.2 = ((bf16[8,32,384]{2,1,0:T(8,128)(2,1)}), bf16[8,32,384]{2,1,0:T(8,128)(2,1)}, u32[]{:S(2)}, u32[]{:S(2)}) async-start(bf16[8,32,384]{2,1,0:T(8,128)(2,1)} %bitcast.32), calls=%async_computation.2 | async-start | bytes 393216 | tf_op jit(solution)/shard_map/all_to_all | solution.py:22
  62.9 23.3 %collective-permute-start.14 = (bf16[1,256,256]{2,1,0:T(8,128)(2,1)S(1)}, bf16[1,256,256]{2,1,0:T(8,128)(2,1)S(1)}, u32[]{:S(2)}, u32[]{:S(2)}) collective-permute-start(bf16[1,256,256]{2,1,0:T(8,128)(2,1)S(1)} %bitcast.30), channel_id=1, source_target_pairs={{0,16},{4,20},{8,24},{12,28},{16,0},{20,4},{24,8},{28,12},{1,17},{... | collective-permute-start | bytes 393224 | tf_op jit(solution)/shard_map/ppermute | solution.py:27
  76.5 21.4 %all-to-all-start.3 = ((bf16[8,32,384]{2,1,0:T(8,128)(2,1)}), bf16[8,32,384]{2,1,0:T(8,128)(2,1)S(1)}, u32[]{:S(2)}, u32[]{:S(2)}) async-start(bf16[8,32,384]{2,1,0:T(8,128)(2,1)} %sum_z.1.refs_5_), calls=%async_computation.3 | async-start | bytes 393216 | tf_op jit(solution)/shard_map/all_to_all | solution.py:22
  79.9 13.6 %collective-permute-start.20 = (bf16[2,64,1024]{2,1,0:T(8,128)(2,1)}, bf16[2,64,1024]{2,1,0:T(8,128)(2,1)S(1)}, u32[]{:S(2)}, u32[]{:S(2)}) collective-permute-start(bf16[2,64,1024]{2,1,0:T(8,128)(2,1)} %copy-done.16), channel_id=1, source_target_pairs={{0,1},{1,0},{2,3},{3,2},{4,5},{5,4},{6,7},{7,6},{8,9},{9,8},{10,11... | collective-permute-start | bytes 786440 | tf_op jit(solution)/shard_map/ppermute | solution.py:27
  81.8 9.4 %collective-permute-start.19 = (bf16[512,256]{1,0:T(8,128)(2,1)S(1)}, bf16[512,256]{1,0:T(8,128)(2,1)S(1)}, u32[]{:S(2)}, u32[]{:S(2)}) collective-permute-start(bf16[512,256]{1,0:T(8,128)(2,1)S(1)} %get-tuple-element.92), channel_id=1, source_target_pairs={{0,4},{4,0},{8,12},{12,8},{16,20},{20,16},{24,28},{28,24},{1,5},{5... | collective-permute-start | bytes 786440 | tf_op jit(solution)/shard_map/ppermute | solution.py:27
  83.8 9.6 %collective-permute-start.27 = (bf16[1,256,256]{2,1,0:T(8,128)(2,1)S(1)}, bf16[1,256,256]{2,1,0:T(8,128)(2,1)S(1)}, u32[]{:S(2)}, u32[]{:S(2)}) collective-permute-start(bf16[1,256,256]{2,1,0:T(8,128)(2,1)S(1)} %constant_dynamic-slice_fusion), channel_id=1, source_target_pairs={{0,16},{4,20},{8,24},{12,28},{16,0},{20,4},{24,8},{28,12},{1,17},{... | collective-permute-start | bytes 393224 | tf_op jit(solution)/shard_map/ppermute | solution.py:27
  86.3 15.6 %collective-permute-start.15 = (bf16[2,256,256]{2,1,0:T(8,128)(2,1)S(1)}, bf16[2,256,256]{2,1,0:T(8,128)(2,1)S(1)}, u32[]{:S(2)}, u32[]{:S(2)}) collective-permute-start(bf16[2,256,256]{2,1,0:T(8,128)(2,1)S(1)} %constant_dynamic-update-slice_fusion.4.refs_4_), channel_id=1, source_target_pairs={{0,8},{4,12},{8,0},{12,4},{16,24},{20,28},{24,16},{28,20},{1,9},{5... | collective-permute-start | bytes 786440 | tf_op jit(solution)/shard_map/ppermute | solution.py:27
  94.2 13.3 %collective-permute-start.21 = (bf16[1,64,1024]{2,1,0:T(8,128)(2,1)}, bf16[1,64,1024]{2,1,0:T(8,128)(2,1)}, u32[]{:S(2)}, u32[]{:S(2)}) collective-permute-start(bf16[1,64,1024]{2,1,0:T(8,128)(2,1)} %get-tuple-element.98), channel_id=1, source_target_pairs={{0,2},{1,3},{2,0},{3,1},{4,6},{5,7},{6,4},{7,5},{8,10},{9,11},{10,... | collective-permute-start | bytes 393224 | tf_op jit(solution)/shard_map/ppermute | solution.py:27
  95.7 13.6 %collective-permute-start.28 = (bf16[256,256]{1,0:T(8,128)(2,1)}, bf16[256,256]{1,0:T(8,128)(2,1)}, u32[]{:S(2)}, u32[]{:S(2)}) collective-permute-start(bf16[256,256]{1,0:T(8,128)(2,1)} %fusion.1), channel_id=1, source_target_pairs={{0,0},{4,16},{8,4},{12,20},{16,8},{20,24},{24,12},{28,28},{1,1},{5... | collective-permute-start | bytes 393224 | tf_op jit(solution)/shard_map/ppermute | solution.py:735
  100.1 9.1 %collective-permute-start.26 = (bf16[128,256]{1,0:T(8,128)(2,1)S(1)}, bf16[128,256]{1,0:T(8,128)(2,1)S(1)}, u32[]{:S(2)}, u32[]{:S(2)}) collective-permute-start(bf16[128,256]{1,0:T(8,128)(2,1)S(1)} %get-tuple-element.105.refs_8_), channel_id=1, source_target_pairs={{0,16},{4,20},{8,24},{12,28},{16,0},{20,4},{24,8},{28,12},{1,17},{... | collective-permute-start | bytes 196616 | tf_op jit(solution)/shard_map/ppermute | solution.py:27
  (31 other events, 104.5 us)

commit v6 on v5

--- a/solution.py
+++ b/solution.py
@@ -658,7 +658,7 @@
     back = [(b, a) for a, b in there]
     pos_lo = lax.ppermute(gate(pos_embed, chunks[0]).astype(BF16), "patch", there)[None]
     att, prob, ef, vw = call(
-        functools.partial(forward_kernel, 256, eb),
+        functools.partial(forward_kernel, 1024, eb),
         "attention_forward",
         (shape((cw, rows), BF16), shape((hl, nv, rows)), shape((5, nv, hl)), shape((5 * nv, cw), BF16)),
         (vk, pix, avail),
@@ -666,7 +666,7 @@
         after=(grad_att, pos_lo),
     )
     px_keep, px_send, z = call(
-        functools.partial(backward_kernel, 256, eb, n_j, vp),
+        functools.partial(backward_kernel, 1024, eb, n_j, vp),
         "attention_backward",
         [shape((n_j // 2, 4 * vp, rows), BF16)] * 2 + [shape((nr, cw + 128), BF16)],
         (pix, ef, vw, prob, grad_att),
@@ -708,7 +708,7 @@
     while turn < owners:
         g_rows = halve(gate(joined(*g_rows), copies_z), (me // turn) % 2, parts * turn)
         turn *= 2
-    px_got = flip(gate(px_send, copies_z), "var", 1)
+    px_got = flip(gate(px_send, first), "var", 1)
     fh = pad16(2 * rl + eb // 2 + 6)
     last = call(
         functools.partial(middle_kernel, eb, vl, n_j, dp),

time: 112 us -> 110 us (0.982)
  Pallas kernels: 27 us -> 25.6 us
    pallas_call x18, Pallas kernels: 27 us -> 25.6 us  [call(): pl.pallas_call(body, out_shape=shapes, in_specs=specs, out_specs=outs, sc...]
    unnamed x47 -> x49, local copies, waits for them, and re-layouts: 3.53 us -> 3.28 us
where the time goes in v6:
time: 110 us; the launch traced here: 109 us
  starting transfers between devices  51.3 us (47%)
  Pallas kernels  25.6 us (23%)
  waiting for transfers between devices  24 us (22%)
  local copies, waits for them, and re-layouts  4.16 us (4%)
  other arithmetic  3.1 us (3%)
    ppermute x27, starting transfers between devices, flip(): return lax.ppermute(x, axis, [(i, i ^ bit) for i in range(n)])  31.6 us
    pallas_call x18, Pallas kernels, call(): pl.pallas_call(body, out_shape=shapes, in_specs=specs, out_specs=outs, sc...  25.6 us
    ppermute x27, waiting for transfers between devices, flip(): return lax.ppermute(x, axis, [(i, i ^ bit) for i in range(n)])  16 us
    all_to_all x4, starting transfers between devices, exchange(): return lax.all_to_all(x, axis, 0, 0, tiled=True)  16 us
    all_to_all x4, waiting for transfers between devices, exchange(): return lax.all_to_all(x, axis, 0, 0, tiled=True)  7.98 us
    unnamed x49, local copies, waits for them, and re-layouts  3.28 us
  transfers between devices with their start and end apart: 33, of which 8 were waited for; matrix products, arithmetic and copies ran while one was open for 4% of the time, Pallas kernels for 16%

profile of v6, /device:TPU:0, one launch (start us, length us, event | category | flops | bytes accessed | tf_op | source)
XLA Modules:
  0.0 109.2 jit_solution(3330150952962013892)
XLA Ops:
  0.7 2.1 %pack.1 = (bf16[128,256]{1,0:T(8,128)(2,1)}, bf16[128,256]{1,0:T(8,128)(2,1)}, bf16[128,256]{1,0:T(8,128)(2,1)}, bf16[128,256]{1,0:T(8,128)(2,1)}, bf16[1,128,256]{2,1,0:T(8,128)(2,1)}) custom-call(f32[32,1024]{1,0:T(8,128)} %refs_0_.4, f32[32,1024]{1,0:T(8,128)} %refs_1_.3, f32[32,1024]{1,0:T(8,128)} %refs_0_.7, f32[1,32]{1,0:T(1,128)} %bitcast.36, ...), custom_call_target="tpu_custom_call" | custom-call | flops 11530000 | bytes 65536 | tf_op jit(solution)/shard_map/pack/pallas_call | solution.py:562
  2.7 2.4 %collective-permute-start = (bf16[128,256]{1,0:T(8,128)(2,1)}, bf16[128,256]{1,0:T(8,128)(2,1)S(1)}, u32[]{:S(2)}, u32[]{:S(2)}) collective-permute-start(bf16[128,256]{1,0:T(8,128)(2,1)} %get-tuple-element.66), channel_id=1, source_target_pairs={{0,3},{1,2},{2,1},{3,0},{4,7},{5,6},{6,5},{7,4},{8,11},{9,10},{10,... | collective-permute-start | bytes 196616 | tf_op jit(solution)/shard_map/ppermute | solution.py:27
  5.8 3.1 %collective-permute-start.1 = (bf16[1,128,256]{2,1,0:T(8,128)(2,1)}, bf16[1,128,256]{2,1,0:T(8,128)(2,1)S(1)}, u32[]{:S(2)}, u32[]{:S(2)}) collective-permute-start(bf16[1,128,256]{2,1,0:T(8,128)(2,1)} %get-tuple-element.67), channel_id=1, source_target_pairs={{0,16},{4,20},{8,24},{12,28},{16,0},{20,4},{24,8},{28,12},{1,17},{... | collective-permute-start | bytes 196616 | tf_op jit(solution)/shard_map/ppermute | solution.py:27
  15.8 3.4 %all-to-all-start = ((bf16[8,32,512]{2,1,0:T(8,128)(2,1)}), bf16[8,32,512]{2,1,0:T(8,128)(2,1)S(1)}, u32[]{:S(2)}, u32[]{:S(2)}) async-start(bf16[8,32,512]{2,1,0:T(8,128)(2,1)} %bitcast.4), calls=%async_computation | async-start | bytes 524288 | tf_op jit(solution)/shard_map/all_to_all | solution.py:22
  19.3 2.0 %collective-permute-start.3 = (bf16[4,128,256]{2,1,0:T(8,128)(2,1)S(1)}, bf16[4,128,256]{2,1,0:T(8,128)(2,1)S(1)}, u32[]{:S(2)}, u32[]{:S(2)}) collective-permute-start(bf16[4,128,256]{2,1,0:T(8,128)(2,1)S(1)} %constant_dynamic-update-slice_fusion.2.refs_0_), channel_id=1, source_target_pairs={{0,4},{4,0},{8,12},{12,8},{16,20},{20,16},{24,28},{28,24},{1,5},{5... | collective-permute-start | bytes 786440 | tf_op jit(solution)/shard_map/ppermute | solution.py:27
  21.3 8.4 %collective-permute-done.3.refs_1_ = bf16[4,128,256]{2,1,0:T(8,128)(2,1)S(1)} collective-permute-done((bf16[4,128,256]{2,1,0:T(8,128)(2,1)S(1)}, bf16[4,128,256]{2,1,0:T(8,128)(2,1)S(1)}, u32[]{:S(2)}, u32[]{:S(2)}) %collective-permute-start.3) | collective-permute-done | bytes 262176 | tf_op jit(solution)/shard_map/ppermute | solution.py:27
  31.2 4.7 %all-to-all-start.1 = ((bf16[8,32,512]{2,1,0:T(8,128)(2,1)}), bf16[8,32,512]{2,1,0:T(8,128)(2,1)S(1)}, u32[]{:S(2)}, u32[]{:S(2)}) async-start(bf16[8,32,512]{2,1,0:T(8,128)(2,1)} %sum.1), calls=%async_computation.1 | async-start | bytes 524288 | tf_op jit(solution)/shard_map/all_to_all | solution.py:22
  42.6 2.0 %collective-permute-done.12.refs_3_ = bf16[256,256]{1,0:T(8,128)(2,1)} collective-permute-done((bf16[256,256]{1,0:T(8,128)(2,1)}, bf16[256,256]{1,0:T(8,128)(2,1)}, u32[]{:S(2)}, u32[]{:S(2)}) %collective-permute-start.12) | collective-permute-done | bytes 131104 | tf_op jit(solution)/shard_map/ppermute | solution.py:27
  45.4 1.9 %grad_att.1.refs_3_.refs_4_ = bf16[256,1024]{1,0:T(8,128)(2,1)S(1)} custom-call(bf16[1024,256]{1,0:T(8,128)(2,1)S(1)} %get-tuple-element.69.refs_1_.refs_0_.refs_2_, bf16[256,256]{1,0:T(8,128)(2,1)S(1)} %collective-permute-done.6.refs_1_, bf16[256,256]{1,0:T(8,128)(2,1)S(1)} %collective-permute-done.11.refs_2_, ...), custom_call_target="tpu_custom_call" | custom-call | flops 11530000 | bytes 65536 | tf_op jit(solution)/shard_map/grad_att/pallas_call | solution.py:562
  47.3 1.8 %attention_forward.1 = (bf16[256,1024]{1,0:T(8,128)(2,1)S(1)}, f32[4,48,1024]{2,1,0:T(8,128)S(1)}, f32[5,48,4]{2,1,0:T(8,128)S(1)}, bf16[240,256]{1,0:T(8,128)(2,1)S(1)}) custom-call(bf16[256,512]{1,0:T(8,128)(2,1)S(1)} %bitcast.25, bf16[4,48,1024]{2,1,0:T(8,128)(2,1)S(1)} %pixels.1.refs_1_.refs_0_, s32[4,48]{1,0:T(4,128)S(1)} %copy-done.13, ...), custom_call_target="tpu_custom_call" | custom-call | flops 11530000 | bytes 65536 | tf_op jit(solution)/shard_map/attention_forward/pallas_call | solution.py:562
  49.1 2.4 %attention_backward.1 = (bf16[2,64,1024]{2,1,0:T(8,128)(2,1)S(1)}, bf16[2,64,1024]{2,1,0:T(8,128)(2,1)S(1)}, bf16[256,384]{1,0:T(8,128)(2,1)S(1)}) custom-call(bf16[4,48,1024]{2,1,0:T(8,128)(2,1)S(1)} %pixels.1.refs_1_.refs_0_, f32[5,48,4]{2,1,0:T(8,128)S(1)} %get-tuple-element.82.refs_1_, bf16[240,256]{1,0:T(8,128)(2,1)S(1)} %get-tuple-element.83.refs_2_, ...), custom_call_target="tpu_custom_call" | custom-call | flops 11530000 | bytes 65536 | tf_op jit(solution)/shard_map/attention_backward/pallas_call | solution.py:562
  55.1 1.9 %collective-permute-start.13 = (bf16[2,256,256]{2,1,0:T(8,128)(2,1)}, bf16[2,256,256]{2,1,0:T(8,128)(2,1)S(1)}, u32[]{:S(2)}, u32[]{:S(2)}) collective-permute-start(bf16[2,256,256]{2,1,0:T(8,128)(2,1)} %dynamic-slice_bitcast_fusion), channel_id=1, source_target_pairs={{0,8},{4,12},{8,0},{12,4},{16,24},{20,28},{24,16},{28,20},{1,9},{5... | collective-permute-start | bytes 786440 | tf_op jit(solution)/shard_map/ppermute | solution.py:27
  57.0 4.5 %all-to-all-start.2 = ((bf16[8,32,384]{2,1,0:T(8,128)(2,1)}), bf16[8,32,384]{2,1,0:T(8,128)(2,1)}, u32[]{:S(2)}, u32[]{:S(2)}) async-start(bf16[8,32,384]{2,1,0:T(8,128)(2,1)} %bitcast.32), calls=%async_computation.2 | async-start | bytes 393216 | tf_op jit(solution)/shard_map/all_to_all | solution.py:22
  61.5 2.9 %collective-permute-start.14 = (bf16[1,256,256]{2,1,0:T(8,128)(2,1)S(1)}, bf16[1,256,256]{2,1,0:T(8,128)(2,1)S(1)}, u32[]{:S(2)}, u32[]{:S(2)}) collective-permute-start(bf16[1,256,256]{2,1,0:T(8,128)(2,1)S(1)} %bitcast.30), channel_id=1, source_target_pairs={{0,16},{4,20},{8,24},{12,28},{16,0},{20,4},{24,8},{28,12},{1,17},{... | collective-permute-start | bytes 393224 | tf_op jit(solution)/shard_map/ppermute | solution.py:27
  66.1 7.1 %all-to-all-done.2.refs_0_ = bf16[8,32,384]{2,1,0:T(8,128)(2,1)} async-done(((bf16[8,32,384]{2,1,0:T(8,128)(2,1)}), bf16[8,32,384]{2,1,0:T(8,128)(2,1)}, u32[]{:S(2)}, u32[]{:S(2)}) %all-to-all-start.2) | async-done | bytes 196640 | tf_op jit(solution)/shard_map/all_to_all | solution.py:22
  73.2 1.8 %sum_z.1.refs_5_ = bf16[8,32,384]{2,1,0:T(8,128)(2,1)} custom-call(bf16[8,32,384]{2,1,0:T(8,128)(2,1)} %all-to-all-done.2.refs_0_, bf16[2,256,256]{2,1,0:T(8,128)(2,1)S(1)} %collective-permute-done.13.refs_1_), custom_call_target="tpu_custom_call" | custom-call | flops 11530000 | bytes 65536 | tf_op jit(solution)/shard_map/sum_z/pallas_call | solution.py:562
  75.0 3.4 %all-to-all-start.3 = ((bf16[8,32,384]{2,1,0:T(8,128)(2,1)}), bf16[8,32,384]{2,1,0:T(8,128)(2,1)S(1)}, u32[]{:S(2)}, u32[]{:S(2)}) async-start(bf16[8,32,384]{2,1,0:T(8,128)(2,1)} %sum_z.1.refs_5_), calls=%async_computation.3 | async-start | bytes 393216 | tf_op jit(solution)/shard_map/all_to_all | solution.py:22
  78.5 1.8 %weight_grad.1 = (bf16[512,256]{1,0:T(8,128)(2,1)S(1)}, bf16[4,128,256]{2,1,0:T(8,128)(2,1)S(1)}) custom-call(bf16[1280,256]{1,0:T(8,128)(2,1)S(1)} %get-tuple-element.86.refs_0_.refs_4_, bf16[256,1024]{1,0:T(8,128)(2,1)S(1)} %get-tuple-element.90.refs_1_.refs_6_, bf16[256,1024]{1,0:T(8,128)(2,1)S(1)} %collective-permute-done.16.refs_2_.refs_7_, ...), custom_call_target="tpu_custom_call" | custom-call | flops 11530000 | bytes 65536 | tf_op jit(solution)/shard_map/weight_grad/pallas_call | solution.py:562
  80.3 2.0 %collective-permute-start.19 = (bf16[512,256]{1,0:T(8,128)(2,1)S(1)}, bf16[512,256]{1,0:T(8,128)(2,1)S(1)}, u32[]{:S(2)}, u32[]{:S(2)}) collective-permute-start(bf16[512,256]{1,0:T(8,128)(2,1)S(1)} %get-tuple-element.92), channel_id=1, source_target_pairs={{0,4},{4,0},{8,12},{12,8},{16,20},{20,16},{24,28},{28,24},{1,5},{5... | collective-permute-start | bytes 786440 | tf_op jit(solution)/shard_map/ppermute | solution.py:27
  82.3 2.4 %collective-permute-start.27 = (bf16[1,256,256]{2,1,0:T(8,128)(2,1)S(1)}, bf16[1,256,256]{2,1,0:T(8,128)(2,1)S(1)}, u32[]{:S(2)}, u32[]{:S(2)}) collective-permute-start(bf16[1,256,256]{2,1,0:T(8,128)(2,1)S(1)} %constant_dynamic-slice_fusion), channel_id=1, source_target_pairs={{0,16},{4,20},{8,24},{12,28},{16,0},{20,4},{24,8},{28,12},{1,17},{... | collective-permute-start | bytes 393224 | tf_op jit(solution)/shard_map/ppermute | solution.py:27
  86.3 2.7 %collective-permute-done.19.refs_1_ = bf16[512,256]{1,0:T(8,128)(2,1)S(1)} collective-permute-done((bf16[512,256]{1,0:T(8,128)(2,1)S(1)}, bf16[512,256]{1,0:T(8,128)(2,1)S(1)}, u32[]{:S(2)}, u32[]{:S(2)}) %collective-permute-start.19) | collective-permute-done | bytes 262176 | tf_op jit(solution)/shard_map/ppermute | solution.py:27
  91.9 2.1 %collective-permute-start.28 = (bf16[256,256]{1,0:T(8,128)(2,1)}, bf16[256,256]{1,0:T(8,128)(2,1)}, u32[]{:S(2)}, u32[]{:S(2)}) collective-permute-start(bf16[256,256]{1,0:T(8,128)(2,1)} %fusion.1), channel_id=1, source_target_pairs={{0,0},{4,16},{8,4},{12,20},{16,8},{20,24},{24,12},{28,28},{1,1},{5... | collective-permute-start | bytes 393224 | tf_op jit(solution)/shard_map/ppermute | solution.py:735
  102.0 2.8 %mixed.1 = bf16[1024,256]{1,0:T(8,128)(2,1)} custom-call(s32[4]{0:T(128)S(1)} %copy-done.14, s32[4]{0:T(128)S(1)} %copy-done.15, bf16[1024,256]{1,0:T(8,128)(2,1)S(1)} %get-tuple-element.69.refs_1_.refs_0_.refs_2_, bf16[256,512]{1,0:T(8,128)(2,1)S(1)} %bitcast.27, bf16[2,256,256]{2,1,0:T(8,128)(2,1)S(1)} %constant_dynamic-update-slice_fusion.4.refs_4_, ...), custom_call_target="tpu_custom_call" | custom-call | flops 11530000 | bytes 65536 | tf_op jit(solution)/shard_map/mixed/pallas_call | solution.py:562
  107.4 1.8 %final.1 = (f32[32,1024]{1,0:T(8,128)}, f32[32,1024]{1,0:T(8,128)}, f32[32,1024]{1,0:T(8,128)}, f32[1,32]{1,0:T(1,128)}, f32[5,12,128]{2,1,0:T(8,128)}, /*index=...) custom-call(f32[32,1024]{1,0:T(8,128)S(1)} %copy-done.1, f32[32,1]{1,0:T(8,128)S(1)} %copy.26.refs_1_, ...), custom_call_target="tpu_custom_call" | custom-call | flops 11530000 | bytes 65536 | tf_op jit(solution)/shard_map/final/pallas_call | solution.py:562
  (119 shorter events, 36.7 us)
Async XLA Ops:
  2.7 8.9 %collective-permute-start = (bf16[128,256]{1,0:T(8,128)(2,1)}, bf16[128,256]{1,0:T(8,128)(2,1)S(1)}, u32[]{:S(2)}, u32[]{:S(2)}) collective-permute-start(bf16[128,256]{1,0:T(8,128)(2,1)} %get-tuple-element.66), channel_id=1, source_target_pairs={{0,3},{1,2},{2,1},{3,0},{4,7},{5,6},{6,5},{7,4},{8,11},{9,10},{10,... | collective-permute-start | bytes 196616 | tf_op jit(solution)/shard_map/ppermute | solution.py:27
  5.8 8.3 %collective-permute-start.1 = (bf16[1,128,256]{2,1,0:T(8,128)(2,1)}, bf16[1,128,256]{2,1,0:T(8,128)(2,1)S(1)}, u32[]{:S(2)}, u32[]{:S(2)}) collective-permute-start(bf16[1,128,256]{2,1,0:T(8,128)(2,1)} %get-tuple-element.67), channel_id=1, source_target_pairs={{0,16},{4,20},{8,24},{12,28},{16,0},{20,4},{24,8},{28,12},{1,17},{... | collective-permute-start | bytes 196616 | tf_op jit(solution)/shard_map/ppermute | solution.py:27
  12.6 18.6 %collective-permute-start.9 = (bf16[1280,256]{1,0:T(8,128)(2,1)S(1)}, bf16[1280,256]{1,0:T(8,128)(2,1)S(1)}, u32[]{:S(2)}, u32[]{:S(2)}) collective-permute-start(bf16[1280,256]{1,0:T(8,128)(2,1)S(1)} %get-tuple-element.86.refs_0_.refs_4_), channel_id=1, source_target_pairs={{0,2},{1,3},{2,0},{3,1},{4,6},{5,7},{6,4},{7,5},{8,10},{9,11},{10,... | collective-permute-start | bytes 1966088 | tf_op jit(solution)/shard_map/ppermute | solution.py:27
  15.8 14.7 %all-to-all-start = ((bf16[8,32,512]{2,1,0:T(8,128)(2,1)}), bf16[8,32,512]{2,1,0:T(8,128)(2,1)S(1)}, u32[]{:S(2)}, u32[]{:S(2)}) async-start(bf16[8,32,512]{2,1,0:T(8,128)(2,1)} %bitcast.4), calls=%async_computation | async-start | bytes 524288 | tf_op jit(solution)/shard_map/all_to_all | solution.py:22
  19.3 10.4 %collective-permute-start.3 = (bf16[4,128,256]{2,1,0:T(8,128)(2,1)S(1)}, bf16[4,128,256]{2,1,0:T(8,128)(2,1)S(1)}, u32[]{:S(2)}, u32[]{:S(2)}) collective-permute-start(bf16[4,128,256]{2,1,0:T(8,128)(2,1)S(1)} %constant_dynamic-update-slice_fusion.2.refs_0_), channel_id=1, source_target_pairs={{0,4},{4,0},{8,12},{12,8},{16,20},{20,16},{24,28},{28,24},{1,5},{5... | collective-permute-start | bytes 786440 | tf_op jit(solution)/shard_map/ppermute | solution.py:27
  21.3 18.8 %collective-permute-start.8 = (bf16[1280,256]{1,0:T(8,128)(2,1)S(1)}, bf16[1280,256]{1,0:T(8,128)(2,1)S(1)}, u32[]{:S(2)}, u32[]{:S(2)}) collective-permute-start(bf16[1280,256]{1,0:T(8,128)(2,1)S(1)} %get-tuple-element.86.refs_0_.refs_4_), channel_id=1, source_target_pairs={{0,1},{1,0},{2,3},{3,2},{4,5},{5,4},{6,7},{7,6},{8,9},{9,8},{10,11... | collective-permute-start | bytes 1966088 | tf_op jit(solution)/shard_map/ppermute | solution.py:27
  31.2 8.8 %collective-permute-start.10 = (bf16[1280,256]{1,0:T(8,128)(2,1)S(1)}, bf16[1280,256]{1,0:T(8,128)(2,1)}, u32[]{:S(2)}, u32[]{:S(2)}) collective-permute-start(bf16[1280,256]{1,0:T(8,128)(2,1)S(1)} %collective-permute-done.9.refs_2_.refs_6_), channel_id=1, source_target_pairs={{0,1},{1,0},{2,3},{3,2},{4,5},{5,4},{6,7},{7,6},{8,9},{9,8},{10,11... | collective-permute-start | bytes 1966088 | tf_op jit(solution)/shard_map/ppermute | solution.py:27
  31.2 14.2 %all-to-all-start.1 = ((bf16[8,32,512]{2,1,0:T(8,128)(2,1)}), bf16[8,32,512]{2,1,0:T(8,128)(2,1)S(1)}, u32[]{:S(2)}, u32[]{:S(2)}) async-start(bf16[8,32,512]{2,1,0:T(8,128)(2,1)} %sum.1), calls=%async_computation.1 | async-start | bytes 524288 | tf_op jit(solution)/shard_map/all_to_all | solution.py:22
  36.9 7.7 %collective-permute-start.12 = (bf16[256,256]{1,0:T(8,128)(2,1)}, bf16[256,256]{1,0:T(8,128)(2,1)}, u32[]{:S(2)}, u32[]{:S(2)}) collective-permute-start(bf16[256,256]{1,0:T(8,128)(2,1)} %get-tuple-element.81), channel_id=1, source_target_pairs={{0,3},{1,2},{2,1},{3,0},{4,7},{5,6},{6,5},{7,4},{8,11},{9,10},{10,... | collective-permute-start | bytes 393224 | tf_op jit(solution)/shard_map/ppermute | solution.py:27
  38.5 8.8 %collective-permute-start.7 = (bf16[256,256]{1,0:T(8,128)(2,1)}, bf16[256,256]{1,0:T(8,128)(2,1)S(1)}, u32[]{:S(2)}, u32[]{:S(2)}) collective-permute-start(bf16[256,256]{1,0:T(8,128)(2,1)} %convert_element_type.26), channel_id=1, source_target_pairs={{0,0},{16,4},{4,8},{20,12},{8,16},{24,20},{12,24},{28,28},{1,1},{1... | collective-permute-start | bytes 393224 | tf_op jit(solution)/shard_map/ppermute | solution.py:659
  51.5 26.9 %collective-permute-start.16 = (bf16[256,1024]{1,0:T(8,128)(2,1)S(1)}, bf16[256,1024]{1,0:T(8,128)(2,1)S(1)}, u32[]{:S(2)}, u32[]{:S(2)}) collective-permute-start(bf16[256,1024]{1,0:T(8,128)(2,1)S(1)} %get-tuple-element.90.refs_1_.refs_6_), channel_id=1, source_target_pairs={{0,1},{1,0},{2,3},{3,2},{4,5},{5,4},{6,7},{7,6},{8,9},{9,8},{10,11... | collective-permute-start | bytes 1572872 | tf_op jit(solution)/shard_map/ppermute | solution.py:27
  51.6 26.8 %collective-permute-start.17 = (bf16[256,1024]{1,0:T(8,128)(2,1)S(1)}, bf16[256,1024]{1,0:T(8,128)(2,1)S(1)}, u32[]{:S(2)}, u32[]{:S(2)}) collective-permute-start(bf16[256,1024]{1,0:T(8,128)(2,1)S(1)} %get-tuple-element.90.refs_1_.refs_6_), channel_id=1, source_target_pairs={{0,2},{1,3},{2,0},{3,1},{4,6},{5,7},{6,4},{7,5},{8,10},{9,11},{10,... | collective-permute-start | bytes 1572872 | tf_op jit(solution)/shard_map/ppermute | solution.py:27
  52.5 25.9 %collective-permute-start.18 = (bf16[256,1024]{1,0:T(8,128)(2,1)S(1)}, bf16[256,1024]{1,0:T(8,128)(2,1)}, u32[]{:S(2)}, u32[]{:S(2)}) collective-permute-start(bf16[256,1024]{1,0:T(8,128)(2,1)S(1)} %get-tuple-element.90.refs_1_.refs_6_), channel_id=1, source_target_pairs={{0,3},{1,2},{2,1},{3,0},{4,7},{5,6},{6,5},{7,4},{8,11},{9,10},{10,... | collective-permute-start | bytes 1572872 | tf_op jit(solution)/shard_map/ppermute | solution.py:27
  55.1 9.3 %collective-permute-start.13 = (bf16[2,256,256]{2,1,0:T(8,128)(2,1)}, bf16[2,256,256]{2,1,0:T(8,128)(2,1)S(1)}, u32[]{:S(2)}, u32[]{:S(2)}) collective-permute-start(bf16[2,256,256]{2,1,0:T(8,128)(2,1)} %dynamic-slice_bitcast_fusion), channel_id=1, source_target_pairs={{0,8},{4,12},{8,0},{12,4},{16,24},{20,28},{24,16},{28,20},{1,9},{5... | collective-permute-start | bytes 786440 | tf_op jit(solution)/shard_map/ppermute | solution.py:27
  57.0 16.2 %all-to-all-start.2 = ((bf16[8,32,384]{2,1,0:T(8,128)(2,1)}), bf16[8,32,384]{2,1,0:T(8,128)(2,1)}, u32[]{:S(2)}, u32[]{:S(2)}) async-start(bf16[8,32,384]{2,1,0:T(8,128)(2,1)} %bitcast.32), calls=%async_computation.2 | async-start | bytes 393216 | tf_op jit(solution)/shard_map/all_to_all | solution.py:22
  61.5 23.3 %collective-permute-start.14 = (bf16[1,256,256]{2,1,0:T(8,128)(2,1)S(1)}, bf16[1,256,256]{2,1,0:T(8,128)(2,1)S(1)}, u32[]{:S(2)}, u32[]{:S(2)}) collective-permute-start(bf16[1,256,256]{2,1,0:T(8,128)(2,1)S(1)} %bitcast.30), channel_id=1, source_target_pairs={{0,16},{4,20},{8,24},{12,28},{16,0},{20,4},{24,8},{28,12},{1,17},{... | collective-permute-start | bytes 393224 | tf_op jit(solution)/shard_map/ppermute | solution.py:27
  75.0 21.2 %all-to-all-start.3 = ((bf16[8,32,384]{2,1,0:T(8,128)(2,1)}), bf16[8,32,384]{2,1,0:T(8,128)(2,1)S(1)}, u32[]{:S(2)}, u32[]{:S(2)}) async-start(bf16[8,32,384]{2,1,0:T(8,128)(2,1)} %sum_z.1.refs_5_), calls=%async_computation.3 | async-start | bytes 393216 | tf_op jit(solution)/shard_map/all_to_all | solution.py:22
  80.3 8.7 %collective-permute-start.19 = (bf16[512,256]{1,0:T(8,128)(2,1)S(1)}, bf16[512,256]{1,0:T(8,128)(2,1)S(1)}, u32[]{:S(2)}, u32[]{:S(2)}) collective-permute-start(bf16[512,256]{1,0:T(8,128)(2,1)S(1)} %get-tuple-element.92), channel_id=1, source_target_pairs={{0,4},{4,0},{8,12},{12,8},{16,20},{20,16},{24,28},{28,24},{1,5},{5... | collective-permute-start | bytes 786440 | tf_op jit(solution)/shard_map/ppermute | solution.py:27
  82.3 8.8 %collective-permute-start.27 = (bf16[1,256,256]{2,1,0:T(8,128)(2,1)S(1)}, bf16[1,256,256]{2,1,0:T(8,128)(2,1)S(1)}, u32[]{:S(2)}, u32[]{:S(2)}) collective-permute-start(bf16[1,256,256]{2,1,0:T(8,128)(2,1)S(1)} %constant_dynamic-slice_fusion), channel_id=1, source_target_pairs={{0,16},{4,20},{8,24},{12,28},{16,0},{20,4},{24,8},{28,12},{1,17},{... | collective-permute-start | bytes 393224 | tf_op jit(solution)/shard_map/ppermute | solution.py:27
  84.8 15.2 %collective-permute-start.15 = (bf16[2,256,256]{2,1,0:T(8,128)(2,1)S(1)}, bf16[2,256,256]{2,1,0:T(8,128)(2,1)S(1)}, u32[]{:S(2)}, u32[]{:S(2)}) collective-permute-start(bf16[2,256,256]{2,1,0:T(8,128)(2,1)S(1)} %constant_dynamic-update-slice_fusion.4.refs_4_), channel_id=1, source_target_pairs={{0,8},{4,12},{8,0},{12,4},{16,24},{20,28},{24,16},{28,20},{1,9},{5... | collective-permute-start | bytes 786440 | tf_op jit(solution)/shard_map/ppermute | solution.py:27
  89.1 8.3 %collective-permute-start.25 = (bf16[256,256]{1,0:T(8,128)(2,1)S(1)}, bf16[256,256]{1,0:T(8,128)(2,1)}, u32[]{:S(2)}, u32[]{:S(2)}) collective-permute-start(bf16[256,256]{1,0:T(8,128)(2,1)S(1)} %get-tuple-element.93.refs_10_.refs_2_), channel_id=1, source_target_pairs={{0,8},{4,12},{8,0},{12,4},{16,24},{20,28},{24,16},{28,20},{1,9},{5... | collective-permute-start | bytes 393224 | tf_op jit(solution)/shard_map/ppermute | solution.py:27
  91.9 9.4 %collective-permute-start.28 = (bf16[256,256]{1,0:T(8,128)(2,1)}, bf16[256,256]{1,0:T(8,128)(2,1)}, u32[]{:S(2)}, u32[]{:S(2)}) collective-permute-start(bf16[256,256]{1,0:T(8,128)(2,1)} %fusion.1), channel_id=1, source_target_pairs={{0,0},{4,16},{8,4},{12,20},{16,8},{20,24},{24,12},{28,28},{1,1},{5... | collective-permute-start | bytes 393224 | tf_op jit(solution)/shard_map/ppermute | solution.py:735
  95.4 12.0 %collective-permute-start.21 = (bf16[1,64,1024]{2,1,0:T(8,128)(2,1)}, bf16[1,64,1024]{2,1,0:T(8,128)(2,1)}, u32[]{:S(2)}, u32[]{:S(2)}) collective-permute-start(bf16[1,64,1024]{2,1,0:T(8,128)(2,1)} %get-tuple-element.98), channel_id=1, source_target_pairs={{0,2},{1,3},{2,0},{3,1},{4,6},{5,7},{6,4},{7,5},{8,10},{9,11},{10,... | collective-permute-start | bytes 393224 | tf_op jit(solution)/shard_map/ppermute | solution.py:27
  98.3 7.3 %collective-permute-start.26 = (bf16[128,256]{1,0:T(8,128)(2,1)S(1)}, bf16[128,256]{1,0:T(8,128)(2,1)S(1)}, u32[]{:S(2)}, u32[]{:S(2)}) collective-permute-start(bf16[128,256]{1,0:T(8,128)(2,1)S(1)} %get-tuple-element.105.refs_8_), channel_id=1, source_target_pairs={{0,16},{4,20},{8,24},{12,28},{16,0},{20,4},{24,8},{28,12},{1,17},{... | collective-permute-start | bytes 196616 | tf_op jit(solution)/shard_map/ppermute | solution.py:27
  (32 other events, 108.4 us)

commit v7 on v6

--- a/solution.py
+++ b/solution.py
@@ -284,7 +284,7 @@
     cw, rows = out_ref.shape
     j = lax.axis_index("var")
     own = full_ref[pl.ds(pl.multiple_of(j * cw, cw), cw), :]
-    tile = 256
+    tile = 512
     for i in range(rows // tile):
         at = slice(i * tile, (i + 1) * tile)
         total = nt(own, cots[0][at, :])

time: 110 us -> 110 us (level)
  no operation moved by 1% of the time
where the time goes in v7:
time: 110 us; the launch traced here: 109 us
  starting transfers between devices  51.3 us (47%)
  Pallas kernels  25.6 us (23%)
  waiting for transfers between devices  24 us (22%)
  local copies, waits for them, and re-layouts  4.16 us (4%)
  other arithmetic  3.1 us (3%)
    ppermute x27, starting transfers between devices, flip(): return lax.ppermute(x, axis, [(i, i ^ bit) for i in range(n)])  31.6 us
    pallas_call x18, Pallas kernels, call(): pl.pallas_call(body, out_shape=shapes, in_specs=specs, out_specs=outs, sc...  25.6 us
    ppermute x27, waiting for transfers between devices, flip(): return lax.ppermute(x, axis, [(i, i ^ bit) for i in range(n)])  16 us
    all_to_all x4, starting transfers between devices, exchange(): return lax.all_to_all(x, axis, 0, 0, tiled=True)  16 us
    all_to_all x4, waiting for transfers between devices, exchange(): return lax.all_to_all(x, axis, 0, 0, tiled=True)  7.98 us
    unnamed x49, local copies, waits for them, and re-layouts  3.28 us
  transfers between devices with their start and end apart: 33, of which 8 were waited for; matrix products, arithmetic and copies ran while one was open for 4% of the time, Pallas kernels for 16%

profile of v7, /device:TPU:0, one launch (start us, length us, event | category | flops | bytes accessed | tf_op | source)
XLA Modules:
  0.0 109.2 jit_solution(3330150952962013892)
XLA Ops:
  0.7 2.1 %pack.1 = (bf16[128,256]{1,0:T(8,128)(2,1)}, bf16[128,256]{1,0:T(8,128)(2,1)}, bf16[128,256]{1,0:T(8,128)(2,1)}, bf16[128,256]{1,0:T(8,128)(2,1)}, bf16[1,128,256]{2,1,0:T(8,128)(2,1)}) custom-call(f32[32,1024]{1,0:T(8,128)} %refs_0_.4, f32[32,1024]{1,0:T(8,128)} %refs_1_.3, f32[32,1024]{1,0:T(8,128)} %refs_0_.7, f32[1,32]{1,0:T(1,128)} %bitcast.36, ...), custom_call_target="tpu_custom_call" | custom-call | flops 11530000 | bytes 65536 | tf_op jit(solution)/shard_map/pack/pallas_call | solution.py:562
  2.7 2.4 %collective-permute-start = (bf16[128,256]{1,0:T(8,128)(2,1)}, bf16[128,256]{1,0:T(8,128)(2,1)S(1)}, u32[]{:S(2)}, u32[]{:S(2)}) collective-permute-start(bf16[128,256]{1,0:T(8,128)(2,1)} %get-tuple-element.66), channel_id=1, source_target_pairs={{0,3},{1,2},{2,1},{3,0},{4,7},{5,6},{6,5},{7,4},{8,11},{9,10},{10,... | collective-permute-start | bytes 196616 | tf_op jit(solution)/shard_map/ppermute | solution.py:27
  5.8 3.1 %collective-permute-start.1 = (bf16[1,128,256]{2,1,0:T(8,128)(2,1)}, bf16[1,128,256]{2,1,0:T(8,128)(2,1)S(1)}, u32[]{:S(2)}, u32[]{:S(2)}) collective-permute-start(bf16[1,128,256]{2,1,0:T(8,128)(2,1)} %get-tuple-element.67), channel_id=1, source_target_pairs={{0,16},{4,20},{8,24},{12,28},{16,0},{20,4},{24,8},{28,12},{1,17},{... | collective-permute-start | bytes 196616 | tf_op jit(solution)/shard_map/ppermute | solution.py:27
  15.8 3.4 %all-to-all-start = ((bf16[8,32,512]{2,1,0:T(8,128)(2,1)}), bf16[8,32,512]{2,1,0:T(8,128)(2,1)S(1)}, u32[]{:S(2)}, u32[]{:S(2)}) async-start(bf16[8,32,512]{2,1,0:T(8,128)(2,1)} %bitcast.4), calls=%async_computation | async-start | bytes 524288 | tf_op jit(solution)/shard_map/all_to_all | solution.py:22
  19.3 2.0 %collective-permute-start.3 = (bf16[4,128,256]{2,1,0:T(8,128)(2,1)S(1)}, bf16[4,128,256]{2,1,0:T(8,128)(2,1)S(1)}, u32[]{:S(2)}, u32[]{:S(2)}) collective-permute-start(bf16[4,128,256]{2,1,0:T(8,128)(2,1)S(1)} %constant_dynamic-update-slice_fusion.2.refs_0_), channel_id=1, source_target_pairs={{0,4},{4,0},{8,12},{12,8},{16,20},{20,16},{24,28},{28,24},{1,5},{5... | collective-permute-start | bytes 786440 | tf_op jit(solution)/shard_map/ppermute | solution.py:27
  21.3 8.4 %collective-permute-done.3.refs_1_ = bf16[4,128,256]{2,1,0:T(8,128)(2,1)S(1)} collective-permute-done((bf16[4,128,256]{2,1,0:T(8,128)(2,1)S(1)}, bf16[4,128,256]{2,1,0:T(8,128)(2,1)S(1)}, u32[]{:S(2)}, u32[]{:S(2)}) %collective-permute-start.3) | collective-permute-done | bytes 262176 | tf_op jit(solution)/shard_map/ppermute | solution.py:27
  31.2 4.7 %all-to-all-start.1 = ((bf16[8,32,512]{2,1,0:T(8,128)(2,1)}), bf16[8,32,512]{2,1,0:T(8,128)(2,1)S(1)}, u32[]{:S(2)}, u32[]{:S(2)}) async-start(bf16[8,32,512]{2,1,0:T(8,128)(2,1)} %sum.1), calls=%async_computation.1 | async-start | bytes 524288 | tf_op jit(solution)/shard_map/all_to_all | solution.py:22
  42.6 2.0 %collective-permute-done.12.refs_3_ = bf16[256,256]{1,0:T(8,128)(2,1)} collective-permute-done((bf16[256,256]{1,0:T(8,128)(2,1)}, bf16[256,256]{1,0:T(8,128)(2,1)}, u32[]{:S(2)}, u32[]{:S(2)}) %collective-permute-start.12) | collective-permute-done | bytes 131104 | tf_op jit(solution)/shard_map/ppermute | solution.py:27
  45.4 1.9 %grad_att.1.refs_3_.refs_4_ = bf16[256,1024]{1,0:T(8,128)(2,1)S(1)} custom-call(bf16[1024,256]{1,0:T(8,128)(2,1)S(1)} %get-tuple-element.69.refs_1_.refs_0_.refs_2_, bf16[256,256]{1,0:T(8,128)(2,1)S(1)} %collective-permute-done.6.refs_1_, bf16[256,256]{1,0:T(8,128)(2,1)S(1)} %collective-permute-done.11.refs_2_, ...), custom_call_target="tpu_custom_call" | custom-call | flops 11530000 | bytes 65536 | tf_op jit(solution)/shard_map/grad_att/pallas_call | solution.py:562
  47.3 1.8 %attention_forward.1 = (bf16[256,1024]{1,0:T(8,128)(2,1)S(1)}, f32[4,48,1024]{2,1,0:T(8,128)S(1)}, f32[5,48,4]{2,1,0:T(8,128)S(1)}, bf16[240,256]{1,0:T(8,128)(2,1)S(1)}) custom-call(bf16[256,512]{1,0:T(8,128)(2,1)S(1)} %bitcast.25, bf16[4,48,1024]{2,1,0:T(8,128)(2,1)S(1)} %pixels.1.refs_1_.refs_0_, s32[4,48]{1,0:T(4,128)S(1)} %copy-done.13, ...), custom_call_target="tpu_custom_call" | custom-call | flops 11530000 | bytes 65536 | tf_op jit(solution)/shard_map/attention_forward/pallas_call | solution.py:562
  49.1 2.4 %attention_backward.1 = (bf16[2,64,1024]{2,1,0:T(8,128)(2,1)S(1)}, bf16[2,64,1024]{2,1,0:T(8,128)(2,1)S(1)}, bf16[256,384]{1,0:T(8,128)(2,1)S(1)}) custom-call(bf16[4,48,1024]{2,1,0:T(8,128)(2,1)S(1)} %pixels.1.refs_1_.refs_0_, f32[5,48,4]{2,1,0:T(8,128)S(1)} %get-tuple-element.82.refs_1_, bf16[240,256]{1,0:T(8,128)(2,1)S(1)} %get-tuple-element.83.refs_2_, ...), custom_call_target="tpu_custom_call" | custom-call | flops 11530000 | bytes 65536 | tf_op jit(solution)/shard_map/attention_backward/pallas_call | solution.py:562
  55.1 1.9 %collective-permute-start.13 = (bf16[2,256,256]{2,1,0:T(8,128)(2,1)}, bf16[2,256,256]{2,1,0:T(8,128)(2,1)S(1)}, u32[]{:S(2)}, u32[]{:S(2)}) collective-permute-start(bf16[2,256,256]{2,1,0:T(8,128)(2,1)} %dynamic-slice_bitcast_fusion), channel_id=1, source_target_pairs={{0,8},{4,12},{8,0},{12,4},{16,24},{20,28},{24,16},{28,20},{1,9},{5... | collective-permute-start | bytes 786440 | tf_op jit(solution)/shard_map/ppermute | solution.py:27
  57.0 4.5 %all-to-all-start.2 = ((bf16[8,32,384]{2,1,0:T(8,128)(2,1)}), bf16[8,32,384]{2,1,0:T(8,128)(2,1)}, u32[]{:S(2)}, u32[]{:S(2)}) async-start(bf16[8,32,384]{2,1,0:T(8,128)(2,1)} %bitcast.32), calls=%async_computation.2 | async-start | bytes 393216 | tf_op jit(solution)/shard_map/all_to_all | solution.py:22
  61.5 2.9 %collective-permute-start.14 = (bf16[1,256,256]{2,1,0:T(8,128)(2,1)S(1)}, bf16[1,256,256]{2,1,0:T(8,128)(2,1)S(1)}, u32[]{:S(2)}, u32[]{:S(2)}) collective-permute-start(bf16[1,256,256]{2,1,0:T(8,128)(2,1)S(1)} %bitcast.30), channel_id=1, source_target_pairs={{0,16},{4,20},{8,24},{12,28},{16,0},{20,4},{24,8},{28,12},{1,17},{... | collective-permute-start | bytes 393224 | tf_op jit(solution)/shard_map/ppermute | solution.py:27
  66.1 7.1 %all-to-all-done.2.refs_0_ = bf16[8,32,384]{2,1,0:T(8,128)(2,1)} async-done(((bf16[8,32,384]{2,1,0:T(8,128)(2,1)}), bf16[8,32,384]{2,1,0:T(8,128)(2,1)}, u32[]{:S(2)}, u32[]{:S(2)}) %all-to-all-start.2) | async-done | bytes 196640 | tf_op jit(solution)/shard_map/all_to_all | solution.py:22
  73.2 1.8 %sum_z.1.refs_5_ = bf16[8,32,384]{2,1,0:T(8,128)(2,1)} custom-call(bf16[8,32,384]{2,1,0:T(8,128)(2,1)} %all-to-all-done.2.refs_0_, bf16[2,256,256]{2,1,0:T(8,128)(2,1)S(1)} %collective-permute-done.13.refs_1_), custom_call_target="tpu_custom_call" | custom-call | flops 11530000 | bytes 65536 | tf_op jit(solution)/shard_map/sum_z/pallas_call | solution.py:562
  75.0 3.4 %all-to-all-start.3 = ((bf16[8,32,384]{2,1,0:T(8,128)(2,1)}), bf16[8,32,384]{2,1,0:T(8,128)(2,1)S(1)}, u32[]{:S(2)}, u32[]{:S(2)}) async-start(bf16[8,32,384]{2,1,0:T(8,128)(2,1)} %sum_z.1.refs_5_), calls=%async_computation.3 | async-start | bytes 393216 | tf_op jit(solution)/shard_map/all_to_all | solution.py:22
  78.5 1.8 %weight_grad.1 = (bf16[512,256]{1,0:T(8,128)(2,1)S(1)}, bf16[4,128,256]{2,1,0:T(8,128)(2,1)S(1)}) custom-call(bf16[1280,256]{1,0:T(8,128)(2,1)S(1)} %get-tuple-element.86.refs_0_.refs_4_, bf16[256,1024]{1,0:T(8,128)(2,1)S(1)} %get-tuple-element.90.refs_1_.refs_6_, bf16[256,1024]{1,0:T(8,128)(2,1)S(1)} %collective-permute-done.16.refs_2_.refs_7_, ...), custom_call_target="tpu_custom_call" | custom-call | flops 11530000 | bytes 65536 | tf_op jit(solution)/shard_map/weight_grad/pallas_call | solution.py:562
  80.3 2.0 %collective-permute-start.19 = (bf16[512,256]{1,0:T(8,128)(2,1)S(1)}, bf16[512,256]{1,0:T(8,128)(2,1)S(1)}, u32[]{:S(2)}, u32[]{:S(2)}) collective-permute-start(bf16[512,256]{1,0:T(8,128)(2,1)S(1)} %get-tuple-element.92), channel_id=1, source_target_pairs={{0,4},{4,0},{8,12},{12,8},{16,20},{20,16},{24,28},{28,24},{1,5},{5... | collective-permute-start | bytes 786440 | tf_op jit(solution)/shard_map/ppermute | solution.py:27
  82.3 2.4 %collective-permute-start.27 = (bf16[1,256,256]{2,1,0:T(8,128)(2,1)S(1)}, bf16[1,256,256]{2,1,0:T(8,128)(2,1)S(1)}, u32[]{:S(2)}, u32[]{:S(2)}) collective-permute-start(bf16[1,256,256]{2,1,0:T(8,128)(2,1)S(1)} %constant_dynamic-slice_fusion), channel_id=1, source_target_pairs={{0,16},{4,20},{8,24},{12,28},{16,0},{20,4},{24,8},{28,12},{1,17},{... | collective-permute-start | bytes 393224 | tf_op jit(solution)/shard_map/ppermute | solution.py:27
  86.3 2.7 %collective-permute-done.19.refs_1_ = bf16[512,256]{1,0:T(8,128)(2,1)S(1)} collective-permute-done((bf16[512,256]{1,0:T(8,128)(2,1)S(1)}, bf16[512,256]{1,0:T(8,128)(2,1)S(1)}, u32[]{:S(2)}, u32[]{:S(2)}) %collective-permute-start.19) | collective-permute-done | bytes 262176 | tf_op jit(solution)/shard_map/ppermute | solution.py:27
  91.9 2.1 %collective-permute-start.28 = (bf16[256,256]{1,0:T(8,128)(2,1)}, bf16[256,256]{1,0:T(8,128)(2,1)}, u32[]{:S(2)}, u32[]{:S(2)}) collective-permute-start(bf16[256,256]{1,0:T(8,128)(2,1)} %fusion.1), channel_id=1, source_target_pairs={{0,0},{4,16},{8,4},{12,20},{16,8},{20,24},{24,12},{28,28},{1,1},{5... | collective-permute-start | bytes 393224 | tf_op jit(solution)/shard_map/ppermute | solution.py:735
  102.0 2.8 %mixed.1 = bf16[1024,256]{1,0:T(8,128)(2,1)} custom-call(s32[4]{0:T(128)S(1)} %copy-done.14, s32[4]{0:T(128)S(1)} %copy-done.15, bf16[1024,256]{1,0:T(8,128)(2,1)S(1)} %get-tuple-element.69.refs_1_.refs_0_.refs_2_, bf16[256,512]{1,0:T(8,128)(2,1)S(1)} %bitcast.27, bf16[2,256,256]{2,1,0:T(8,128)(2,1)S(1)} %constant_dynamic-update-slice_fusion.4.refs_4_, ...), custom_call_target="tpu_custom_call" | custom-call | flops 11530000 | bytes 65536 | tf_op jit(solution)/shard_map/mixed/pallas_call | solution.py:562
  107.4 1.8 %final.1 = (f32[32,1024]{1,0:T(8,128)}, f32[32,1024]{1,0:T(8,128)}, f32[32,1024]{1,0:T(8,128)}, f32[1,32]{1,0:T(1,128)}, f32[5,12,128]{2,1,0:T(8,128)}, /*index=...) custom-call(f32[32,1024]{1,0:T(8,128)S(1)} %copy-done.1, f32[32,1]{1,0:T(8,128)S(1)} %copy.26.refs_1_, ...), custom_call_target="tpu_custom_call" | custom-call | flops 11530000 | bytes 65536 | tf_op jit(solution)/shard_map/final/pallas_call | solution.py:562
  (119 shorter events, 36.7 us)
Async XLA Ops:
  2.7 8.9 %collective-permute-start = (bf16[128,256]{1,0:T(8,128)(2,1)}, bf16[128,256]{1,0:T(8,128)(2,1)S(1)}, u32[]{:S(2)}, u32[]{:S(2)}) collective-permute-start(bf16[128,256]{1,0:T(8,128)(2,1)} %get-tuple-element.66), channel_id=1, source_target_pairs={{0,3},{1,2},{2,1},{3,0},{4,7},{5,6},{6,5},{7,4},{8,11},{9,10},{10,... | collective-permute-start | bytes 196616 | tf_op jit(solution)/shard_map/ppermute | solution.py:27
  5.8 8.3 %collective-permute-start.1 = (bf16[1,128,256]{2,1,0:T(8,128)(2,1)}, bf16[1,128,256]{2,1,0:T(8,128)(2,1)S(1)}, u32[]{:S(2)}, u32[]{:S(2)}) collective-permute-start(bf16[1,128,256]{2,1,0:T(8,128)(2,1)} %get-tuple-element.67), channel_id=1, source_target_pairs={{0,16},{4,20},{8,24},{12,28},{16,0},{20,4},{24,8},{28,12},{1,17},{... | collective-permute-start | bytes 196616 | tf_op jit(solution)/shard_map/ppermute | solution.py:27
  12.6 18.6 %collective-permute-start.9 = (bf16[1280,256]{1,0:T(8,128)(2,1)S(1)}, bf16[1280,256]{1,0:T(8,128)(2,1)S(1)}, u32[]{:S(2)}, u32[]{:S(2)}) collective-permute-start(bf16[1280,256]{1,0:T(8,128)(2,1)S(1)} %get-tuple-element.86.refs_0_.refs_4_), channel_id=1, source_target_pairs={{0,2},{1,3},{2,0},{3,1},{4,6},{5,7},{6,4},{7,5},{8,10},{9,11},{10,... | collective-permute-start | bytes 1966088 | tf_op jit(solution)/shard_map/ppermute | solution.py:27
  15.8 14.7 %all-to-all-start = ((bf16[8,32,512]{2,1,0:T(8,128)(2,1)}), bf16[8,32,512]{2,1,0:T(8,128)(2,1)S(1)}, u32[]{:S(2)}, u32[]{:S(2)}) async-start(bf16[8,32,512]{2,1,0:T(8,128)(2,1)} %bitcast.4), calls=%async_computation | async-start | bytes 524288 | tf_op jit(solution)/shard_map/all_to_all | solution.py:22
  19.3 10.4 %collective-permute-start.3 = (bf16[4,128,256]{2,1,0:T(8,128)(2,1)S(1)}, bf16[4,128,256]{2,1,0:T(8,128)(2,1)S(1)}, u32[]{:S(2)}, u32[]{:S(2)}) collective-permute-start(bf16[4,128,256]{2,1,0:T(8,128)(2,1)S(1)} %constant_dynamic-update-slice_fusion.2.refs_0_), channel_id=1, source_target_pairs={{0,4},{4,0},{8,12},{12,8},{16,20},{20,16},{24,28},{28,24},{1,5},{5... | collective-permute-start | bytes 786440 | tf_op jit(solution)/shard_map/ppermute | solution.py:27
  21.3 18.8 %collective-permute-start.8 = (bf16[1280,256]{1,0:T(8,128)(2,1)S(1)}, bf16[1280,256]{1,0:T(8,128)(2,1)S(1)}, u32[]{:S(2)}, u32[]{:S(2)}) collective-permute-start(bf16[1280,256]{1,0:T(8,128)(2,1)S(1)} %get-tuple-element.86.refs_0_.refs_4_), channel_id=1, source_target_pairs={{0,1},{1,0},{2,3},{3,2},{4,5},{5,4},{6,7},{7,6},{8,9},{9,8},{10,11... | collective-permute-start | bytes 1966088 | tf_op jit(solution)/shard_map/ppermute | solution.py:27
  31.2 8.8 %collective-permute-start.10 = (bf16[1280,256]{1,0:T(8,128)(2,1)S(1)}, bf16[1280,256]{1,0:T(8,128)(2,1)}, u32[]{:S(2)}, u32[]{:S(2)}) collective-permute-start(bf16[1280,256]{1,0:T(8,128)(2,1)S(1)} %collective-permute-done.9.refs_2_.refs_6_), channel_id=1, source_target_pairs={{0,1},{1,0},{2,3},{3,2},{4,5},{5,4},{6,7},{7,6},{8,9},{9,8},{10,11... | collective-permute-start | bytes 1966088 | tf_op jit(solution)/shard_map/ppermute | solution.py:27
  31.2 14.2 %all-to-all-start.1 = ((bf16[8,32,512]{2,1,0:T(8,128)(2,1)}), bf16[8,32,512]{2,1,0:T(8,128)(2,1)S(1)}, u32[]{:S(2)}, u32[]{:S(2)}) async-start(bf16[8,32,512]{2,1,0:T(8,128)(2,1)} %sum.1), calls=%async_computation.1 | async-start | bytes 524288 | tf_op jit(solution)/shard_map/all_to_all | solution.py:22
  36.9 7.7 %collective-permute-start.12 = (bf16[256,256]{1,0:T(8,128)(2,1)}, bf16[256,256]{1,0:T(8,128)(2,1)}, u32[]{:S(2)}, u32[]{:S(2)}) collective-permute-start(bf16[256,256]{1,0:T(8,128)(2,1)} %get-tuple-element.81), channel_id=1, source_target_pairs={{0,3},{1,2},{2,1},{3,0},{4,7},{5,6},{6,5},{7,4},{8,11},{9,10},{10,... | collective-permute-start | bytes 393224 | tf_op jit(solution)/shard_map/ppermute | solution.py:27
  38.5 8.8 %collective-permute-start.7 = (bf16[256,256]{1,0:T(8,128)(2,1)}, bf16[256,256]{1,0:T(8,128)(2,1)S(1)}, u32[]{:S(2)}, u32[]{:S(2)}) collective-permute-start(bf16[256,256]{1,0:T(8,128)(2,1)} %convert_element_type.26), channel_id=1, source_target_pairs={{0,0},{16,4},{4,8},{20,12},{8,16},{24,20},{12,24},{28,28},{1,1},{1... | collective-permute-start | bytes 393224 | tf_op jit(solution)/shard_map/ppermute | solution.py:659
  51.5 26.9 %collective-permute-start.16 = (bf16[256,1024]{1,0:T(8,128)(2,1)S(1)}, bf16[256,1024]{1,0:T(8,128)(2,1)S(1)}, u32[]{:S(2)}, u32[]{:S(2)}) collective-permute-start(bf16[256,1024]{1,0:T(8,128)(2,1)S(1)} %get-tuple-element.90.refs_1_.refs_6_), channel_id=1, source_target_pairs={{0,1},{1,0},{2,3},{3,2},{4,5},{5,4},{6,7},{7,6},{8,9},{9,8},{10,11... | collective-permute-start | bytes 1572872 | tf_op jit(solution)/shard_map/ppermute | solution.py:27
  51.6 26.8 %collective-permute-start.17 = (bf16[256,1024]{1,0:T(8,128)(2,1)S(1)}, bf16[256,1024]{1,0:T(8,128)(2,1)S(1)}, u32[]{:S(2)}, u32[]{:S(2)}) collective-permute-start(bf16[256,1024]{1,0:T(8,128)(2,1)S(1)} %get-tuple-element.90.refs_1_.refs_6_), channel_id=1, source_target_pairs={{0,2},{1,3},{2,0},{3,1},{4,6},{5,7},{6,4},{7,5},{8,10},{9,11},{10,... | collective-permute-start | bytes 1572872 | tf_op jit(solution)/shard_map/ppermute | solution.py:27
  52.5 25.9 %collective-permute-start.18 = (bf16[256,1024]{1,0:T(8,128)(2,1)S(1)}, bf16[256,1024]{1,0:T(8,128)(2,1)}, u32[]{:S(2)}, u32[]{:S(2)}) collective-permute-start(bf16[256,1024]{1,0:T(8,128)(2,1)S(1)} %get-tuple-element.90.refs_1_.refs_6_), channel_id=1, source_target_pairs={{0,3},{1,2},{2,1},{3,0},{4,7},{5,6},{6,5},{7,4},{8,11},{9,10},{10,... | collective-permute-start | bytes 1572872 | tf_op jit(solution)/shard_map/ppermute | solution.py:27
  55.1 9.3 %collective-permute-start.13 = (bf16[2,256,256]{2,1,0:T(8,128)(2,1)}, bf16[2,256,256]{2,1,0:T(8,128)(2,1)S(1)}, u32[]{:S(2)}, u32[]{:S(2)}) collective-permute-start(bf16[2,256,256]{2,1,0:T(8,128)(2,1)} %dynamic-slice_bitcast_fusion), channel_id=1, source_target_pairs={{0,8},{4,12},{8,0},{12,4},{16,24},{20,28},{24,16},{28,20},{1,9},{5... | collective-permute-start | bytes 786440 | tf_op jit(solution)/shard_map/ppermute | solution.py:27
  57.0 16.2 %all-to-all-start.2 = ((bf16[8,32,384]{2,1,0:T(8,128)(2,1)}), bf16[8,32,384]{2,1,0:T(8,128)(2,1)}, u32[]{:S(2)}, u32[]{:S(2)}) async-start(bf16[8,32,384]{2,1,0:T(8,128)(2,1)} %bitcast.32), calls=%async_computation.2 | async-start | bytes 393216 | tf_op jit(solution)/shard_map/all_to_all | solution.py:22
  61.5 23.3 %collective-permute-start.14 = (bf16[1,256,256]{2,1,0:T(8,128)(2,1)S(1)}, bf16[1,256,256]{2,1,0:T(8,128)(2,1)S(1)}, u32[]{:S(2)}, u32[]{:S(2)}) collective-permute-start(bf16[1,256,256]{2,1,0:T(8,128)(2,1)S(1)} %bitcast.30), channel_id=1, source_target_pairs={{0,16},{4,20},{8,24},{12,28},{16,0},{20,4},{24,8},{28,12},{1,17},{... | collective-permute-start | bytes 393224 | tf_op jit(solution)/shard_map/ppermute | solution.py:27
  75.0 21.2 %all-to-all-start.3 = ((bf16[8,32,384]{2,1,0:T(8,128)(2,1)}), bf16[8,32,384]{2,1,0:T(8,128)(2,1)S(1)}, u32[]{:S(2)}, u32[]{:S(2)}) async-start(bf16[8,32,384]{2,1,0:T(8,128)(2,1)} %sum_z.1.refs_5_), calls=%async_computation.3 | async-start | bytes 393216 | tf_op jit(solution)/shard_map/all_to_all | solution.py:22
  80.3 8.7 %collective-permute-start.19 = (bf16[512,256]{1,0:T(8,128)(2,1)S(1)}, bf16[512,256]{1,0:T(8,128)(2,1)S(1)}, u32[]{:S(2)}, u32[]{:S(2)}) collective-permute-start(bf16[512,256]{1,0:T(8,128)(2,1)S(1)} %get-tuple-element.92), channel_id=1, source_target_pairs={{0,4},{4,0},{8,12},{12,8},{16,20},{20,16},{24,28},{28,24},{1,5},{5... | collective-permute-start | bytes 786440 | tf_op jit(solution)/shard_map/ppermute | solution.py:27
  82.3 8.8 %collective-permute-start.27 = (bf16[1,256,256]{2,1,0:T(8,128)(2,1)S(1)}, bf16[1,256,256]{2,1,0:T(8,128)(2,1)S(1)}, u32[]{:S(2)}, u32[]{:S(2)}) collective-permute-start(bf16[1,256,256]{2,1,0:T(8,128)(2,1)S(1)} %constant_dynamic-slice_fusion), channel_id=1, source_target_pairs={{0,16},{4,20},{8,24},{12,28},{16,0},{20,4},{24,8},{28,12},{1,17},{... | collective-permute-start | bytes 393224 | tf_op jit(solution)/shard_map/ppermute | solution.py:27
  84.8 15.2 %collective-permute-start.15 = (bf16[2,256,256]{2,1,0:T(8,128)(2,1)S(1)}, bf16[2,256,256]{2,1,0:T(8,128)(2,1)S(1)}, u32[]{:S(2)}, u32[]{:S(2)}) collective-permute-start(bf16[2,256,256]{2,1,0:T(8,128)(2,1)S(1)} %constant_dynamic-update-slice_fusion.4.refs_4_), channel_id=1, source_target_pairs={{0,8},{4,12},{8,0},{12,4},{16,24},{20,28},{24,16},{28,20},{1,9},{5... | collective-permute-start | bytes 786440 | tf_op jit(solution)/shard_map/ppermute | solution.py:27
  89.1 8.3 %collective-permute-start.25 = (bf16[256,256]{1,0:T(8,128)(2,1)S(1)}, bf16[256,256]{1,0:T(8,128)(2,1)}, u32[]{:S(2)}, u32[]{:S(2)}) collective-permute-start(bf16[256,256]{1,0:T(8,128)(2,1)S(1)} %get-tuple-element.93.refs_10_.refs_2_), channel_id=1, source_target_pairs={{0,8},{4,12},{8,0},{12,4},{16,24},{20,28},{24,16},{28,20},{1,9},{5... | collective-permute-start | bytes 393224 | tf_op jit(solution)/shard_map/ppermute | solution.py:27
  91.9 9.4 %collective-permute-start.28 = (bf16[256,256]{1,0:T(8,128)(2,1)}, bf16[256,256]{1,0:T(8,128)(2,1)}, u32[]{:S(2)}, u32[]{:S(2)}) collective-permute-start(bf16[256,256]{1,0:T(8,128)(2,1)} %fusion.1), channel_id=1, source_target_pairs={{0,0},{4,16},{8,4},{12,20},{16,8},{20,24},{24,12},{28,28},{1,1},{5... | collective-permute-start | bytes 393224 | tf_op jit(solution)/shard_map/ppermute | solution.py:735
  95.4 12.0 %collective-permute-start.21 = (bf16[1,64,1024]{2,1,0:T(8,128)(2,1)}, bf16[1,64,1024]{2,1,0:T(8,128)(2,1)}, u32[]{:S(2)}, u32[]{:S(2)}) collective-permute-start(bf16[1,64,1024]{2,1,0:T(8,128)(2,1)} %get-tuple-element.98), channel_id=1, source_target_pairs={{0,2},{1,3},{2,0},{3,1},{4,6},{5,7},{6,4},{7,5},{8,10},{9,11},{10,... | collective-permute-start | bytes 393224 | tf_op jit(solution)/shard_map/ppermute | solution.py:27
  98.3 7.3 %collective-permute-start.26 = (bf16[128,256]{1,0:T(8,128)(2,1)S(1)}, bf16[128,256]{1,0:T(8,128)(2,1)S(1)}, u32[]{:S(2)}, u32[]{:S(2)}) collective-permute-start(bf16[128,256]{1,0:T(8,128)(2,1)S(1)} %get-tuple-element.105.refs_8_), channel_id=1, source_target_pairs={{0,16},{4,20},{8,24},{12,28},{16,0},{20,4},{24,8},{28,12},{1,17},{... | collective-permute-start | bytes 196616 | tf_op jit(solution)/shard_map/ppermute | solution.py:27
  (32 other events, 108.4 us)
